TPU v7x, 32 devices: a whole 2x2x4 slice. The times are simulated.
32 devices in a mesh: groups: 2 (over x), planes: 4 (over y, core), chan: 4 (over z).
Axes of the slice: x: 2, y: 2, z: 4, core: 2. Of those that a mesh axis runs over, the one named last changes fastest.
Arguments:
- field: float32 [2, 16, 128, 128, 128], P('groups', None, ('planes', 'chan')), parts along dimension 0, may hold values from -6 to 6
- cotangent: float32 [2, 16, 128, 128, 128], P('groups', None, ('planes', 'chan')), parts along dimension 0, may hold values from -6 to 6
- spec_weight: float32 [2, 16, 16, 64, 2048], P(None, None, None, 'planes', 'chan'), may hold values from -1.5 to 1.5
- point_weight: float32 [16, 16], replicated, may hold values from -1.5 to 1.5
- bias: float32 [16], replicated, may hold values from -3 to 3
Outputs:
- output: float32 [2, 16, 128, 128, 128], P('groups', None, ('planes', 'chan')), parts along dimension 0
- field_grad: float32 [2, 16, 128, 128, 128], P('groups', None, ('planes', 'chan')), parts along dimension 0
- weight_grad: float32 [4, 16, 16, 64, 2048], P('groups', None, None, 'planes', 'chan'), parts along dimension 0
There are 2 independent parts, one for each index of `groups`. A program takes and returns all parts, laid end to end along the dimension named above; an argument that names none is the same for every part. Nothing has to cross between parts.
All inputs are finite; a program needn't handle non-finite values.
Results may differ from a plain program's by a relative error of at most 0.0001.
Values sent between devices are 32-bit elements; how exact they have to be, the bound alone decides.
No kernel may reach another device: no remote copies, remote signals or barrier semaphores. Data moves between devices by JAX's collectives and lax.ppermute only.
A program may use at most 192 MiB of HBM per device.

v0:
```python
import math

import jax
import jax.numpy as jnp
from jax import lax
from jax.sharding import PartitionSpec as P

GX = 128
GY = 128
GZ = 128
MODES = 32


exact_mode = lax.Precision.HIGHEST


def retained(length):
    indices = jnp.arange(2 * MODES)
    return jnp.where(indices < MODES, indices, length - 2 * MODES + indices)


def phase_table(positions, freqs, length):
    turn_count = positions[:, None] * freqs[None, :] % length
    angles = turn_count.astype(jnp.float32) * (2.0 * math.pi / length)
    return (jnp.cos(angles), jnp.sin(angles))


def analysis(field):
    batch_size, channels, local_planes, second_length, third_length = field.shape
    plane_count = lax.axis_size("planes")
    channel_groups = lax.axis_size("chan")
    group_width = channels // channel_groups
    local_modes = 2 * MODES // plane_count
    first_length = local_planes * plane_count * channel_groups
    cosine, sine_part = phase_table(
        jnp.arange(second_length), retained(second_length), second_length
    )
    second_table = jnp.stack([cosine, -sine_part], 1).reshape(
        second_length, 2, plane_count, local_modes
    )
    cosine, sine_part = phase_table(jnp.arange(third_length), jnp.arange(MODES), third_length)
    third_table = jnp.stack(
        [jnp.stack([cosine, -sine_part], 1), jnp.stack([sine_part, cosine], 1)], 0
    )
    grouped = field.reshape(
        batch_size, channel_groups, group_width, local_planes, second_length, third_length
    )
    second_pass = jnp.einsum("bcdxyz,yspk->bcdxspkz", grouped, second_table, precision=exact_mode)
    spectra = jnp.einsum("bcdxspkz,sztm->bpckxdtm", second_pass, third_table, precision=exact_mode)
    spectra = spectra.reshape(
        batch_size, plane_count * channel_groups, local_modes, local_planes, group_width * 2 * MODES
    )
    arrived = lax.all_to_all(spectra, ("planes", "chan"), split_axis=1, concat_axis=3, tiled=True)
    positions = jnp.arange(first_length)
    arrived = arrived.reshape(batch_size, local_modes, first_length, group_width, 2, MODES)
    cosine, sine_part = phase_table(positions, retained(first_length), first_length)
    first_table = jnp.stack(
        [jnp.stack([cosine, -sine_part], 1), jnp.stack([sine_part, cosine], 1)], 1
    )
    first_pass = jnp.einsum("bkxdsm,xstf->bkdtfm", arrived, first_table, precision=exact_mode)
    first_pass = first_pass.reshape(batch_size, local_modes, group_width, 2, 2 * MODES * MODES)
    return lax.all_to_all(first_pass, "chan", split_axis=4, concat_axis=2, tiled=True)


def synthesis(spectrum):
    batch_size, local_modes, channels = (spectrum.shape[0], spectrum.shape[1], spectrum.shape[2])
    plane_count = lax.axis_size("planes")
    channel_groups = lax.axis_size("chan")
    group_width = channels // channel_groups
    local_planes = GX // (plane_count * channel_groups)
    gathered = lax.all_to_all(spectrum, "chan", split_axis=2, concat_axis=4, tiled=True)
    gathered = gathered.reshape(batch_size, local_modes, group_width, 2, 2 * MODES, MODES)
    cosine, sine_part = phase_table(jnp.arange(GX), retained(GX), GX)
    cosine_t = cosine.T
    sine_t = sine_part.T
    first_inverse = jnp.stack(
        [jnp.stack([cosine_t, sine_t], -1), jnp.stack([-sine_t, cosine_t], -1)], 0
    )
    first_pass = jnp.einsum("bkdsfm,sfxt->bkxdtm", gathered, first_inverse, precision=exact_mode)
    first_pass = first_pass.reshape(batch_size, local_modes, GX, group_width * 2 * MODES)
    returned = lax.all_to_all(
        first_pass[:, None], ("planes", "chan"), split_axis=3, concat_axis=1, tiled=True
    )
    returned = returned.reshape(
        batch_size, plane_count, channel_groups, local_modes, local_planes, group_width, 2, MODES
    )
    source_form = "bpckxdtm"
    cosine, sine_part = phase_table(jnp.arange(GZ), jnp.arange(MODES), GZ)
    cosine_t = cosine.T
    sine_t = sine_part.T
    third_inverse = jnp.stack(
        [jnp.stack([cosine_t, sine_t], 1), jnp.stack([-sine_t, cosine_t], 1)], 0
    )
    depth_pass = jnp.einsum(
        source_form + ",tmuz->bcdxpkuz", returned, third_inverse, precision=exact_mode
    )
    cosine, sine_part = phase_table(jnp.arange(GY), retained(GY), GY)
    second_inverse = jnp.stack([cosine.T, -sine_part.T], 0).reshape(2, plane_count, local_modes, GY)
    physical = jnp.einsum("bcdxpkuz,upky->bcdxyz", depth_pass, second_inverse, precision=exact_mode)
    return physical.reshape(batch_size, channels, local_planes, GY, GZ)


def by_sample(function, values):
    result = function(values)
    return result


def mode_weighting(mode_count):
    depth_mode = jnp.arange(mode_count) % MODES
    return jnp.where(depth_mode == 0, 1.0, 2.0).astype(jnp.float32) / float(GX * GY * GZ)


def contract(operand, weights):
    return jnp.einsum("bkin,iokn->bkon", operand, weights, precision=exact_mode)


def adjoint(operand, weights):
    return jnp.einsum("bkon,iokn->bkin", operand, weights, precision=exact_mode)


def outer_sum(first_operand, second_operand):
    return jnp.einsum("bkin,bkon->iokn", first_operand, second_operand, precision=exact_mode)


def local(field, cotangent, spec_weight, point_weight, bias):
    spectrum = by_sample(analysis, field)
    weight_re = spec_weight[0]
    weight_im = spec_weight[1]
    spec_re = spectrum[:, :, :, 0]
    spec_im = spectrum[:, :, :, 1]
    weighting = mode_weighting(spectrum.shape[-1])
    mixed_re = (contract(spec_re, weight_re) - contract(spec_im, weight_im)) * weighting
    mixed_im = (contract(spec_re, weight_im) + contract(spec_im, weight_re)) * weighting
    mixed_modes = jnp.stack([mixed_re, mixed_im], 3)
    spectral = by_sample(synthesis, mixed_modes)
    pointwise = jnp.einsum("bixyz,io->boxyz", field, point_weight, precision=exact_mode)
    preactivation = spectral + pointwise + bias[None, :, None, None, None]
    normal_cdf = 0.5 * (1.0 + lax.erf(preactivation * (1.0 / math.sqrt(2.0))))
    output = preactivation * normal_cdf
    derivative = normal_cdf + preactivation * jnp.exp(-0.5 * preactivation * preactivation) * (
        1.0 / math.sqrt(2.0 * math.pi)
    )
    pre_grad = cotangent * derivative
    raw_grad = by_sample(analysis, pre_grad)
    grad_re = raw_grad[:, :, :, 0] * weighting
    grad_im = raw_grad[:, :, :, 1] * weighting
    spectrum_grad = jnp.stack(
        [
            adjoint(grad_re, weight_re) + adjoint(grad_im, weight_im),
            adjoint(grad_im, weight_re) - adjoint(grad_re, weight_im),
        ],
        3,
    )
    weight_grad = jnp.stack(
        [
            outer_sum(spec_re, grad_re) + outer_sum(spec_im, grad_im),
            outer_sum(spec_re, grad_im) - outer_sum(spec_im, grad_re),
        ],
        0,
    )
    local_grad = jnp.einsum("boxyz,io->bixyz", pre_grad, point_weight, precision=exact_mode)
    field_grad = local_grad + by_sample(synthesis, spectrum_grad)
    return (output, field_grad, weight_grad)


def solution(mesh):
    in_specs = (
        P("groups", None, ("planes", "chan"), None, None),
        P("groups", None, ("planes", "chan"), None, None),
        P(None, None, None, "planes", "chan"),
        P(),
        P(),
    )
    out_specs = (
        P("groups", None, ("planes", "chan"), None, None),
        P("groups", None, ("planes", "chan"), None, None),
        P("groups", None, None, "planes", "chan"),
    )
    return jax.shard_map(local, mesh=mesh, in_specs=in_specs, out_specs=out_specs, check_vma=False)
```

profile of v0, /device:TPU:0, one launch (start us, length us, event | category | flops | bytes accessed | tf_op | source)
XLA Modules:
  0.0 735.8 jit_solution(8426604456952516511)
XLA Ops:
  26.4 12.5 %reshape.755 = f32[1,16,16,8,256]{4,3,2,1,0:T(8,128)} reshape(f32[1,4,4,16,8,4,2,32]{7,6,5,4,3,2,1,0:T(2,128)} %copy.104) | data formatting | bytes 4194304 | tf_op jit(solution)/shard_map/reshape | solution.py:50
  46.6 49.1 %all-to-all-done = f32[1,16,16,8,256]{4,3,2,0,1:T(8,128)S(1)} async-done(((f32[1,16,16,8,256]{4,3,2,0,1:T(8,128)}), f32[1,16,16,8,256]{4,3,2,0,1:T(8,128)S(1)}, u32[]{:S(2)}, u32[]{:S(2)}) %all-to-all-start) | async-done | bytes 2097184 | tf_op jit(solution)/shard_map/all_to_all | solution.py:53
  120.4 12.0 %copy.225 = f32[1,16,4,2,64,32]{1,3,2,5,4,0:T(2,128)} copy(f32[1,16,4,2,64,32]{4,5,2,1,3,0:T(8,128)} %fusion.68) | data formatting | bytes 2097152 | tf_op jit(solution)/shard_map/reshape | solution.py:61
  132.4 13.5 %reshape.821 = f32[4,1,65536]{2,1,0:T(1,128)} reshape(f32[2048,1,4,2,16]{4,3,2,1,0:T(2,128)} %bitcast.388) | data formatting | bytes 2097152
  149.6 25.9 %all-to-all-done.1 = f32[4,1,65536]{2,1,0:T(1,128)S(1)} async-done(((f32[4,1,65536]{2,1,0:T(1,128)}), f32[4,1,65536]{2,1,0:T(1,128)S(1)}, u32[]{:S(2)}, u32[]{:S(2)}) %all-to-all-start.1) | async-done | bytes 1048608 | tf_op jit(solution)/shard_map/all_to_all | solution.py:62
  179.8 14.3 %reshape.822 = f32[2048,1,4,2,16]{4,3,2,1,0:T(2,128)} reshape(f32[4,65536]{1,0:T(4,128)S(1)} %reduce.16) | data formatting | bytes 2097152
  217.4 25.0 %all-to-all-done.2 = f32[1,16,16,2,512]{4,1,3,0,2:T(8,128)S(1)} async-done(((f32[1,16,16,2,512]{4,1,3,0,2:T(8,128)}), f32[1,16,16,2,512]{4,1,3,0,2:T(8,128)S(1)}, u32[]{:S(2)}, u32[]{:S(2)}) %all-to-all-start.2) | async-done | bytes 1048608 | tf_op jit(solution)/shard_map/all_to_all | solution.py:71
  262.9 48.3 %all-to-all-done.3 = f32[1,1,16,128,256]{4,2,1,0,3:T(8,128)} async-done(((f32[1,1,16,128,256]{4,2,1,0,3:T(8,128)}), f32[1,1,16,128,256]{4,2,1,0,3:T(8,128)}, u32[]{:S(2)}, u32[]{:S(2)}) %all-to-all-start.3) | async-done | bytes 2097184 | tf_op jit(solution)/shard_map/all_to_all | solution.py:81
  322.3 14.1 %fusion.52 = f32[4,4,8,4,16,2,128]{6,4,1,2,0,3,5:T(8,128)S(1)} fusion(f32[4,4,16,8,4,2,32]{6,5,4,3,1,0,2:T(2,128)} %reshape.819, f32[1,32,2,128]{3,1,0,2:T(8,128)S(1)} %get-tuple-element.42, f32[1,32,2,128]{3,1,0,2:T(8,128)S(1)} %get-tuple-element.41), kind=kOutput, calls=%fused_computation.60 | convolution fusion | flops 1610629120 | bytes 10551296 | tf_op jit(solution)/shard_map/bpckxdtm,tmuz->bcdxpkuz/dot_general | solution.py:94
  344.3 21.9 %fusion.5 = (f32[1,16,8,128,128]{4,1,3,2,0:T(8,128)S(1)}, f32[16,8,128,128]{3,0,2,1:T(8,128)}) fusion(f32[1,16,8,128,128]{4,3,2,1,0:T(8,128)S(1)} %bitcast.408, f32[16]{0:T(128)S(1)} %copy-done.25, f32[16,8,128,128]{3,2,1,0:T(8,128)S(1)} %bitcast.396, f32[16,16]{1,0:T(8,128)S(1)} %copy-done, f32[16,8,128,128]{3,2,1,0:T(8,128)S(1)} %bitcast.397), kind=kOutput, calls=%fused_computation.7 | convolution fusion | flops 425721856 | bytes 41944128 | tf_op jit(solution)/shard_map/bixyz,io->boxyz/dot_general | solution.py:136
  366.3 11.7 %fusion.61 = f32[4,4,8,2,4,16,128]{6,5,2,1,0,4,3:T(8,128)S(1)} fusion(f32[4,4,8,128,128,1,1]{4,1,0,3,2,6,5:T(4,128)S(1)} %bitcast.387, f32[128,1,4,16]{0,3,2,1:T(8,128)} %copy-done.20, f32[128,1,4,16]{0,3,2,1:T(8,128)} %copy-done.19), kind=kOutput, calls=%fused_computation.64 | convolution fusion | flops 3221241856 | bytes 16842752 | tf_op jit(solution)/shard_map/bcdxyz,yspk->bcdxspkz/dot_general | solution.py:48
  393.3 11.2 %reshape.768 = f32[1,16,16,8,256]{4,3,2,1,0:T(8,128)S(1)} reshape(f32[1,4,4,16,8,4,2,32]{7,6,5,4,3,2,1,0:T(2,128)} %copy.127) | data formatting | bytes 4194304 | tf_op jit(solution)/shard_map/reshape | solution.py:50
  404.5 52.5 %all_to_all.126 = f32[1,16,16,8,256]{4,3,2,0,1:T(8,128)S(1)} all-to-all(f32[1,16,16,8,256]{4,3,2,0,1:T(8,128)S(1)} %bitcast.401), channel_id=1, replica_groups=mesh['groups'=2,'planes'=4,'chan'=4] {'planes','chan'}, dimensions={1} | all-to-all | bytes 4194304 | tf_op jit(solution)/shard_map/all_to_all | solution.py:53
  478.8 12.0 %copy.233 = f32[1,16,4,2,64,32]{1,3,2,5,4,0:T(2,128)} copy(f32[1,16,4,2,64,32]{4,5,2,1,3,0:T(8,128)} %fusion.71) | data formatting | bytes 2097152 | tf_op jit(solution)/shard_map/reshape | solution.py:61
  490.8 12.8 %reshape.823 = f32[4,1,65536]{2,1,0:T(1,128)S(1)} reshape(f32[2048,1,4,2,16]{4,3,2,1,0:T(2,128)} %bitcast.389) | data formatting | bytes 2097152
  503.6 28.8 %all_to_all.127 = f32[4,1,65536]{2,1,0:T(1,128)S(1)} all-to-all(f32[4,1,65536]{2,1,0:T(1,128)S(1)} %reshape.823), channel_id=1, replica_groups=mesh['groups'=2,'planes'=4,'chan'=4] {'chan'}, dimensions={0} | all-to-all | bytes 2097152 | tf_op jit(solution)/shard_map/all_to_all | solution.py:62
  536.2 14.3 %reshape.824 = f32[2048,1,4,2,16]{4,3,2,1,0:T(2,128)} reshape(f32[4,65536]{1,0:T(4,128)S(1)} %reduce.17) | data formatting | bytes 2097152
  561.3 12.7 %add_bitcast_fusion = (f32[1,16,16,16,512]{4,3,2,1,0:T(8,128)}, f32[1,16,16,16,512]{4,3,2,1,0:T(8,128)}, f32[16,512,16]{1,0,2:T(8,128)S(1)}, f32[16,512,16]{1,0,...) fusion(f32[16,512,16]{1,0,2:T(8,128)S(1)} %get-tuple-element.30, ...), kind=kLoop, calls=%fused_computation.51 | loop fusion | flops 28835840 | bytes 37748736 | tf_op jit(solution)/shard_map/stack | solution.py:154
  574.3 27.8 %all_to_all.128 = f32[1,16,16,2,512]{4,1,3,0,2:T(8,128)S(1)} all-to-all(f32[1,16,16,2,512]{4,1,3,0,2:T(8,128)S(1)} %pad_maximum_fusion.2), channel_id=1, replica_groups=mesh['groups'=2,'planes'=4,'chan'=4] {'chan'}, dimensions={2} | all-to-all | bytes 2097152 | tf_op jit(solution)/shard_map/all_to_all | solution.py:71
  632.2 10.6 %pad_maximum_fusion = f32[2,16,16,16,512]{4,3,2,1,0:T(8,128)} fusion(f32[1,16,16,16,512]{4,3,2,1,0:T(8,128)} %get-tuple-element.28, f32[1,16,16,16,512]{4,3,2,1,0:T(8,128)S(1)} %bitcast.399), kind=kLoop, calls=%fused_computation | loop fusion | flops 4194304 | bytes 33554432 | tf_op jit(solution)/shard_map/stack | solution.py:154
  642.9 27.8 %all-to-all-done.7 = f32[1,1,16,128,256]{4,2,1,0,3:T(8,128)} async-done(((f32[1,1,16,128,256]{4,2,1,0,3:T(8,128)}), f32[1,1,16,128,256]{4,2,1,0,3:T(8,128)}, u32[]{:S(2)}, u32[]{:S(2)}) %all-to-all-start.7) | async-done | bytes 2097184 | tf_op jit(solution)/shard_map/all_to_all | solution.py:81
  681.7 13.8 %fusion.58 = f32[4,4,8,4,16,2,128]{6,4,1,2,0,3,5:T(8,128)S(1)} fusion(f32[4,4,16,8,4,2,32]{6,5,4,3,1,0,2:T(2,128)} %reshape.820, f32[1,32,2,128]{3,1,0,2:T(8,128)S(1)} %copy-done.18, f32[1,32,2,128]{3,1,0,2:T(8,128)S(1)} %copy-done.16), kind=kOutput, calls=%fused_computation.62 | convolution fusion | flops 1610629120 | bytes 10551296 | tf_op jit(solution)/shard_map/bpckxdtm,tmuz->bcdxpkuz/dot_general | solution.py:94
  705.6 12.0 %copy.144 = f32[1,4,4,8,128,128]{5,2,1,4,3,0:T(4,128)} copy(f32[1,4,4,8,128,128]{5,4,3,2,1,0:T(8,128)} %fusion.46) | data formatting | bytes 16777216 | tf_op jit(solution)/shard_map/bcdxpkuz,upky->bcdxyz/transpose | solution.py:99
  717.6 12.1 %fusion.17 = f32[1,16,8,128,128]{4,1,3,2,0:T(8,128)S(1)} fusion(f32[16,8,128,128]{3,0,2,1:T(8,128)} %bitcast.392, f32[1,16,8,128,128]{4,1,3,2,0:T(8,128)} %copy-done.1, f32[16,16]{1,0:T(8,128)S(1)} %copy-done), kind=kOutput, calls=%fused_computation.24 | convolution fusion | flops 404750336 | bytes 25166848 | tf_op jit(solution)/shard_map/boxyz,io->bixyz/dot_general | solution.py:161
  (134 shorter events, 237.7 us)
Async XLA Ops:
  0.6 343.6 %copy-start = (f32[16,16]{1,0:T(8,128)S(1)}, f32[16,16]{1,0:T(8,128)}, u32[]{:S(2)}) copy-start(f32[16,16]{1,0:T(8,128)} %param.8) | copy-start | bytes 3076
  38.9 56.7 %all-to-all-start = ((f32[1,16,16,8,256]{4,3,2,0,1:T(8,128)}), f32[1,16,16,8,256]{4,3,2,0,1:T(8,128)S(1)}, u32[]{:S(2)}, u32[]{:S(2)}) async-start(f32[1,16,16,8,256]{4,3,2,0,1:T(8,128)} %bitcast.51), calls=%async_computation | async-start | bytes 4194304 | tf_op jit(solution)/shard_map/all_to_all | solution.py:53
  145.9 29.6 %all-to-all-start.1 = ((f32[4,1,65536]{2,1,0:T(1,128)}), f32[4,1,65536]{2,1,0:T(1,128)S(1)}, u32[]{:S(2)}, u32[]{:S(2)}) async-start(f32[4,1,65536]{2,1,0:T(1,128)} %reshape.821), calls=%async_computation.1 | async-start | bytes 2097152 | tf_op jit(solution)/shard_map/all_to_all | solution.py:62
  213.6 28.8 %all-to-all-start.2 = ((f32[1,16,16,2,512]{4,1,3,0,2:T(8,128)}), f32[1,16,16,2,512]{4,1,3,0,2:T(8,128)S(1)}, u32[]{:S(2)}, u32[]{:S(2)}) async-start(f32[1,16,16,2,512]{4,1,3,0,2:T(8,128)} %pad_maximum_fusion.1), calls=%async_computation.2 | async-start | bytes 2097152 | tf_op jit(solution)/shard_map/all_to_all | solution.py:71
  217.4 37.6 %copy-start.7 = (f32[1,64,128,2]{2,1,0,3:T(8,128)}, f32[1,64,128,2]{2,1,0,3:T(8,128)S(1)}, u32[]{:S(2)}) copy-start(f32[1,64,128,2]{2,1,0,3:T(8,128)S(1)} %get-tuple-element.37) | copy-start | bytes 196612
  217.4 37.6 %copy-start.9 = (f32[1,64,128,2]{2,1,0,3:T(8,128)}, f32[1,64,128,2]{2,1,0,3:T(8,128)S(1)}, u32[]{:S(2)}) copy-start(f32[1,64,128,2]{2,1,0,3:T(8,128)S(1)} %get-tuple-element.38) | copy-start | bytes 196612
  257.0 54.2 %all-to-all-start.3 = ((f32[1,1,16,128,256]{4,2,1,0,3:T(8,128)}), f32[1,1,16,128,256]{4,2,1,0,3:T(8,128)}, u32[]{:S(2)}, u32[]{:S(2)}) async-start(f32[1,1,16,128,256]{4,2,1,0,3:T(8,128)} %copy.116), calls=%async_computation.3 | async-start | bytes 4194304 | tf_op jit(solution)/shard_map/all_to_all | solution.py:81
  262.0 74.3 %copy-start.15 = (f32[1,32,2,128]{3,1,0,2:T(8,128)}, f32[1,32,2,128]{3,1,0,2:T(8,128)S(1)}, u32[]{:S(2)}) copy-start(f32[1,32,2,128]{3,1,0,2:T(8,128)S(1)} %get-tuple-element.41) | copy-start | bytes 98308
  262.1 74.3 %copy-start.17 = (f32[1,32,2,128]{3,1,0,2:T(8,128)}, f32[1,32,2,128]{3,1,0,2:T(8,128)S(1)}, u32[]{:S(2)}) copy-start(f32[1,32,2,128]{3,1,0,2:T(8,128)S(1)} %get-tuple-element.42) | copy-start | bytes 98308
  322.3 14.2 %copy-start.21 = (f32[1,4,16,128]{3,2,0,1:T(8,128)S(1)}, f32[1,4,16,128]{3,2,0,1:T(8,128)}, u32[]{:S(2)}) copy-start(f32[1,4,16,128]{3,2,0,1:T(8,128)} %get-tuple-element.45) | copy-start | bytes 98308
  322.3 14.2 %copy-start.23 = (f32[1,4,16,128]{3,2,0,1:T(8,128)S(1)}, f32[1,4,16,128]{3,2,0,1:T(8,128)}, u32[]{:S(2)}) copy-start(f32[1,4,16,128]{3,2,0,1:T(8,128)} %get-tuple-element.46) | copy-start | bytes 98308
  322.3 22.0 %slice-start = ((s8[8388608]{0:T(1024)(128)(4,1)}), s8[4194304]{0:T(1024)(128)(4,1)S(1)}, s32[]{:S(2)}) async-start(s8[8388608]{0:T(1024)(128)(4,1)} %bitcast.394), calls=%async_computation.8 | async-start | bytes 8388608
  322.3 22.0 %slice-start.4 = ((s8[8388608]{0:T(1024)(128)(4,1)}), s8[4194304]{0:T(1024)(128)(4,1)S(1)}, s32[]{:S(2)}) async-start(s8[8388608]{0:T(1024)(128)(4,1)} %bitcast.407), calls=%async_computation.12 | async-start | bytes 8388608
  366.3 11.7 %copy-start.1 = (f32[1,16,8,128,128]{4,1,3,2,0:T(8,128)}, f32[1,16,8,128,128]{4,1,3,2,0:T(8,128)S(1)}, u32[]{:S(2)}) copy-start(f32[1,16,8,128,128]{4,1,3,2,0:T(8,128)S(1)} %get-tuple-element.57) | copy-start | bytes 25165828
  366.3 11.7 %copy-start.12 = (f32[1,128,2,32]{1,3,0,2:T(8,128)S(1)}, f32[1,128,2,32]{1,3,0,2:T(8,128)}, u32[]{:S(2)}) copy-start(f32[1,128,2,32]{1,3,0,2:T(8,128)} %copy-done.11) | copy-start | bytes 98308
  366.3 11.7 %copy-start.14 = (f32[1,128,2,32]{1,3,0,2:T(8,128)S(1)}, f32[1,128,2,32]{1,3,0,2:T(8,128)}, u32[]{:S(2)}) copy-start(f32[1,128,2,32]{1,3,0,2:T(8,128)} %copy-done.13) | copy-start | bytes 98308
  574.0 31.4 %copy-start.8 = (f32[1,64,128,2]{2,1,0,3:T(8,128)S(1)}, f32[1,64,128,2]{2,1,0,3:T(8,128)}, u32[]{:S(2)}) copy-start(f32[1,64,128,2]{2,1,0,3:T(8,128)} %copy-done.7) | copy-start | bytes 196612
  574.0 31.4 %copy-start.10 = (f32[1,64,128,2]{2,1,0,3:T(8,128)S(1)}, f32[1,64,128,2]{2,1,0,3:T(8,128)}, u32[]{:S(2)}) copy-start(f32[1,64,128,2]{2,1,0,3:T(8,128)} %copy-done.9) | copy-start | bytes 196612
  616.6 54.0 %all-to-all-start.7 = ((f32[1,1,16,128,256]{4,2,1,0,3:T(8,128)}), f32[1,1,16,128,256]{4,2,1,0,3:T(8,128)}, u32[]{:S(2)}, u32[]{:S(2)}) async-start(f32[1,1,16,128,256]{4,2,1,0,3:T(8,128)} %copy.139), calls=%async_computation.7 | async-start | bytes 4194304 | tf_op jit(solution)/shard_map/all_to_all | solution.py:81
  621.3 11.0 %slice-start.2 = ((s8[8388608]{0:T(1024)(128)(4,1)}), s8[4194304]{0:T(1024)(128)(4,1)S(1)}, s32[]{:S(2)}) async-start(s8[8388608]{0:T(1024)(128)(4,1)} %bitcast.398), calls=%async_computation.10 | async-start | bytes 8388608
  642.9 38.9 %copy-start.16 = (f32[1,32,2,128]{3,1,0,2:T(8,128)S(1)}, f32[1,32,2,128]{3,1,0,2:T(8,128)}, u32[]{:S(2)}) copy-start(f32[1,32,2,128]{3,1,0,2:T(8,128)} %copy-done.15) | copy-start | bytes 98308
  642.9 38.9 %copy-start.18 = (f32[1,32,2,128]{3,1,0,2:T(8,128)S(1)}, f32[1,32,2,128]{3,1,0,2:T(8,128)}, u32[]{:S(2)}) copy-start(f32[1,32,2,128]{3,1,0,2:T(8,128)} %copy-done.17) | copy-start | bytes 98308
  681.7 13.8 %copy-start.22 = (f32[1,4,16,128]{3,2,0,1:T(8,128)S(1)}, f32[1,4,16,128]{3,2,0,1:T(8,128)}, u32[]{:S(2)}) copy-start(f32[1,4,16,128]{3,2,0,1:T(8,128)} %get-tuple-element.45) | copy-start | bytes 98308
  681.7 13.8 %copy-start.24 = (f32[1,4,16,128]{3,2,0,1:T(8,128)S(1)}, f32[1,4,16,128]{3,2,0,1:T(8,128)}, u32[]{:S(2)}) copy-start(f32[1,4,16,128]{3,2,0,1:T(8,128)} %get-tuple-element.46) | copy-start | bytes 98308
  (13 other events, 102.1 us)
where the time goes:
time: 744 us; the launch traced here: 736 us
  local copies, waits for them, and re-layouts  238 us (32%)
  waiting for transfers between devices  176 us (24%)
  matrix products  141 us (19%)
  blocking collectives  109 us (15%)
  other arithmetic  46.7 us (6%)
  starting transfers between devices  24.1 us (3%)
    all_to_all x2, waiting for transfers between devices, synthesis(): lax.all_to_all(first_pass[:, None], ('planes', 'chan'), split_axis=3, con...  76.1 us
    unnamed x71, local copies, waits for them, and re-layouts  68.4 us
    another operation x8, local copies, waits for them, and re-layouts  58.7 us
    all_to_all x1, blocking collectives, analysis(): lax.all_to_all(spectra, ('planes', 'chan'), split_axis=1, concat_axis=3,...  52.5 us
    all_to_all x1, waiting for transfers between devices, analysis(): lax.all_to_all(spectra, ('planes', 'chan'), split_axis=1, concat_axis=3,...  49.1 us
    all_to_all x1, blocking collectives, analysis(): lax.all_to_all(first_pass, 'chan', split_axis=4, concat_axis=2, tiled=True)  28.8 us
    dot_general x2, matrix products, synthesis(): jnp.einsum(source_form + ',tmuz->bcdxpkuz', returned, third_inverse, prec...  27.9 us
    all_to_all x1, blocking collectives, synthesis(): lax.all_to_all(spectrum, 'chan', split_axis=2, concat_axis=4, tiled=True)  27.8 us
  transfers between devices with their start and end apart: 5, of which 5 were waited for; matrix products, arithmetic and copies ran while one was open for 3% of the time, Pallas kernels for 0%

commit v1 on v0

v1 whole, which is shorter than its diff:
```python
import functools
import math

import numpy as np

import jax
import jax.numpy as jnp
from jax import lax
from jax.experimental import pallas as pl
from jax.experimental.pallas import tpu as pltpu
from jax.sharding import PartitionSpec as P


exact_mode = lax.Precision.HIGHEST


def retained(s, length):
    indices = jnp.arange(2 * s.modes)
    return jnp.where(indices < s.modes, indices, length - 2 * s.modes + indices)


def phase_table(positions, freqs, length):
    turn_count = positions[:, None] * freqs[None, :] % length
    angles = turn_count.astype(jnp.float32) * (2.0 * math.pi / length)
    return (jnp.cos(angles), jnp.sin(angles))


def plain_analysis(s, field):
    batch_size, channels, local_planes, second_length, third_length = field.shape
    plane_count = lax.axis_size("planes")
    channel_groups = lax.axis_size("chan")
    group_width = channels // channel_groups
    local_modes = 2 * s.modes // plane_count
    first_length = local_planes * plane_count * channel_groups
    cosine, sine_part = phase_table(
        jnp.arange(second_length), retained(s, second_length), second_length
    )
    second_table = jnp.stack([cosine, -sine_part], 1).reshape(
        second_length, 2, plane_count, local_modes
    )
    cosine, sine_part = phase_table(jnp.arange(third_length), jnp.arange(s.modes), third_length)
    third_table = jnp.stack(
        [jnp.stack([cosine, -sine_part], 1), jnp.stack([sine_part, cosine], 1)], 0
    )
    grouped = field.reshape(
        batch_size, channel_groups, group_width, local_planes, second_length, third_length
    )
    second_pass = jnp.einsum("bcdxyz,yspk->bcdxspkz", grouped, second_table, precision=exact_mode)
    spectra = jnp.einsum("bcdxspkz,sztm->bpckxdtm", second_pass, third_table, precision=exact_mode)
    spectra = spectra.reshape(
        batch_size, plane_count * channel_groups, local_modes, local_planes, group_width * 2 * s.modes
    )
    arrived = lax.all_to_all(spectra, ("planes", "chan"), split_axis=1, concat_axis=3, tiled=True)
    positions = jnp.arange(first_length)
    arrived = arrived.reshape(batch_size, local_modes, first_length, group_width, 2, s.modes)
    cosine, sine_part = phase_table(positions, retained(s, first_length), first_length)
    first_table = jnp.stack(
        [jnp.stack([cosine, -sine_part], 1), jnp.stack([sine_part, cosine], 1)], 1
    )
    first_pass = jnp.einsum("bkxdsm,xstf->bkdtfm", arrived, first_table, precision=exact_mode)
    first_pass = first_pass.reshape(batch_size, local_modes, group_width, 2, 2 * s.modes * s.modes)
    return lax.all_to_all(first_pass, "chan", split_axis=4, concat_axis=2, tiled=True)


def plain_synthesis(s, spectrum):
    batch_size, local_modes, channels = (spectrum.shape[0], spectrum.shape[1], spectrum.shape[2])
    plane_count = lax.axis_size("planes")
    channel_groups = lax.axis_size("chan")
    group_width = channels // channel_groups
    local_planes = s.gx // (plane_count * channel_groups)
    gathered = lax.all_to_all(spectrum, "chan", split_axis=2, concat_axis=4, tiled=True)
    gathered = gathered.reshape(batch_size, local_modes, group_width, 2, 2 * s.modes, s.modes)
    cosine, sine_part = phase_table(jnp.arange(s.gx), retained(s, s.gx), s.gx)
    cosine_t = cosine.T
    sine_t = sine_part.T
    first_inverse = jnp.stack(
        [jnp.stack([cosine_t, sine_t], -1), jnp.stack([-sine_t, cosine_t], -1)], 0
    )
    first_pass = jnp.einsum("bkdsfm,sfxt->bkxdtm", gathered, first_inverse, precision=exact_mode)
    first_pass = first_pass.reshape(batch_size, local_modes, s.gx, group_width * 2 * s.modes)
    returned = lax.all_to_all(
        first_pass[:, None], ("planes", "chan"), split_axis=3, concat_axis=1, tiled=True
    )
    returned = returned.reshape(
        batch_size, plane_count, channel_groups, local_modes, local_planes, group_width, 2, s.modes
    )
    source_form = "bpckxdtm"
    cosine, sine_part = phase_table(jnp.arange(s.gz), jnp.arange(s.modes), s.gz)
    cosine_t = cosine.T
    sine_t = sine_part.T
    third_inverse = jnp.stack(
        [jnp.stack([cosine_t, sine_t], 1), jnp.stack([-sine_t, cosine_t], 1)], 0
    )
    depth_pass = jnp.einsum(
        source_form + ",tmuz->bcdxpkuz", returned, third_inverse, precision=exact_mode
    )
    cosine, sine_part = phase_table(jnp.arange(s.gy), retained(s, s.gy), s.gy)
    second_inverse = jnp.stack([cosine.T, -sine_part.T], 0).reshape(2, plane_count, local_modes, s.gy)
    physical = jnp.einsum("bcdxpkuz,upky->bcdxyz", depth_pass, second_inverse, precision=exact_mode)
    return physical.reshape(batch_size, channels, local_planes, s.gy, s.gz)


def mode_weighting(s, mode_count):
    depth_mode = jnp.arange(mode_count) % s.modes
    return jnp.where(depth_mode == 0, 1.0, 2.0).astype(jnp.float32) / float(s.gx * s.gy * s.gz)


def contract(operand, weights):
    return jnp.einsum("bkin,iokn->bkon", operand, weights, precision=exact_mode)


def adjoint(operand, weights):
    return jnp.einsum("bkon,iokn->bkin", operand, weights, precision=exact_mode)


def outer_sum(first_operand, second_operand):
    return jnp.einsum("bkin,bkon->iokn", first_operand, second_operand, precision=exact_mode)


def plain_local(s, field, cotangent, spec_weight, point_weight, bias):
    spectrum = plain_analysis(s, field)
    weight_re = spec_weight[0]
    weight_im = spec_weight[1]
    spec_re = spectrum[:, :, :, 0]
    spec_im = spectrum[:, :, :, 1]
    weighting = mode_weighting(s, spectrum.shape[-1])
    mixed_re = (contract(spec_re, weight_re) - contract(spec_im, weight_im)) * weighting
    mixed_im = (contract(spec_re, weight_im) + contract(spec_im, weight_re)) * weighting
    mixed_modes = jnp.stack([mixed_re, mixed_im], 3)
    spectral = plain_synthesis(s, mixed_modes)
    pointwise = jnp.einsum("bixyz,io->boxyz", field, point_weight, precision=exact_mode)
    preactivation = spectral + pointwise + bias[None, :, None, None, None]
    normal_cdf = 0.5 * (1.0 + lax.erf(preactivation * (1.0 / math.sqrt(2.0))))
    output = preactivation * normal_cdf
    derivative = normal_cdf + preactivation * jnp.exp(-0.5 * preactivation * preactivation) * (
        1.0 / math.sqrt(2.0 * math.pi)
    )
    pre_grad = cotangent * derivative
    raw_grad = plain_analysis(s, pre_grad)
    grad_re = raw_grad[:, :, :, 0] * weighting
    grad_im = raw_grad[:, :, :, 1] * weighting
    spectrum_grad = jnp.stack(
        [
            adjoint(grad_re, weight_re) + adjoint(grad_im, weight_im),
            adjoint(grad_im, weight_re) - adjoint(grad_re, weight_im),
        ],
        3,
    )
    weight_grad = jnp.stack(
        [
            outer_sum(spec_re, grad_re) + outer_sum(spec_im, grad_im),
            outer_sum(spec_re, grad_im) - outer_sum(spec_im, grad_re),
        ],
        0,
    )
    local_grad = jnp.einsum("boxyz,io->bixyz", pre_grad, point_weight, precision=exact_mode)
    field_grad = local_grad + plain_synthesis(s, spectrum_grad)
    return (output, field_grad, weight_grad)


LANES = 128
X_CHUNKS = 1
MODE_CHUNKS = 1
f32 = jnp.float32
bf16 = jnp.bfloat16


class Sizes:
    def __init__(self, field, spec_weight):
        self.planes = lax.axis_size("planes")
        self.chan = lax.axis_size("chan")
        self.owners = self.planes * self.chan
        _, self.ch, self.lx, self.gy, self.gz = field.shape
        self.gx = self.lx * self.owners
        _, _, _, self.jl, local_flat = spec_weight.shape
        self.jy = self.jl * self.planes
        self.flat = local_flat
        self.modes = self.jy // 2
        self.jxl = local_flat // self.modes
        self.jx = self.jxl * self.chan
        self.gw = self.ch // self.chan
        self.scale = 1.0 / float(self.gx * self.gy * self.gz)

    def fits(self):
        return (
            self.gw * self.modes == LANES
            and self.gz == LANES
            and self.gy == LANES
            and self.jy * 2 == LANES
            and self.jx * 2 == LANES
            and self.gw % 2 == 0
            and self.flat % LANES == 0
            and self.jl % (16 * MODE_CHUNKS) == 0
            and self.lx % (4 * X_CHUNKS) == 0
            and self.gx == 2 * LANES // 2
        )


def kept(count, length):
    index = np.arange(count)
    return np.where(index < count // 2, index, length - count + index)


def waves(freqs, length):
    turns = (freqs[:, None] * np.arange(length)[None, :]) % length
    angles = turns * (2.0 * math.pi / length)
    return np.cos(angles), np.sin(angles)


def two_terms(table):
    table = np.asarray(table, np.float32)
    high = table.astype(jnp.bfloat16)
    low = (table - high.astype(np.float32)).astype(jnp.bfloat16)
    return high, low


def stacked_square(table):
    high, low = two_terms(table)
    return np.concatenate([np.concatenate([high, high], 1), np.concatenate([low, low], 1)], 0)


def second_tables(s):
    cosine, sine = waves(kept(s.jy, s.gy), s.gy)
    forward = np.concatenate([cosine, -sine], 0)
    return stacked_square(forward), stacked_square(forward.T)


def third_tables(s):
    cosine, sine = waves(np.arange(s.modes), s.gz)
    base = np.zeros((s.gw, 2, s.gz, 2, s.gw, s.modes))
    for c in range(s.gw):
        base[c, 0, :, 0, c] = cosine.T
        base[c, 0, :, 1, c] = -sine.T
        base[c, 1, :, 0, c] = sine.T
        base[c, 1, :, 1, c] = cosine.T
    forward = base.reshape(s.gw * 2 * s.gz, 2 * LANES)
    inverse = np.zeros((s.gw, 2, s.gw, s.modes, 2, s.gz))
    for c in range(s.gw):
        inverse[c, 0, c, :, 0, :] = cosine
        inverse[c, 0, c, :, 1, :] = sine
        inverse[c, 1, c, :, 0, :] = -sine
        inverse[c, 1, c, :, 1, :] = cosine
    inverse = inverse.reshape(s.gw, 2 * LANES, 2 * s.gz)
    return two_terms(forward) + two_terms(inverse)


def first_tables(s):
    cosine, sine = waves(kept(s.jx, s.gx), s.gx)
    lxk = s.lx // X_CHUNKS
    c5 = cosine.reshape(s.chan, s.jxl, s.owners, X_CHUNKS, lxk)
    s5 = sine.reshape(s.chan, s.jxl, s.owners, X_CHUNKS, lxk)
    forward = np.zeros((s.chan, 2, s.jxl, X_CHUNKS, s.owners, 2, lxk))
    inverse = np.zeros((X_CHUNKS, s.owners, 2, lxk, s.chan, 2, s.jxl))
    for out, inp, sign_f, wave in ((0, 0, 1, c5), (0, 1, 1, s5), (1, 0, -1, s5), (1, 1, 1, c5)):
        forward[:, out, :, :, :, inp] = sign_f * wave.transpose(0, 1, 3, 2, 4)
        inverse[:, :, inp, :, :, out] = sign_f * wave.transpose(3, 2, 4, 0, 1)
    rows = s.chan * 2 * s.jxl
    return forward.reshape(rows, -1), inverse.reshape(-1, rows)


def terms(value):
    high = value.astype(bf16)
    return high, (value - high.astype(f32)).astype(bf16)


def dot(a, b):
    return jnp.dot(a, b, preferred_element_type=f32)


def square_dot(table, value):
    high, low = terms(value)
    both = dot(table, jnp.concatenate([high, low], 0))
    half = both.shape[0] // 2
    return both[:half] + both[half:]


def gelu_parts(v):
    normal_cdf = 0.5 * (1.0 + lax.erf(v * (1.0 / math.sqrt(2.0))))
    slope = normal_cdf + v * jnp.exp(-0.5 * v * v) * (1.0 / math.sqrt(2.0 * math.pi))
    return normal_cdf, slope


def forward_second(s, x, pair, tile, table_ref, wide_high, wide_low):
    out = square_dot(table_ref[...], tile)
    rows = pl.ds(pl.multiple_of(x * s.jy, s.jy), s.jy)
    for c in range(2):
        for part in range(2):
            high, low = terms(out[part * s.jy:(part + 1) * s.jy, c * s.gz:(c + 1) * s.gz])
            at = ((pair * 2 + c) * 2 + part) * s.gz
            wide_high[rows, at:at + s.gz] = high
            wide_low[rows, at:at + s.gz] = low


def forward_third(s, lxk, wide_high, wide_low, high_ref, low_ref, out_ref):
    high = wide_high[...]
    out = dot(high, high_ref[...]) + dot(wide_low[...], high_ref[...]) + dot(high, low_ref[...])
    for x in range(lxk):
        for part in range(2):
            for p in range(s.planes):
                start = x * s.jy + p * s.jl
                out_ref[p, 0, pl.ds(part * lxk + x, s.jl, stride=2 * lxk), :] = out[
                    start:start + s.jl, part * LANES:(part + 1) * LANES
                ]


def gather_modes(s, lxk, in_ref, sum_high, sum_low):
    for x in range(lxk):
        for part in range(2):
            for p in range(s.planes):
                piece = in_ref[p, 0, pl.ds(part * lxk + x, s.jl, stride=2 * lxk), :]
                high, low = terms(piece)
                start = x * s.jy + p * s.jl
                sum_high[start:start + s.jl, part * LANES:(part + 1) * LANES] = high
                sum_low[start:start + s.jl, part * LANES:(part + 1) * LANES] = low


def inverse_third(s, sum_high, sum_low, high_ref, low_ref, depth):
    high = sum_high[...]
    low = sum_low[...]
    for c in range(s.gw):
        depth[c] = dot(high, high_ref[c]) + dot(low, high_ref[c]) + dot(high, low_ref[c])


def inverse_second(s, x, pair, table_ref, depth):
    rows = pl.ds(pl.multiple_of(x * s.jy, s.jy), s.jy)
    sides = []
    for c in range(2):
        both = depth[pair * 2 + c, rows, :]
        sides.append(jnp.concatenate([both[:, :s.gz], both[:, s.gz:]], 0))
    return square_dot(table_ref[...], jnp.concatenate(sides, 1))


def analysis_kernel(s, lxk, field_ref, second_ref, high_ref, low_ref, out_ref, wide_high, wide_low):
    def one(x, carry):
        for pair in range(s.gw // 2):
            tile = jnp.concatenate([field_ref[0, pair * 2, x], field_ref[0, pair * 2 + 1, x]], 1)
            forward_second(s, x, pair, tile, second_ref, wide_high, wide_low)
        return carry

    lax.fori_loop(0, lxk, one, 0)
    forward_third(s, lxk, wide_high, wide_low, high_ref, low_ref, out_ref)


def middle_kernel(
    s, lxk, in_ref, point_ref, cot_ref, inv_high, inv_low, inv_second, second_ref, high_ref, low_ref,
    output_ref, grad_ref, out_ref, sum_high, sum_low, depth, wide_high, wide_low,
):
    gather_modes(s, lxk, in_ref, sum_high, sum_low)
    inverse_third(s, sum_high, sum_low, inv_high, inv_low, depth)

    def one(x, carry):
        for pair in range(s.gw // 2):
            plane = inverse_second(s, x, pair, inv_second, depth)
            grads = []
            for c in range(2):
                v = plane[:, c * s.gz:(c + 1) * s.gz] + point_ref[0, pair * 2 + c, x]
                normal_cdf, slope = gelu_parts(v)
                output_ref[0, pair * 2 + c, x] = v * normal_cdf
                grad = cot_ref[0, pair * 2 + c, x] * slope
                grad_ref[0, pair * 2 + c, x] = grad
                grads.append(grad)
            forward_second(s, x, pair, jnp.concatenate(grads, 1), second_ref, wide_high, wide_low)
        return carry

    lax.fori_loop(0, lxk, one, 0)
    forward_third(s, lxk, wide_high, wide_low, high_ref, low_ref, out_ref)


def final_kernel(s, lxk, in_ref, local_ref, inv_high, inv_low, inv_second, out_ref, sum_high, sum_low, depth):
    gather_modes(s, lxk, in_ref, sum_high, sum_low)
    inverse_third(s, sum_high, sum_low, inv_high, inv_low, depth)

    def one(x, carry):
        for pair in range(s.gw // 2):
            plane = inverse_second(s, x, pair, inv_second, depth)
            for c in range(2):
                out_ref[0, pair * 2 + c, x] = (
                    plane[:, c * s.gz:(c + 1) * s.gz] + local_ref[0, pair * 2 + c, x]
                )
        return carry

    lax.fori_loop(0, lxk, one, 0)


def whole(array):
    rank = len(array.shape)
    return pl.BlockSpec(array.shape, lambda *_: (0,) * rank, pipeline_mode=pl.Buffered(1))


def cost(flops, *arrays):
    count = sum(int(np.prod(a.shape)) * a.dtype.itemsize for a in arrays)
    return pl.CostEstimate(flops=int(flops), bytes_accessed=count, transcendentals=0)


def grid_spec(s, lxk, chunk):
    return pl.BlockSpec((1, s.gw, lxk, s.gy, s.gz), lambda g: (0, g, chunk, 0, 0))


def mode_spec(s, lxk):
    return pl.BlockSpec((s.planes, 1, s.jl * 2 * lxk, LANES), lambda g: (0, g, 0, 0))


def mode_shape(s, lxk):
    return jax.ShapeDtypeStruct((s.planes, s.chan, s.jl * 2 * lxk, LANES), f32)


def wide_scratch(s, lxk):
    return [pltpu.VMEM((lxk * s.jy, s.gw * 2 * s.gz), bf16)] * 2


def sum_scratch(s, lxk):
    return [
        pltpu.VMEM((lxk * s.jy, 2 * LANES), bf16),
        pltpu.VMEM((lxk * s.jy, 2 * LANES), bf16),
        pltpu.VMEM((s.gw, lxk * s.jy, 2 * s.gz), f32),
    ]


def analysis(s, field, chunk, second, third):
    lxk = s.lx // X_CHUNKS
    out = mode_shape(s, lxk)
    tables = (second[0], third[0], third[1])
    return pl.pallas_call(
        functools.partial(analysis_kernel, s, lxk),
        grid=(s.chan,),
        in_specs=[grid_spec(s, lxk, chunk)] + [whole(t) for t in tables],
        out_specs=mode_spec(s, lxk),
        out_shape=out,
        scratch_shapes=wide_scratch(s, lxk),
        cost_estimate=cost(6e9 / X_CHUNKS, field, out),
        name="analysis",
    )(field, *tables)


def middle(s, modes, point, cotangent, chunk, second, third, output, grad):
    lxk = s.lx // X_CHUNKS
    out = mode_shape(s, lxk)
    tables = (third[2], third[3], second[1], second[0], third[0], third[1])
    spec = grid_spec(s, lxk, chunk)
    aliased = [] if output is None else [output, grad]
    count = 3 + len(tables)

    def body(*refs):
        middle_kernel(s, lxk, *refs[:count], *refs[count + len(aliased):])

    return pl.pallas_call(
        body,
        grid=(s.chan,),
        in_specs=[mode_spec(s, lxk), spec, spec]
        + [whole(t) for t in tables]
        + [pl.BlockSpec(memory_space=pl.ANY)] * len(aliased),
        out_specs=[spec, spec, mode_spec(s, lxk)],
        out_shape=[jax.ShapeDtypeStruct(point.shape, f32)] * 2 + [out],
        scratch_shapes=sum_scratch(s, lxk) + wide_scratch(s, lxk),
        input_output_aliases={count + i: i for i in range(len(aliased))},
        cost_estimate=cost(1.2e10 / X_CHUNKS, modes, point, cotangent, point, point),
        name="middle",
    )(modes, point, cotangent, *tables, *aliased)


def final(s, modes, local_grad, chunk, second, third, grad):
    lxk = s.lx // X_CHUNKS
    tables = (third[2], third[3], second[1])
    spec = grid_spec(s, lxk, chunk)
    aliased = [] if grad is None else [grad]
    count = 2 + len(tables)

    def body(*refs):
        final_kernel(s, lxk, *refs[:count], *refs[count + len(aliased):])

    return pl.pallas_call(
        body,
        grid=(s.chan,),
        in_specs=[mode_spec(s, lxk), spec]
        + [whole(t) for t in tables]
        + [pl.BlockSpec(memory_space=pl.ANY)] * len(aliased),
        out_specs=spec,
        out_shape=jax.ShapeDtypeStruct(local_grad.shape, f32),
        scratch_shapes=sum_scratch(s, lxk),
        input_output_aliases={count + i: i for i in range(len(aliased))},
        cost_estimate=cost(6e9 / X_CHUNKS, modes, local_grad, local_grad),
        name="final",
    )(modes, local_grad, *tables, *aliased)


def pointwise_kernel(channels, values_ref, weight_ref, bias_ref, out_ref):
    def rows(step, carry):
        at = pl.ds(pl.multiple_of(step * 32, 32), 32)
        sources = [values_ref[0, i, 0, at, :] for i in range(channels)]
        for o in range(channels):
            total = sources[0] * weight_ref[0, o] + bias_ref[o]
            for i in range(1, channels):
                total = total + sources[i] * weight_ref[i, o]
            out_ref[0, o, 0, at, :] = total
        return carry

    lax.fori_loop(0, values_ref.shape[3] // 32, rows, 0)


def pointwise(values, weight, bias):
    _, channels, lx, gy, gz = values.shape
    spec = pl.BlockSpec((1, channels, 1, gy, gz), lambda x: (0, 0, x, 0, 0))
    return pl.pallas_call(
        functools.partial(pointwise_kernel, channels),
        grid=(lx,),
        in_specs=[spec, pl.BlockSpec(memory_space=pltpu.SMEM), pl.BlockSpec(memory_space=pltpu.SMEM)],
        out_specs=spec,
        out_shape=jax.ShapeDtypeStruct(values.shape, f32),
        cost_estimate=cost(1e10, values, values),
        name="pointwise",
    )(values, weight, bias)


def first_kernel(rows, chunks, *refs):
    ins, (stacked_ref, out_ref) = refs[:chunks], refs[chunks:]
    sides = []
    per = ins[0].shape[1] // 2
    for j in range(2):
        parts = [r[o, j * per:(j + 1) * per, :] for r in ins for o in range(r.shape[0])]
        sides.append(jnp.concatenate(parts, 0))
    high, low = terms(jnp.concatenate(sides, 1))
    both = dot(stacked_ref[...], high)
    out = both[:rows] + both[rows:] + dot(stacked_ref[:rows, :], low)
    step = out_ref.shape[1] // 2
    for c in range(out_ref.shape[0]):
        for j in range(2):
            out_ref[c, j * step:(j + 1) * step, :] = out[
                c * step:(c + 1) * step, j * LANES:(j + 1) * LANES
            ]


def first_pass(s, chunks, table, mode_chunk):
    lxk = s.lx // X_CHUNKS
    rows = table.shape[0]
    stacked = np.concatenate(two_terms(table), 0)
    pairs = s.jl // MODE_CHUNKS // 2
    out = jax.ShapeDtypeStruct((s.chan, pairs * 2 * 2 * s.jxl, LANES), f32)
    offset = mode_chunk * pairs
    return pl.pallas_call(
        functools.partial(first_kernel, rows, len(chunks)),
        grid=(pairs,),
        in_specs=[pl.BlockSpec((s.owners, 4 * lxk, LANES), lambda j: (0, j + offset, 0))] * len(chunks)
        + [whole(stacked)],
        out_specs=pl.BlockSpec((s.chan, 4 * s.jxl, LANES), lambda j: (0, j, 0)),
        out_shape=out,
        cost_estimate=cost(1e9 / MODE_CHUNKS, out, out, out),
        name="first_forward",
    )(*chunks, stacked)


def back_kernel(chunks, in_ref, *refs):
    tables, outs = refs[:chunks], refs[chunks:]
    step = in_ref.shape[1] // 2
    sides = []
    for j in range(2):
        parts = [in_ref[c, j * step:(j + 1) * step, :] for c in range(in_ref.shape[0])]
        sides.append(jnp.concatenate(parts, 0))
    value = jnp.concatenate(sides, 1)
    for table_ref, out_ref in zip(tables, outs):
        out = square_dot(table_ref[...], value)
        per = out_ref.shape[1] // 2
        for o in range(out_ref.shape[0]):
            for j in range(2):
                out_ref[o, j * per:(j + 1) * per, :] = out[
                    o * per:(o + 1) * per, j * LANES:(j + 1) * LANES
                ]


def first_inverse(s, modes, table):
    lxk = s.lx // X_CHUNKS
    rows = table.shape[0] // X_CHUNKS
    squares = [stacked_square(table[k * rows:(k + 1) * rows]) for k in range(X_CHUNKS)]
    pairs = s.jl // 2
    out = jax.ShapeDtypeStruct((s.owners, s.jl * 2 * lxk, LANES), f32)
    return pl.pallas_call(
        functools.partial(back_kernel, X_CHUNKS),
        grid=(pairs,),
        in_specs=[pl.BlockSpec((s.chan, 4 * s.jxl, LANES), lambda j: (0, j, 0))]
        + [whole(t) for t in squares],
        out_specs=[pl.BlockSpec((s.owners, 4 * lxk, LANES), lambda j: (0, j, 0))] * X_CHUNKS,
        out_shape=[out] * X_CHUNKS,
        cost_estimate=cost(1e9, out, out, out),
        name="first_inverse",
    )(modes, *squares)


def swap_groups(pieces, width):
    count = len(pieces)
    lane = lax.broadcasted_iota(jnp.int32, pieces[0].shape, 1)
    step = count // 2
    pieces = list(pieces)
    while step:
        upper = (lane // (width * step)) % 2 == 1
        for a in range(count):
            if a & step:
                continue
            low, high = pieces[a], pieces[a + step]
            pieces[a] = jnp.where(upper, pltpu.roll(high, width * step, 1), low)
            pieces[a + step] = jnp.where(upper, high, pltpu.roll(low, LANES - width * step, 1))
        step //= 2
    return pieces


def spread_modes(s, count, in_ref, out_ref, factor=None):
    stride = 2 * s.jxl
    for g in range(s.chan):
        for part in range(2):
            for a in range(s.jxl // s.gw):
                pieces = [
                    in_ref[g, pl.ds(part * s.jxl + a * s.gw + b, count, stride=stride), :]
                    for b in range(s.gw)
                ]
                for c, piece in enumerate(swap_groups(pieces, s.modes)):
                    if factor is not None:
                        piece = piece * factor
                    out_ref[part, g * s.gw + c, :, a * LANES:(a + 1) * LANES] = piece


def depth_factor(s, shape):
    lane = lax.broadcasted_iota(jnp.int32, shape, 1)
    return jnp.where(lane % s.modes == 0, s.scale, 2.0 * s.scale).astype(f32)


def mix_kernel(s, count, in_ref, weight_ref, out_ref, kept_ref):
    @pl.when(pl.program_id(0) == 0)
    def _():
        spread_modes(s, count, in_ref, kept_ref)

    factor = depth_factor(s, (count, LANES))
    pieces = s.flat // LANES
    block = [[[None] * pieces for _ in range(s.gw)] for _ in range(2)]
    for a in range(pieces):
        at = slice(a * LANES, (a + 1) * LANES)
        reals = [None] * s.gw
        imags = [None] * s.gw
        for i in range(s.ch):
            real = kept_ref[0, i, :, at]
            imag = kept_ref[1, i, :, at]
            for o in range(s.gw):
                w_real = weight_ref[0, i, o, :, at]
                w_imag = weight_ref[1, i, o, :, at]
                new_real = real * w_real - imag * w_imag
                new_imag = real * w_imag + imag * w_real
                reals[o] = new_real if i == 0 else reals[o] + new_real
                imags[o] = new_imag if i == 0 else imags[o] + new_imag
        for o in range(s.gw):
            block[0][o][a] = reals[o] * factor
            block[1][o][a] = imags[o] * factor
    store_block(s, count, block, out_ref)


def store_block(s, count, block, out_ref):
    stride = 2 * s.jxl
    for part in range(2):
        for a in range(s.flat // LANES):
            for b, piece in enumerate(swap_groups([block[part][c][a] for c in range(s.gw)], s.modes)):
                out_ref[0, pl.ds(part * s.jxl + a * s.gw + b, count, stride=stride), :] = piece


def mix(s, modes, spec_weight, mode_chunk):
    count = s.jl // MODE_CHUNKS
    kept_shape = jax.ShapeDtypeStruct((2, s.ch, count, s.flat), f32)
    return pl.pallas_call(
        functools.partial(mix_kernel, s, count),
        grid=(s.chan,),
        in_specs=[
            whole(modes),
            pl.BlockSpec((2, s.ch, s.gw, count, s.flat), lambda g: (0, 0, g, mode_chunk, 0)),
        ],
        out_specs=[
            pl.BlockSpec((1, count * 2 * s.jxl, LANES), lambda g: (g, 0, 0)),
            whole(kept_shape),
        ],
        out_shape=[jax.ShapeDtypeStruct(modes.shape, f32), kept_shape],
        cost_estimate=cost(1e8, modes, modes, spec_weight),
        name="mix",
    )(modes, spec_weight)


def unmix_kernel(s, count, in_ref, weight_ref, out_ref, kept_ref):
    factor = depth_factor(s, (count, LANES))

    @pl.when(pl.program_id(0) == 0)
    def _():
        spread_modes(s, count, in_ref, kept_ref, factor)

    pieces = s.flat // LANES
    block = [[[None] * pieces for _ in range(s.gw)] for _ in range(2)]
    for a in range(pieces):
        at = slice(a * LANES, (a + 1) * LANES)
        reals = [None] * s.gw
        imags = [None] * s.gw
        for o in range(s.ch):
            real = kept_ref[0, o, :, at]
            imag = kept_ref[1, o, :, at]
            for i in range(s.gw):
                w_real = weight_ref[0, i, o, :, at]
                w_imag = weight_ref[1, i, o, :, at]
                new_real = real * w_real + imag * w_imag
                new_imag = imag * w_real - real * w_imag
                reals[i] = new_real if o == 0 else reals[i] + new_real
                imags[i] = new_imag if o == 0 else imags[i] + new_imag
        for i in range(s.gw):
            block[0][i][a] = reals[i]
            block[1][i][a] = imags[i]
    store_block(s, count, block, out_ref)


def unmix(s, modes, spec_weight, mode_chunk):
    count = s.jl // MODE_CHUNKS
    kept_shape = jax.ShapeDtypeStruct((2, s.ch, count, s.flat), f32)
    return pl.pallas_call(
        functools.partial(unmix_kernel, s, count),
        grid=(s.chan,),
        in_specs=[
            whole(modes),
            pl.BlockSpec((2, s.gw, s.ch, count, s.flat), lambda g: (0, g, 0, mode_chunk, 0)),
        ],
        out_specs=[
            pl.BlockSpec((1, count * 2 * s.jxl, LANES), lambda g: (g, 0, 0)),
            whole(kept_shape),
        ],
        out_shape=[jax.ShapeDtypeStruct(modes.shape, f32), kept_shape],
        cost_estimate=cost(1e8, modes, modes, spec_weight),
        name="unmix",
    )(modes, spec_weight)


def weight_kernel(s, width, spec_ref, grad_ref, out_ref):
    for i in range(width):
        for a in range(s.flat // LANES):
            at = slice(a * LANES, (a + 1) * LANES)
            real = spec_ref[0, i, :, at]
            imag = spec_ref[1, i, :, at]
            for o in range(s.ch):
                g_real = grad_ref[0, o, :, at]
                g_imag = grad_ref[1, o, :, at]
                out_ref[0, i, o, :, at] = real * g_real + imag * g_imag
                out_ref[1, i, o, :, at] = real * g_imag - imag * g_real


def weight_grads(s, spec, grad, mode_chunk, total):
    count = s.jl // MODE_CHUNKS
    width = 2
    aliased = [] if total is None else [total]

    def body(spec_ref, grad_ref, *refs):
        weight_kernel(s, width, spec_ref, grad_ref, refs[-1])

    shape = jax.ShapeDtypeStruct((2, s.ch, s.ch, s.jl, s.flat), f32)
    return pl.pallas_call(
        body,
        grid=(s.ch // width,),
        in_specs=[pl.BlockSpec((2, width, count, s.flat), lambda i: (0, i, 0, 0)), whole(grad)]
        + [pl.BlockSpec(memory_space=pl.ANY)] * len(aliased),
        out_specs=pl.BlockSpec((2, width, s.ch, count, s.flat), lambda i: (0, i, 0, mode_chunk, 0)),
        out_shape=shape,
        input_output_aliases={2 + i: i for i in range(len(aliased))},
        cost_estimate=cost(1e8, shape),
        name="weight_grads",
    )(spec, grad, *aliased)


def over_owners(s, value):
    flat = value.reshape((s.owners,) + value.shape[-2:])
    return lax.all_to_all(flat, ("planes", "chan"), 0, 0, tiled=True)


def over_chan(value):
    return lax.all_to_all(value, "chan", 0, 0, tiled=True)


def joined(parts):
    return parts[0] if len(parts) == 1 else jnp.concatenate(parts, 1)


def fast_local(s, field, cotangent, spec_weight, point_weight, bias):
    second = second_tables(s)
    third = third_tables(s)
    forward, inverse = first_tables(s)
    x_chunks = range(X_CHUNKS)
    mode_chunks = range(MODE_CHUNKS)
    by_planes = (s.planes, s.chan)

    arrived = [over_owners(s, analysis(s, field, k, second, third)) for k in x_chunks]
    point = pointwise(field, point_weight, bias)
    owned = [over_chan(first_pass(s, arrived, forward, m)) for m in mode_chunks]
    mixed = [mix(s, owned[m], spec_weight, m) for m in mode_chunks]
    returned = joined([over_chan(v[0]) for v in mixed])
    back = [over_owners(s, v) for v in first_inverse(s, returned, inverse)]
    output = grad = None
    arrived = []
    for k in x_chunks:
        modes = back[k].reshape(by_planes + back[k].shape[1:])
        output, grad, sent = middle(s, modes, point, cotangent, k, second, third, output, grad)
        arrived.append(over_owners(s, sent))
    local_grad = pointwise(grad, point_weight.T, jnp.zeros_like(bias))
    owned = [over_chan(first_pass(s, arrived, forward, m)) for m in mode_chunks]
    unmixed = [unmix(s, owned[m], spec_weight, m) for m in mode_chunks]
    returned = joined([over_chan(v[0]) for v in unmixed])
    weight_grad = None
    for m in mode_chunks:
        weight_grad = weight_grads(s, mixed[m][1], unmixed[m][1], m, weight_grad)
    back = [over_owners(s, v) for v in first_inverse(s, returned, inverse)]
    field_grad = None
    for k in x_chunks:
        modes = back[k].reshape(by_planes + back[k].shape[1:])
        field_grad = final(s, modes, local_grad, k, second, third, field_grad)
    return output, field_grad, weight_grad


def local(field, cotangent, spec_weight, point_weight, bias):
    s = Sizes(field, spec_weight)
    if s.fits():
        return fast_local(s, field, cotangent, spec_weight, point_weight, bias)
    return plain_local(s, field, cotangent, spec_weight, point_weight, bias)


def solution(mesh):
    in_specs = (
        P("groups", None, ("planes", "chan"), None, None),
        P("groups", None, ("planes", "chan"), None, None),
        P(None, None, None, "planes", "chan"),
        P(),
        P(),
    )
    out_specs = (
        P("groups", None, ("planes", "chan"), None, None),
        P("groups", None, ("planes", "chan"), None, None),
        P("groups", None, None, "planes", "chan"),
    )
    return jax.shard_map(local, mesh=mesh, in_specs=in_specs, out_specs=out_specs, check_vma=False)
```

time: 744 us -> 453 us (0.61)
  local copies, waits for them, and re-layouts: 238 us -> 3.87 us
  Pallas kernels: 0 us -> 147 us
  matrix products: 141 us -> 0 us
  blocking collectives: 109 us -> 230 us
  waiting for transfers between devices: 176 us -> 60.8 us
  other arithmetic: 46.7 us -> 0 us
  starting transfers between devices: 24.1 us -> 7.44 us
    pallas_call x0 -> x12, Pallas kernels: none -> 147 us  [the longest x1 29.7 us: middle(): pl.pallas_call(body, grid=(s.chan,), in_specs=[mode_spec(s, lxk), spec, s...]
    dot_general x14 -> x0, matrix products: 141 us -> none  [the longest x2 27.9 us: synthesis(): jnp.einsum(source_form + ',tmuz->bcdxpkuz', returned, third_inverse, prec...]
    all_to_all x3 -> x6, blocking collectives: 109 us -> 230 us  [the longest x4 120 us: over_chan(): return lax.all_to_all(value, 'chan', 0, 0, tiled=True)]
    all_to_all x5 -> x2, waiting for transfers between devices: 176 us -> 60.8 us  [over_owners(): return lax.all_to_all(flat, ('planes', 'chan'), 0, 0, tiled=True)]
    unnamed x71 -> x7, local copies, waits for them, and re-layouts: 68.4 us -> 3.35 us
    another operation x10 -> x1, local copies, waits for them, and re-layouts: 62.7 us -> 0.52 us
    reshape x4 -> x0, local copies, waits for them, and re-layouts: 47.7 us -> none  [the longest x2 24 us: analysis(): first_pass.reshape(batch_size, local_modes, group_width, 2, 2 * MODES * M...]
    all_to_all x11 -> x0, local copies, waits for them, and re-layouts: 30.8 us -> none  [the longest x5 21.8 us: analysis(): lax.all_to_all(first_pass, 'chan', split_axis=4, concat_axis=2, tiled=True)]
  transfers between devices with their start and end apart: 5 -> 2, of which waited for: 5 -> 2; matrix products, arithmetic and copies ran while one was open for 3% -> 0% of each run, Pallas kernels for 0% -> 8%
where the time goes in v1:
time: 453 us; the launch traced here: 451 us
  blocking collectives  230 us (51%)
  Pallas kernels  147 us (32%)
  waiting for transfers between devices  60.8 us (13%)
  starting transfers between devices  7.44 us (2%)
    all_to_all x4, blocking collectives, over_chan(): return lax.all_to_all(value, 'chan', 0, 0, tiled=True)  120 us
    all_to_all x2, blocking collectives, over_owners(): return lax.all_to_all(flat, ('planes', 'chan'), 0, 0, tiled=True)  111 us
    all_to_all x2, waiting for transfers between devices, over_owners(): return lax.all_to_all(flat, ('planes', 'chan'), 0, 0, tiled=True)  60.8 us
    pallas_call x1, Pallas kernels, middle(): pl.pallas_call(body, grid=(s.chan,), in_specs=[mode_spec(s, lxk), spec, s...  29.7 us
    pallas_call x2, Pallas kernels, pointwise(): pl.pallas_call(functools.partial(pointwise_kernel, channels), grid=(lx,),...  27.5 us
    pallas_call x1, Pallas kernels, final(): pl.pallas_call(body, grid=(s.chan,), in_specs=[mode_spec(s, lxk), spec] +...  15.1 us
    pallas_call x1, Pallas kernels, analysis(): pl.pallas_call(functools.partial(analysis_kernel, s, lxk), grid=(s.chan,)...  14.8 us
    pallas_call x1, Pallas kernels, mix(): pl.pallas_call(functools.partial(mix_kernel, s, count), grid=(s.chan,), i...  13 us
  transfers between devices with their start and end apart: 2, of which 2 were waited for; matrix products, arithmetic and copies ran while one was open for 0% of the time, Pallas kernels for 8%

profile of v1, /device:TPU:0, one launch (start us, length us, event | category | flops | bytes accessed | tf_op | source)
XLA Modules:
  0.0 450.5 jit_solution(6418977721966450908)
XLA Ops:
  0.6 14.8 %analysis.1 = f32[4,4,256,128]{3,2,1,0:T(8,128)} custom-call(f32[1,16,8,128,128]{4,3,2,1,0:T(8,128)} %values_ref.1, bf16[256,256]{1,0:T(8,128)(2,1)} %constant.18.clone.second_ref.refs_6_, bf16[1024,256]{1,0:T(8,128)(2,1)} %constant.19.clone.high_ref.refs_7_, bf16[1024,256]{1,0:T(8,128)(2,1)} %constant.20.clone.low_ref.refs_8_), custom_call_target="tpu_custom_call" | custom-call | flops 6000000000 | bytes 10485760 | tf_op jit(solution)/shard_map/analysis/pallas_call | solution.py:423
  15.4 56.8 %all_to_all.40.refs_0_ = f32[16,256,128]{2,1,0:T(8,128)} all-to-all(f32[16,256,128]{2,1,0:T(8,128)} %bitcast.8), channel_id=1, replica_groups=mesh['groups'=2,'planes'=4,'chan'=4] {'planes','chan'}, dimensions={0} | all-to-all | bytes 4194304 | tf_op jit(solution)/shard_map/all_to_all | solution.py:766
  72.3 6.2 %first_forward.2 = f32[4,512,128]{2,1,0:T(8,128)} custom-call(f32[16,256,128]{2,1,0:T(8,128)} %all_to_all.40.refs_0_, bf16[256,256]{1,0:T(8,128)(2,1)} %constant.21.clone.refs_1_), custom_call_target="tpu_custom_call" | custom-call | flops 1000000000 | bytes 3145728 | tf_op jit(solution)/shard_map/first_forward/pallas_call | solution.py:539
  78.5 30.3 %all_to_all.41.in_ref = f32[4,512,128]{2,1,0:T(8,128)} all-to-all(f32[4,512,128]{2,1,0:T(8,128)} %first_forward.2), channel_id=1, replica_groups=mesh['groups'=2,'planes'=4,'chan'=4] {'chan'}, dimensions={0} | all-to-all | bytes 2097152 | tf_op jit(solution)/shard_map/all_to_all | solution.py:770
  108.8 13.0 %mix.1 = (f32[4,512,128]{2,1,0:T(8,128)}, f32[2,16,16,512]{3,2,1,0:T(8,128)}) custom-call(f32[4,512,128]{2,1,0:T(8,128)} %all_to_all.41.in_ref, f32[2,16,16,16,512]{4,3,2,1,0:T(8,128)} %weight_ref.5), custom_call_target="tpu_custom_call" | custom-call | flops 100000000 | bytes 18874368 | tf_op jit(solution)/shard_map/mix/pallas_call | solution.py:663
  121.8 29.6 %all_to_all.42.in_ref = f32[4,512,128]{2,1,0:T(8,128)} all-to-all(f32[4,512,128]{2,1,0:T(8,128)} %get-tuple-element.10), channel_id=1, replica_groups=mesh['groups'=2,'planes'=4,'chan'=4] {'chan'}, dimensions={0} | all-to-all | bytes 2097152 | tf_op jit(solution)/shard_map/all_to_all | solution.py:770
  151.4 6.3 %first_inverse.2 = f32[16,256,128]{2,1,0:T(8,128)} custom-call(f32[4,512,128]{2,1,0:T(8,128)} %all_to_all.42.in_ref, bf16[512,256]{1,0:T(8,128)(2,1)} %constant.22.clone.refs_0_), custom_call_target="tpu_custom_call" | custom-call | flops 1000000000 | bytes 6291456 | tf_op jit(solution)/shard_map/first_inverse/pallas_call | solution.py:575
  157.7 3.7 all-to-all-start.3
  161.4 13.8 %pointwise.2.refs_1_ = f32[1,16,8,128,128]{4,3,2,1,0:T(8,128)} custom-call(f32[1,16,8,128,128]{4,3,2,1,0:T(8,128)} %values_ref.1, f32[16,16]{1,0:T(8,128)} %weight_ref.4, f32[16]{0:T(128)} %bias_ref.1), custom_call_target="tpu_custom_call" | custom-call | flops 10000000000 | bytes 16777216 | tf_op jit(solution)/shard_map/pointwise/pallas_call | solution.py:503
  175.2 35.5 %all-to-all-done.3 = f32[16,256,128]{2,1,0:T(8,128)S(1)} async-done(((f32[16,256,128]{2,1,0:T(8,128)}), f32[16,256,128]{2,1,0:T(8,128)S(1)}, u32[]{:S(2)}, u32[]{:S(2)}) %all-to-all-start.3) | async-done | bytes 2097184 | tf_op jit(solution)/shard_map/all_to_all | solution.py:766
  210.7 1.3 copy-done.1
  212.1 29.7 %middle.1 = (f32[1,16,8,128,128]{4,3,2,1,0:T(8,128)}, f32[1,16,8,128,128]{4,3,2,1,0:T(8,128)}, f32[4,4,256,128]{3,2,1,0:T(8,128)}) custom-call(f32[4,4,256,128]{3,2,1,0:T(8,128)} %bitcast.6, f32[1,16,8,128,128]{4,3,2,1,0:T(8,128)} %pointwise.2.refs_1_, f32[1,16,8,128,128]{4,3,2,1,0:T(8,128)} %refs_2_.2, bf16[4,256,256]{2,1,0:T(8,128)(2,1)} %constant.23.clone.refs_3_.refs_2_, ...), custom_call_target="tpu_custom_call" | custom-call | flops 12000000000 | bytes 35651584 | tf_op jit(solution)/shard_map/middle/pallas_call | solution.py:446
  241.8 53.8 %all_to_all.43.refs_0_ = f32[16,256,128]{2,1,0:T(8,128)} all-to-all(f32[16,256,128]{2,1,0:T(8,128)} %bitcast.7), channel_id=1, replica_groups=mesh['groups'=2,'planes'=4,'chan'=4] {'planes','chan'}, dimensions={0} | all-to-all | bytes 4194304 | tf_op jit(solution)/shard_map/all_to_all | solution.py:766
  295.5 6.3 %first_forward.3 = f32[4,512,128]{2,1,0:T(8,128)} custom-call(f32[16,256,128]{2,1,0:T(8,128)} %all_to_all.43.refs_0_, bf16[256,256]{1,0:T(8,128)(2,1)} %constant.21.clone.refs_1_), custom_call_target="tpu_custom_call" | custom-call | flops 1000000000 | bytes 3145728 | tf_op jit(solution)/shard_map/first_forward/pallas_call | solution.py:539
  301.8 30.2 %all_to_all.44.in_ref = f32[4,512,128]{2,1,0:T(8,128)} all-to-all(f32[4,512,128]{2,1,0:T(8,128)} %first_forward.3), channel_id=1, replica_groups=mesh['groups'=2,'planes'=4,'chan'=4] {'chan'}, dimensions={0} | all-to-all | bytes 2097152 | tf_op jit(solution)/shard_map/all_to_all | solution.py:770
  332.0 13.0 %unmix.1 = (f32[4,512,128]{2,1,0:T(8,128)}, f32[2,16,16,512]{3,2,1,0:T(8,128)}) custom-call(f32[4,512,128]{2,1,0:T(8,128)} %all_to_all.44.in_ref, f32[2,16,16,16,512]{4,3,2,1,0:T(8,128)} %weight_ref.5), custom_call_target="tpu_custom_call" | custom-call | flops 100000000 | bytes 18874368 | tf_op jit(solution)/shard_map/unmix/pallas_call | solution.py:712
  345.0 29.7 %all_to_all.45.in_ref = f32[4,512,128]{2,1,0:T(8,128)} all-to-all(f32[4,512,128]{2,1,0:T(8,128)} %get-tuple-element.13), channel_id=1, replica_groups=mesh['groups'=2,'planes'=4,'chan'=4] {'chan'}, dimensions={0} | all-to-all | bytes 2097152 | tf_op jit(solution)/shard_map/all_to_all | solution.py:770
  374.7 6.3 %first_inverse.3 = f32[16,256,128]{2,1,0:T(8,128)} custom-call(f32[4,512,128]{2,1,0:T(8,128)} %all_to_all.45.in_ref, bf16[512,256]{1,0:T(8,128)(2,1)} %constant.22.clone.refs_0_), custom_call_target="tpu_custom_call" | custom-call | flops 1000000000 | bytes 6291456 | tf_op jit(solution)/shard_map/first_inverse/pallas_call | solution.py:575
  381.0 3.7 all-to-all-start.7
  385.9 13.7 %pointwise.3.refs_1_ = f32[1,16,8,128,128]{4,3,2,1,0:T(8,128)} custom-call(f32[1,16,8,128,128]{4,3,2,1,0:T(8,128)} %get-tuple-element.14.values_ref, f32[16,16]{1,0:T(8,128)} %bitcast.9, f32[16]{0:T(128)} %broadcast_1_bias_ref.2.bias_ref), custom_call_target="tpu_custom_call" | custom-call | flops 10000000000 | bytes 16777216 | tf_op jit(solution)/shard_map/pointwise/pallas_call | solution.py:503
  399.7 9.1 %weight_grads.1 = f32[2,16,16,16,512]{4,3,2,1,0:T(8,128)} custom-call(f32[2,16,16,512]{3,2,1,0:T(8,128)} %get-tuple-element.15.spec_ref, f32[2,16,16,512]{3,2,1,0:T(8,128)} %get-tuple-element.16.grad_ref), custom_call_target="tpu_custom_call" | custom-call | flops 100000000 | bytes 16777216 | tf_op jit(solution)/shard_map/weight_grads/pallas_call | solution.py:751
  408.8 25.3 %all-to-all-done.7 = f32[16,256,128]{2,1,0:T(8,128)S(1)} async-done(((f32[16,256,128]{2,1,0:T(8,128)}), f32[16,256,128]{2,1,0:T(8,128)S(1)}, u32[]{:S(2)}, u32[]{:S(2)}) %all-to-all-start.7) | async-done | bytes 2097184 | tf_op jit(solution)/shard_map/all_to_all | solution.py:766
  434.0 1.4 copy-done
  435.4 15.1 %final.1 = f32[1,16,8,128,128]{4,3,2,1,0:T(8,128)} custom-call(f32[4,4,256,128]{3,2,1,0:T(8,128)} %bitcast.5, f32[1,16,8,128,128]{4,3,2,1,0:T(8,128)} %pointwise.3.refs_1_, bf16[4,256,256]{2,1,0:T(8,128)(2,1)} %constant.23.clone.refs_3_.refs_2_, bf16[4,256,256]{2,1,0:T(8,128)(2,1)} %constant.24.clone.refs_4_.refs_3_, ...), custom_call_target="tpu_custom_call" | custom-call | flops 6000000000 | bytes 18874368 | tf_op jit(solution)/shard_map/final/pallas_call | solution.py:471
  (6 shorter events, 1.2 us)
Async XLA Ops:
  157.7 53.0 %all-to-all-start.3 = ((f32[16,256,128]{2,1,0:T(8,128)}), f32[16,256,128]{2,1,0:T(8,128)S(1)}, u32[]{:S(2)}, u32[]{:S(2)}) async-start(f32[16,256,128]{2,1,0:T(8,128)} %first_inverse.2), calls=%async_computation.3 | async-start | bytes 4194304 | tf_op jit(solution)/shard_map/all_to_all | solution.py:766
  210.7 1.3 copy-start.1
  345.0 39.8 %copy-start.2 = (f32[16,16]{1,0:T(8,128)S(1)}, f32[16,16]{1,0:T(8,128)}, u32[]{:S(2)}) copy-start(f32[16,16]{1,0:T(8,128)} %weight_ref.4) | copy-start | bytes 3076
  381.0 53.0 %all-to-all-start.7 = ((f32[16,256,128]{2,1,0:T(8,128)}), f32[16,256,128]{2,1,0:T(8,128)S(1)}, u32[]{:S(2)}, u32[]{:S(2)}) async-start(f32[16,256,128]{2,1,0:T(8,128)} %first_inverse.3), calls=%async_computation.7 | async-start | bytes 4194304 | tf_op jit(solution)/shard_map/all_to_all | solution.py:766
  434.0 1.4 copy-start

commit v2 on v0

v2 whole, which is shorter than its diff:
```python
import functools
import math

import numpy as np

import jax
import jax.numpy as jnp
from jax import lax
from jax.experimental import pallas as pl
from jax.experimental.pallas import tpu as pltpu
from jax.sharding import PartitionSpec as P


exact_mode = lax.Precision.HIGHEST


def retained(s, length):
    indices = jnp.arange(2 * s.modes)
    return jnp.where(indices < s.modes, indices, length - 2 * s.modes + indices)


def phase_table(positions, freqs, length):
    turn_count = positions[:, None] * freqs[None, :] % length
    angles = turn_count.astype(jnp.float32) * (2.0 * math.pi / length)
    return (jnp.cos(angles), jnp.sin(angles))


def plain_analysis(s, field):
    batch_size, channels, local_planes, second_length, third_length = field.shape
    plane_count = lax.axis_size("planes")
    channel_groups = lax.axis_size("chan")
    group_width = channels // channel_groups
    local_modes = 2 * s.modes // plane_count
    first_length = local_planes * plane_count * channel_groups
    cosine, sine_part = phase_table(
        jnp.arange(second_length), retained(s, second_length), second_length
    )
    second_table = jnp.stack([cosine, -sine_part], 1).reshape(
        second_length, 2, plane_count, local_modes
    )
    cosine, sine_part = phase_table(jnp.arange(third_length), jnp.arange(s.modes), third_length)
    third_table = jnp.stack(
        [jnp.stack([cosine, -sine_part], 1), jnp.stack([sine_part, cosine], 1)], 0
    )
    grouped = field.reshape(
        batch_size, channel_groups, group_width, local_planes, second_length, third_length
    )
    second_pass = jnp.einsum("bcdxyz,yspk->bcdxspkz", grouped, second_table, precision=exact_mode)
    spectra = jnp.einsum("bcdxspkz,sztm->bpckxdtm", second_pass, third_table, precision=exact_mode)
    spectra = spectra.reshape(
        batch_size, plane_count * channel_groups, local_modes, local_planes, group_width * 2 * s.modes
    )
    arrived = lax.all_to_all(spectra, ("planes", "chan"), split_axis=1, concat_axis=3, tiled=True)
    positions = jnp.arange(first_length)
    arrived = arrived.reshape(batch_size, local_modes, first_length, group_width, 2, s.modes)
    cosine, sine_part = phase_table(positions, retained(s, first_length), first_length)
    first_table = jnp.stack(
        [jnp.stack([cosine, -sine_part], 1), jnp.stack([sine_part, cosine], 1)], 1
    )
    first_pass = jnp.einsum("bkxdsm,xstf->bkdtfm", arrived, first_table, precision=exact_mode)
    first_pass = first_pass.reshape(batch_size, local_modes, group_width, 2, 2 * s.modes * s.modes)
    return lax.all_to_all(first_pass, "chan", split_axis=4, concat_axis=2, tiled=True)


def plain_synthesis(s, spectrum):
    batch_size, local_modes, channels = (spectrum.shape[0], spectrum.shape[1], spectrum.shape[2])
    plane_count = lax.axis_size("planes")
    channel_groups = lax.axis_size("chan")
    group_width = channels // channel_groups
    local_planes = s.gx // (plane_count * channel_groups)
    gathered = lax.all_to_all(spectrum, "chan", split_axis=2, concat_axis=4, tiled=True)
    gathered = gathered.reshape(batch_size, local_modes, group_width, 2, 2 * s.modes, s.modes)
    cosine, sine_part = phase_table(jnp.arange(s.gx), retained(s, s.gx), s.gx)
    cosine_t = cosine.T
    sine_t = sine_part.T
    first_inverse = jnp.stack(
        [jnp.stack([cosine_t, sine_t], -1), jnp.stack([-sine_t, cosine_t], -1)], 0
    )
    first_pass = jnp.einsum("bkdsfm,sfxt->bkxdtm", gathered, first_inverse, precision=exact_mode)
    first_pass = first_pass.reshape(batch_size, local_modes, s.gx, group_width * 2 * s.modes)
    returned = lax.all_to_all(
        first_pass[:, None], ("planes", "chan"), split_axis=3, concat_axis=1, tiled=True
    )
    returned = returned.reshape(
        batch_size, plane_count, channel_groups, local_modes, local_planes, group_width, 2, s.modes
    )
    source_form = "bpckxdtm"
    cosine, sine_part = phase_table(jnp.arange(s.gz), jnp.arange(s.modes), s.gz)
    cosine_t = cosine.T
    sine_t = sine_part.T
    third_inverse = jnp.stack(
        [jnp.stack([cosine_t, sine_t], 1), jnp.stack([-sine_t, cosine_t], 1)], 0
    )
    depth_pass = jnp.einsum(
        source_form + ",tmuz->bcdxpkuz", returned, third_inverse, precision=exact_mode
    )
    cosine, sine_part = phase_table(jnp.arange(s.gy), retained(s, s.gy), s.gy)
    second_inverse = jnp.stack([cosine.T, -sine_part.T], 0).reshape(2, plane_count, local_modes, s.gy)
    physical = jnp.einsum("bcdxpkuz,upky->bcdxyz", depth_pass, second_inverse, precision=exact_mode)
    return physical.reshape(batch_size, channels, local_planes, s.gy, s.gz)


def mode_weighting(s, mode_count):
    depth_mode = jnp.arange(mode_count) % s.modes
    return jnp.where(depth_mode == 0, 1.0, 2.0).astype(jnp.float32) / float(s.gx * s.gy * s.gz)


def contract(operand, weights):
    return jnp.einsum("bkin,iokn->bkon", operand, weights, precision=exact_mode)


def adjoint(operand, weights):
    return jnp.einsum("bkon,iokn->bkin", operand, weights, precision=exact_mode)


def outer_sum(first_operand, second_operand):
    return jnp.einsum("bkin,bkon->iokn", first_operand, second_operand, precision=exact_mode)


def plain_local(s, field, cotangent, spec_weight, point_weight, bias):
    spectrum = plain_analysis(s, field)
    weight_re = spec_weight[0]
    weight_im = spec_weight[1]
    spec_re = spectrum[:, :, :, 0]
    spec_im = spectrum[:, :, :, 1]
    weighting = mode_weighting(s, spectrum.shape[-1])
    mixed_re = (contract(spec_re, weight_re) - contract(spec_im, weight_im)) * weighting
    mixed_im = (contract(spec_re, weight_im) + contract(spec_im, weight_re)) * weighting
    mixed_modes = jnp.stack([mixed_re, mixed_im], 3)
    spectral = plain_synthesis(s, mixed_modes)
    pointwise = jnp.einsum("bixyz,io->boxyz", field, point_weight, precision=exact_mode)
    preactivation = spectral + pointwise + bias[None, :, None, None, None]
    normal_cdf = 0.5 * (1.0 + lax.erf(preactivation * (1.0 / math.sqrt(2.0))))
    output = preactivation * normal_cdf
    derivative = normal_cdf + preactivation * jnp.exp(-0.5 * preactivation * preactivation) * (
        1.0 / math.sqrt(2.0 * math.pi)
    )
    pre_grad = cotangent * derivative
    raw_grad = plain_analysis(s, pre_grad)
    grad_re = raw_grad[:, :, :, 0] * weighting
    grad_im = raw_grad[:, :, :, 1] * weighting
    spectrum_grad = jnp.stack(
        [
            adjoint(grad_re, weight_re) + adjoint(grad_im, weight_im),
            adjoint(grad_im, weight_re) - adjoint(grad_re, weight_im),
        ],
        3,
    )
    weight_grad = jnp.stack(
        [
            outer_sum(spec_re, grad_re) + outer_sum(spec_im, grad_im),
            outer_sum(spec_re, grad_im) - outer_sum(spec_im, grad_re),
        ],
        0,
    )
    local_grad = jnp.einsum("boxyz,io->bixyz", pre_grad, point_weight, precision=exact_mode)
    field_grad = local_grad + plain_synthesis(s, spectrum_grad)
    return (output, field_grad, weight_grad)


LANES = 128
BLOCK = 4
MODE_CHUNKS = 2
f32 = jnp.float32
bf16 = jnp.bfloat16


class Sizes:
    def __init__(self, field, spec_weight):
        self.planes = lax.axis_size("planes")
        self.chan = lax.axis_size("chan")
        self.owners = self.planes * self.chan
        _, self.ch, self.lx, self.gy, self.gz = field.shape
        self.gx = self.lx * self.owners
        _, _, _, self.jl, local_flat = spec_weight.shape
        self.jy = self.jl * self.planes
        self.flat = local_flat
        self.modes = self.jy // 2
        self.jxl = local_flat // self.modes
        self.jx = self.jxl * self.chan
        self.gw = self.ch // self.chan
        self.scale = 1.0 / float(self.gx * self.gy * self.gz)

    def fits(self):
        return (
            self.gw == 4
            and self.gw * self.modes == LANES
            and self.gz == LANES
            and self.gy == LANES
            and self.jy * 2 == LANES
            and self.jx * 2 == LANES
            and self.flat % LANES == 0
            and self.ch * 16 == 2 * LANES
            and self.jl % (8 * MODE_CHUNKS) == 0
            and self.lx % (2 * BLOCK) == 0
            and self.gx == LANES
            and self.chan & (self.chan - 1) == 0
            and self.planes & (self.planes - 1) == 0
        )


def kept(count, length):
    index = np.arange(count)
    return np.where(index < count // 2, index, length - count + index)


def waves(freqs, length):
    turns = (freqs[:, None] * np.arange(length)[None, :]) % length
    angles = turns * (2.0 * math.pi / length)
    return np.cos(angles), np.sin(angles)


def two_terms(table):
    table = np.asarray(table, np.float32)
    high = table.astype(jnp.bfloat16)
    low = (table - high.astype(np.float32)).astype(jnp.bfloat16)
    return high, low


def stacked_square(table):
    high, low = two_terms(table)
    return np.concatenate([np.concatenate([high, high], 1), np.concatenate([low, low], 1)], 0)


def second_tables(s):
    cosine, sine = waves(kept(s.jy, s.gy), s.gy)
    forward = np.concatenate([cosine, sine], 0)
    inverse = np.concatenate(
        [np.concatenate([cosine.T, -sine.T], 1), np.concatenate([sine.T, cosine.T], 1)], 0
    )
    return stacked_square(forward), stacked_square(inverse)


def third_tables(s):
    cosine, sine = waves(np.arange(s.modes), s.gz)
    table = np.zeros((2, s.gz, 2, 2, s.modes))
    for c in range(2):
        table[c, :, 0, c] = cosine.T
        table[c, :, 1, c] = -sine.T
    table = table.reshape(2 * s.gz, LANES)
    forward = np.concatenate(two_terms(table), 1)
    high, low = two_terms(table.T)
    wide = np.concatenate([high, low], 1)
    return forward, np.concatenate([wide, wide], 0)


def first_tables(s):
    cosine, sine = waves(kept(s.jx, s.gx), s.gx)
    c4 = cosine.reshape(s.chan, s.jxl, s.owners, s.lx)
    s4 = sine.reshape(s.chan, s.jxl, s.owners, s.lx)
    forward = np.zeros((s.chan, 2, s.jxl, s.owners, 2, s.lx))
    inverse = np.zeros((s.owners, 2, s.lx, s.chan, 2, s.jxl))
    for out, inp, sign, wave in ((0, 0, 1, c4), (0, 1, 1, s4), (1, 0, -1, s4), (1, 1, 1, c4)):
        forward[:, out, :, :, inp] = sign * wave
        inverse[:, inp, :, :, out] = sign * wave.transpose(2, 3, 0, 1)
    rows = s.chan * 2 * s.jxl
    return forward.reshape(rows, -1), inverse.reshape(-1, rows)


def terms(value):
    high = value.astype(bf16)
    return high, (value - high.astype(f32)).astype(bf16)


def dot(a, b):
    return jnp.dot(a, b, preferred_element_type=f32)


def square_dot(table, value):
    high, low = terms(value)
    both = dot(table, jnp.concatenate([high, low], 0))
    half = both.shape[0] // 2
    return both[:half] + both[half:]


def gelu_parts(v):
    normal_cdf = 0.5 * (1.0 + lax.erf(v * (1.0 / math.sqrt(2.0))))
    slope = normal_cdf + v * jnp.exp(-0.5 * v * v) * (1.0 / math.sqrt(2.0 * math.pi))
    return normal_cdf, slope


def half_lanes(shape):
    return lax.broadcasted_iota(jnp.int32, shape, 1) < LANES // 2


def place_terms(s, row, value, split):
    half = split.shape[0] // 2
    high, low = terms(value)
    split[pl.ds(pl.multiple_of(row * s.gy, s.gy), s.gy), :] = high
    split[pl.ds(pl.multiple_of(half + row * s.gy, s.gy), s.gy), :] = low


def forward_planes(s, split, third_ref, second_ref, held):
    half = split.shape[0] // 2
    both = dot(split[...], third_ref[...])
    deep = both[:half, :LANES] + both[:half, LANES:] + both[half:, :LANES]
    first = half_lanes((s.jy, LANES))
    for x in range(BLOCK):
        side = [deep[(2 * x + q) * s.gy:(2 * x + q + 1) * s.gy] for q in range(2)]
        out = square_dot(second_ref[...], jnp.concatenate(side, 1))
        pairs = []
        for k in range(2):
            turned = pltpu.roll(out[s.jy:, k * LANES:(k + 1) * LANES], LANES // 2, 1)
            pairs.append(out[:s.jy, k * LANES:(k + 1) * LANES] + jnp.where(first, turned, -turned))
        rows = slice(x * s.jy, (x + 1) * s.jy)
        held[rows, :LANES] = jnp.where(first, pairs[0], pltpu.roll(pairs[1], LANES // 2, 1))
        held[rows, LANES:] = jnp.where(first, pltpu.roll(pairs[0], LANES // 2, 1), pairs[1])


def scatter_modes(s, outs, held):
    me = lax.axis_index("planes")
    first = pl.program_id(1) * BLOCK
    for k, group in enumerate(outs):

        @pl.when(pl.program_id(0) == k)
        def _(group=group):
            for d, out_ref in enumerate(group):
                for x in range(BLOCK):
                    at = pl.ds(pl.multiple_of(x * s.jy + (me ^ d) * s.jl, s.jl), s.jl)
                    for part in range(2):
                        rows = pl.ds(part * s.lx + first + x, s.jl, stride=2 * s.lx)
                        out_ref[rows, :] = held[at, part * LANES:(part + 1) * LANES]


def gather_modes(s, ins, gathered):
    me = lax.axis_index("planes")
    first = pl.program_id(1) * BLOCK
    for k, group in enumerate(ins):

        @pl.when(pl.program_id(0) == k)
        def _(group=group):
            for d, in_ref in enumerate(group):
                for x in range(BLOCK):
                    for part in range(2):
                        at = pl.ds(pl.multiple_of(part * s.jy + (me ^ d) * s.jl, s.jl), s.jl)
                        rows = pl.ds(part * s.lx + first + x, s.jl, stride=2 * s.lx)
                        gathered[x // 2, at, (x % 2) * LANES:(x % 2 + 1) * LANES] = in_ref[rows, :]


def by_group(s, refs):
    return [refs[k:k + s.planes] for k in range(0, len(refs), s.planes)]


def inverse_planes(s, gathered, second_ref, third_ref, planes):
    first = half_lanes((s.gy, LANES))
    sides = []
    for step in range(BLOCK // 2):
        out = square_dot(second_ref[...], gathered[step])
        for k in range(2):
            real = out[:s.gy, k * LANES:(k + 1) * LANES]
            imag = out[s.gy:, k * LANES:(k + 1) * LANES]
            for side in (
                jnp.where(first, real, pltpu.roll(imag, LANES // 2, 1)),
                jnp.where(first, pltpu.roll(real, LANES // 2, 1), imag),
            ):
                high, low = terms(side)
                sides.append(jnp.concatenate([high, low], 1))
    both = dot(jnp.concatenate(sides, 0), third_ref[...])
    planes[...] = both[:, :2 * s.gz] + both[:, 2 * s.gz:]


def plane_rows(s, row):
    return pl.ds(pl.multiple_of(row * s.gy, s.gy), s.gy)


def analysis_kernel(s, field_ref, third_ref, second_ref, outs, split, held):
    for x in range(BLOCK):
        for q in range(2):
            tile = jnp.concatenate([field_ref[0, 2 * q, x], field_ref[0, 2 * q + 1, x]], 1)
            place_terms(s, 2 * x + q, tile, split)
    forward_planes(s, split, third_ref, second_ref, held)
    scatter_modes(s, outs, held)


def middle_kernel(
    s, ins, point_ref, cot_ref, inv_second, inv_third, third_ref, second_ref,
    output_ref, grad_ref, outs, gathered, planes, split, held,
):
    gather_modes(s, ins, gathered)
    inverse_planes(s, gathered, inv_second, inv_third, planes)

    def one(x, carry):
        for q in range(2):
            grads = []
            for c in range(2):
                v = planes[plane_rows(s, 2 * x + q), c * s.gz:(c + 1) * s.gz] + point_ref[0, 2 * q + c, x]
                normal_cdf, slope = gelu_parts(v)
                output_ref[0, 2 * q + c, x] = v * normal_cdf
                grad = cot_ref[0, 2 * q + c, x] * slope
                grad_ref[0, 2 * q + c, x] = grad
                grads.append(grad)
            place_terms(s, 2 * x + q, jnp.concatenate(grads, 1), split)
        return carry

    lax.fori_loop(0, BLOCK, one, 0)
    forward_planes(s, split, third_ref, second_ref, held)
    scatter_modes(s, outs, held)


def final_kernel(s, ins, local_ref, inv_second, inv_third, out_ref, gathered, planes):
    gather_modes(s, ins, gathered)
    inverse_planes(s, gathered, inv_second, inv_third, planes)

    def one(x, carry):
        for q in range(2):
            for c in range(2):
                out_ref[0, 2 * q + c, x] = (
                    planes[plane_rows(s, 2 * x + q), c * s.gz:(c + 1) * s.gz] + local_ref[0, 2 * q + c, x]
                )
        return carry

    lax.fori_loop(0, BLOCK, one, 0)


def whole(array):
    rank = len(array.shape)
    return pl.BlockSpec(array.shape, lambda *_: (0,) * rank, pipeline_mode=pl.Buffered(1))


def cost(flops, *arrays):
    count = sum(int(np.prod(a.shape)) * a.dtype.itemsize for a in arrays)
    return pl.CostEstimate(flops=int(flops), bytes_accessed=count, transcendentals=0)


def anywhere():
    return pl.BlockSpec(memory_space=pl.ANY)


def chan_index():
    return lax.axis_index("chan").astype(jnp.int32).reshape(1)


def grid_spec(s, start):
    return pl.BlockSpec(
        (1, s.gw, BLOCK, s.gy, s.gz), lambda k, x, me: (0, me[0] ^ (start + k), x, 0, 0)
    )


def mode_shape(s):
    return jax.ShapeDtypeStruct((s.jl * 2 * s.lx, LANES), f32)


def forward_scratch(s):
    return [
        pltpu.VMEM((2 * BLOCK * 2 * s.gy, 2 * s.gz), bf16),
        pltpu.VMEM((BLOCK * s.jy, 2 * LANES), f32),
    ]


def inverse_scratch(s):
    return [
        pltpu.VMEM((BLOCK // 2, 2 * s.jy, 2 * LANES), f32),
        pltpu.VMEM((BLOCK * 2 * s.gy, 2 * s.gz), f32),
    ]


def group_call(s, groups, body, in_specs, out_specs, out_shape, scratch, aliases, estimate, operands):
    return pl.pallas_call(
        body,
        grid_spec=pltpu.PrefetchScalarGridSpec(
            num_scalar_prefetch=1,
            grid=(groups, s.lx // BLOCK),
            in_specs=in_specs,
            out_specs=out_specs,
            scratch_shapes=scratch,
        ),
        out_shape=out_shape,
        input_output_aliases=aliases,
        cost_estimate=estimate,
    )(chan_index(), *operands)


def analysis(s, field, second, third):
    tables = (third[0], second[0])
    out = mode_shape(s)
    count = 1 + len(tables)

    def body(me_ref, *refs):
        analysis_kernel(s, *refs[:count], by_group(s, refs[count:-2]), *refs[-2:])

    return by_group(s, group_call(
        s, s.chan, body,
        [grid_spec(s, 0)] + [whole(t) for t in tables],
        [whole(out)] * s.owners,
        [out] * s.owners,
        forward_scratch(s),
        {},
        cost(6e9, *[out] * 80),
        (field, *tables),
    ))


def middle(s, modes, point, cotangent, start, second, third, totals):
    tables = (second[1], third[1], third[0], second[0])
    out = mode_shape(s)
    spec = grid_spec(s, start)
    sources = len(modes)
    count = sources + 2 + len(tables)

    def body(me_ref, *refs):
        rest = refs[count + len(totals):]
        middle_kernel(
            s, by_group(s, refs[:sources]), *refs[sources:count], rest[0], rest[1],
            by_group(s, rest[2:-4]), *rest[-4:],
        )

    grid = jax.ShapeDtypeStruct(point.shape, f32)
    results = group_call(
        s, sources // s.planes, body,
        [whole(out)] * sources + [spec, spec] + [whole(t) for t in tables] + [anywhere()] * len(totals),
        [spec, spec] + [whole(out)] * sources,
        [grid, grid] + [out] * sources,
        inverse_scratch(s) + forward_scratch(s),
        {1 + count + i: i for i in range(len(totals))},
        cost(6e9, *[out] * 144),
        (*modes, point, cotangent, *tables, *totals),
    )
    return results[:2], by_group(s, results[2:])


def final(s, modes, local_grad, start, second, third, totals):
    tables = (second[1], third[1])
    out = mode_shape(s)
    spec = grid_spec(s, start)
    sources = len(modes)
    count = sources + 1 + len(tables)

    def body(me_ref, *refs):
        final_kernel(s, by_group(s, refs[:sources]), *refs[sources:count], *refs[count + len(totals):])

    return group_call(
        s, sources // s.planes, body,
        [whole(out)] * sources + [spec] + [whole(t) for t in tables] + [anywhere()] * len(totals),
        [spec],
        [jax.ShapeDtypeStruct(local_grad.shape, f32)],
        inverse_scratch(s),
        {1 + count + i: i for i in range(len(totals))},
        cost(3e9, *[out] * 72),
        (*modes, local_grad, *tables, *totals),
    )


def pointwise_kernel(values_ref, mixing_ref, bias_ref, out_ref):
    channels, strip = values_ref.shape[1], mixing_ref.shape[1] // values_ref.shape[1]
    rows = channels * strip

    def strips(step, carry):
        at = [pl.ds(pl.multiple_of((2 * step + k) * strip, strip), strip) for k in range(2)]
        value = jnp.concatenate([values_ref[0, :, 0, a, :].reshape(rows, LANES) for a in at], 1)
        high, low = terms(value)
        both = dot(mixing_ref[...], high)
        out = both[:rows] + both[rows:] + dot(mixing_ref[:rows, :], low)
        for k in range(2):
            one = out[:, k * LANES:(k + 1) * LANES] + bias_ref[...]
            out_ref[0, :, 0, at[k], :] = one.reshape(channels, strip, LANES)
        return carry

    lax.fori_loop(0, values_ref.shape[3] // (2 * strip), strips, 0, unroll=True)


def pointwise(values, weight, bias):
    _, channels, lx, gy, gz = values.shape
    strip = 2 * LANES // channels
    mixing = jnp.kron(weight.T, jnp.eye(strip, dtype=f32))
    high = lax.reduce_precision(mixing, 8, 7)
    mixing = jnp.concatenate([high.astype(bf16), (mixing - high).astype(bf16)], 0)
    bias_rows = jnp.broadcast_to(jnp.repeat(bias, strip)[:, None], (channels * strip, LANES))
    spec = pl.BlockSpec((1, channels, 1, gy, gz), lambda x: (0, 0, x, 0, 0))
    return pl.pallas_call(
        pointwise_kernel,
        grid=(lx,),
        in_specs=[spec, whole(mixing), whole(bias_rows)],
        out_specs=spec,
        out_shape=jax.ShapeDtypeStruct(values.shape, f32),
        cost_estimate=cost(6e9, values, values),
        name="pointwise",
    )(values, mixing, bias_rows)


def distances(s):
    return [(p, c) for p in range(s.planes) for c in range(s.chan)]


def owner_rows(s, p, c, step):
    owner = (lax.axis_index("planes") ^ p) * s.chan + (lax.axis_index("chan") ^ c)
    return pl.ds(pl.multiple_of(owner * step, step), step)


def first_kernel(s, ins, stacked_ref, outs, gathered, held):
    me = lax.axis_index("chan")
    rows = held.shape[0]
    per = 2 * s.lx
    for in_ref, (p, c) in zip(ins, distances(s)):
        for j in range(2):
            gathered[owner_rows(s, p, c, per), j * LANES:(j + 1) * LANES] = in_ref[j * per:(j + 1) * per, :]
    high, low = terms(gathered[...])
    both = dot(stacked_ref[...], high)
    held[...] = both[:rows] + both[rows:] + dot(stacked_ref[:rows, :], low)
    step = rows // s.chan
    for d, out_ref in enumerate(outs):
        at = pl.ds(pl.multiple_of((me ^ d) * step, step), step)
        for j in range(2):
            out_ref[j * step:(j + 1) * step, :] = held[at, j * LANES:(j + 1) * LANES]


def first_pass(s, arrived, table, mode_chunk, after):
    rows = table.shape[0]
    stacked = np.concatenate(two_terms(table), 0)
    pairs = s.jl // MODE_CHUNKS // 2
    out = jax.ShapeDtypeStruct((pairs * 2 * 2 * s.jxl, LANES), f32)
    offset = mode_chunk * pairs

    def body(*refs):
        outs = refs[s.owners + 1 + len(after):-2]
        first_kernel(s, refs[:s.owners], refs[s.owners], outs, *refs[-2:])

    return pl.pallas_call(
        body,
        grid=(pairs,),
        in_specs=[pl.BlockSpec((4 * s.lx, LANES), lambda j: (j + offset, 0))] * s.owners
        + [whole(stacked)]
        + [anywhere()] * len(after),
        out_specs=[pl.BlockSpec((4 * s.jxl, LANES), lambda j: (j, 0))] * s.chan,
        out_shape=[out] * s.chan,
        scratch_shapes=[
            pltpu.VMEM((s.owners * 2 * s.lx, 2 * LANES), f32),
            pltpu.VMEM((rows, 2 * LANES), f32),
        ],
        cost_estimate=cost(1e9 / MODE_CHUNKS, *[out] * 12),
        name="first_forward",
    )(*arrived, stacked, *after)


def back_kernel(s, ins, table_ref, outs, gathered, held):
    me = lax.axis_index("chan")
    step = 2 * s.jxl
    for d, in_ref in enumerate(ins):
        at = pl.ds(pl.multiple_of((me ^ d) * step, step), step)
        for j in range(2):
            gathered[at, j * LANES:(j + 1) * LANES] = in_ref[j * step:(j + 1) * step, :]
    held[...] = square_dot(table_ref[...], gathered[...])
    per = 2 * s.lx
    for out_ref, (p, c) in zip(outs, distances(s)):
        for j in range(2):
            out_ref[j * per:(j + 1) * per, :] = held[owner_rows(s, p, c, per), j * LANES:(j + 1) * LANES]


def first_inverse(s, modes, table, mode_chunk, totals):
    square = stacked_square(table)
    pairs = s.jl // MODE_CHUNKS // 2
    offset = mode_chunk * pairs
    out = mode_shape(s)
    count = s.chan + 1

    def body(*refs):
        back_kernel(s, refs[:s.chan], refs[s.chan], refs[count + len(totals):-2], *refs[-2:])

    return pl.pallas_call(
        body,
        grid=(pairs,),
        in_specs=[pl.BlockSpec((4 * s.jxl, LANES), lambda j: (j, 0))] * s.chan
        + [whole(square)]
        + [anywhere()] * len(totals),
        out_specs=[pl.BlockSpec((4 * s.lx, LANES), lambda j: (j + offset, 0))] * s.owners,
        out_shape=[out] * s.owners,
        scratch_shapes=[
            pltpu.VMEM((s.chan * 2 * s.jxl, 2 * LANES), f32),
            pltpu.VMEM((s.owners * 2 * s.lx, 2 * LANES), f32),
        ],
        input_output_aliases={count + i: i for i in range(len(totals))},
        cost_estimate=cost(1e9 / MODE_CHUNKS, *modes, *modes, *modes),
        name="first_inverse",
    )(*modes, square, *totals)


def swap_groups(pieces, width):
    count = len(pieces)
    lane = lax.broadcasted_iota(jnp.int32, pieces[0].shape, 1)
    step = count // 2
    pieces = list(pieces)
    while step:
        upper = (lane // (width * step)) % 2 == 1
        for a in range(count):
            if a & step:
                continue
            low, high = pieces[a], pieces[a + step]
            pieces[a] = jnp.where(upper, pltpu.roll(high, width * step, 1), low)
            pieces[a + step] = jnp.where(upper, high, pltpu.roll(low, LANES - width * step, 1))
        step //= 2
    return pieces


def spread_modes(s, count, ins, out_ref, factor=None):
    stride = 2 * s.jxl
    me = lax.axis_index("chan")
    for d, in_ref in enumerate(ins):
        for part in range(2):
            for a in range(s.jxl // s.gw):
                pieces = [
                    in_ref[pl.ds(part * s.jxl + a * s.gw + b, count, stride=stride), :]
                    for b in range(s.gw)
                ]
                for c, piece in enumerate(swap_groups(pieces, s.modes)):
                    if factor is not None:
                        piece = piece * factor
                    out_ref[part, (me ^ d) * s.gw + c, :, a * LANES:(a + 1) * LANES] = piece


def depth_factor(s, shape):
    lane = lax.broadcasted_iota(jnp.int32, shape, 1)
    return jnp.where(lane % s.modes == 0, s.scale, 2.0 * s.scale).astype(f32)


def store_block(s, count, block, outs, held):
    stride = 2 * s.jxl
    for part in range(2):
        for a in range(s.flat // LANES):
            for b, piece in enumerate(swap_groups([block[part][c][a] for c in range(s.gw)], s.modes)):
                held[pl.ds(part * s.jxl + a * s.gw + b, count, stride=stride), :] = piece
    for d, out_ref in enumerate(outs):

        @pl.when(pl.program_id(0) == d)
        def _(out_ref=out_ref):
            out_ref[...] = held[...]


def mix_kernel(s, count, adjoint, *refs):
    ins, weight_ref, outs = refs[1:1 + s.chan], refs[1 + s.chan], refs[2 + s.chan:2 + 2 * s.chan]
    kept_ref, held = refs[-2:]
    factor = depth_factor(s, (count, LANES))

    @pl.when(pl.program_id(0) == 0)
    def _():
        spread_modes(s, count, ins, kept_ref, factor if adjoint else None)

    pieces = s.flat // LANES
    block = [[[None] * pieces for _ in range(s.gw)] for _ in range(2)]
    for a in range(pieces):
        at = slice(a * LANES, (a + 1) * LANES)
        reals = [None] * s.gw
        imags = [None] * s.gw
        for i in range(s.ch):
            real = kept_ref[0, i, :, at]
            imag = kept_ref[1, i, :, at]
            for o in range(s.gw):
                pick = (o, i) if adjoint else (i, o)
                w_real = weight_ref[(0,) + pick + (slice(None), at)]
                w_imag = weight_ref[(1,) + pick + (slice(None), at)]
                if adjoint:
                    new_real = real * w_real + imag * w_imag
                    new_imag = imag * w_real - real * w_imag
                else:
                    new_real = real * w_real - imag * w_imag
                    new_imag = real * w_imag + imag * w_real
                reals[o] = new_real if i == 0 else reals[o] + new_real
                imags[o] = new_imag if i == 0 else imags[o] + new_imag
        for o in range(s.gw):
            block[0][o][a] = reals[o] if adjoint else reals[o] * factor
            block[1][o][a] = imags[o] if adjoint else imags[o] * factor
    store_block(s, count, block, outs, held)


def mix(s, modes, spec_weight, mode_chunk, adjoint):
    count = s.jl // MODE_CHUNKS
    kept_shape = jax.ShapeDtypeStruct((2, s.ch, count, s.flat), f32)
    me = chan_index()
    if adjoint:
        weights = pl.BlockSpec((2, s.gw, s.ch, count, s.flat), lambda d, me: (0, d ^ me[0], 0, mode_chunk, 0))
    else:
        weights = pl.BlockSpec((2, s.ch, s.gw, count, s.flat), lambda d, me: (0, 0, d ^ me[0], mode_chunk, 0))
    out = jax.ShapeDtypeStruct(modes[0].shape, f32)
    results = pl.pallas_call(
        functools.partial(mix_kernel, s, count, adjoint),
        grid_spec=pltpu.PrefetchScalarGridSpec(
            num_scalar_prefetch=1,
            grid=(s.chan,),
            in_specs=[whole(v) for v in modes] + [weights],
            out_specs=[whole(out)] * s.chan + [whole(kept_shape)],
            scratch_shapes=[pltpu.VMEM(out.shape, f32)],
        ),
        out_shape=[out] * s.chan + [kept_shape],
        cost_estimate=cost(1e8, *modes, *modes, *[kept_shape] * 8),
        name="unmix" if adjoint else "mix",
    )(me, *modes, spec_weight)
    return results[:s.chan], results[s.chan]


def weight_kernel(s, width, spec_ref, grad_ref, out_ref):
    for i in range(width):
        for a in range(s.flat // LANES):
            at = slice(a * LANES, (a + 1) * LANES)
            real = spec_ref[0, i, :, at]
            imag = spec_ref[1, i, :, at]
            for o in range(s.ch):
                g_real = grad_ref[0, o, :, at]
                g_imag = grad_ref[1, o, :, at]
                out_ref[0, i, o, :, at] = real * g_real + imag * g_imag
                out_ref[1, i, o, :, at] = real * g_imag - imag * g_real


def weight_grads(s, spec, grad, mode_chunk, total):
    count = s.jl // MODE_CHUNKS
    width = 2
    aliased = [] if total is None else [total]

    def body(spec_ref, grad_ref, *refs):
        weight_kernel(s, width, spec_ref, grad_ref, refs[-1])

    shape = jax.ShapeDtypeStruct((2, s.ch, s.ch, s.jl, s.flat), f32)
    return pl.pallas_call(
        body,
        grid=(s.ch // width,),
        in_specs=[pl.BlockSpec((2, width, count, s.flat), lambda i: (0, i, 0, 0)), whole(grad)]
        + [pl.BlockSpec(memory_space=pl.ANY)] * len(aliased),
        out_specs=pl.BlockSpec((2, width, s.ch, count, s.flat), lambda i: (0, i, 0, mode_chunk, 0)),
        out_shape=shape,
        input_output_aliases={2 + i: i for i in range(len(aliased))},
        cost_estimate=cost(1e8, shape),
        name="weight_grads",
    )(spec, grad, *aliased)


def over_owners(s, p, c, value):
    if p == 0 and c == 0:
        return value
    pairs = [(i, i ^ (p * s.chan + c)) for i in range(s.owners)]
    return lax.ppermute(value, ("planes", "chan"), pairs)


def over_chan(s, values):
    moved = [values[0]]
    for d in range(1, s.chan):
        moved.append(lax.ppermute(values[d], "chan", [(i, i ^ d) for i in range(s.chan)]))
    return moved


def mode_side(s, sent, tables, spec_weight, adjoint, after):
    mode_chunks = range(MODE_CHUNKS)
    arrived = [over_owners(s, p, c, sent[c][p]) for p, c in distances(s)]
    owned = []
    for m in mode_chunks:
        sent_on = first_pass(s, arrived, tables[0], m, after)
        after = sent_on[:1]
        owned.append(over_chan(s, sent_on))
    mixed = [mix(s, owned[m], spec_weight, m, adjoint) for m in mode_chunks]
    returned = [over_chan(s, v[0]) for v in mixed]
    totals = ()
    for m in mode_chunks:
        totals = first_inverse(s, returned[m], tables[1], m, totals)
    back = {d: over_owners(s, *d, value) for d, value in zip(distances(s), totals)}
    return back, [v[1] for v in mixed]


def fast_local(s, field, cotangent, spec_weight, point_weight, bias):
    second = second_tables(s)
    third = third_tables(s)
    first = first_tables(s)
    halves = [range(k, k + s.chan // 2) for k in (0, s.chan // 2)]
    sent = analysis(s, field, second, third)
    point = pointwise(field, point_weight, bias)
    back, spec_kept = mode_side(s, sent, first, spec_weight, False, (point,))
    totals, sent = (), []
    for half in halves:
        modes = [back[p, c] for c in half for p in range(s.planes)]
        totals, parts = middle(s, modes, point, cotangent, half[0], second, third, totals)
        sent += parts
    output, grad = totals
    local_grad = pointwise(grad, point_weight.T, jnp.zeros_like(bias))
    back, grad_kept = mode_side(s, sent, first, spec_weight, True, (local_grad,))
    weight_grad = None
    for m in range(MODE_CHUNKS):
        weight_grad = weight_grads(
            s, spec_kept[m], grad_kept[m], m, weight_grad
        )
    totals = ()
    for half in halves:
        modes = [back[p, c] for c in half for p in range(s.planes)]
        totals = final(s, modes, local_grad, half[0], second, third, totals)
    return output, totals[0], weight_grad


def local(field, cotangent, spec_weight, point_weight, bias):
    s = Sizes(field, spec_weight)
    if s.fits():
        return fast_local(s, field, cotangent, spec_weight, point_weight, bias)
    return plain_local(s, field, cotangent, spec_weight, point_weight, bias)


def solution(mesh):
    in_specs = (
        P("groups", None, ("planes", "chan"), None, None),
        P("groups", None, ("planes", "chan"), None, None),
        P(None, None, None, "planes", "chan"),
        P(),
        P(),
    )
    out_specs = (
        P("groups", None, ("planes", "chan"), None, None),
        P("groups", None, ("planes", "chan"), None, None),
        P("groups", None, None, "planes", "chan"),
    )
    return jax.shard_map(local, mesh=mesh, in_specs=in_specs, out_specs=out_specs, check_vma=False)
```

time: 744 us -> 410 us (0.55)
  the two profiles are of different devices: /device:TPU:0 before, /device:TPU:13 now
where the time goes in v2:
time: 410 us; the launch traced here: 407 us
  Pallas kernels  158 us (39%)
  starting transfers between devices  133 us (32%)
  waiting for transfers between devices  96.1 us (23%)
  local copies, waits for them, and re-layouts  15.2 us (4%)
    ppermute x60, starting transfers between devices, over_owners(): return lax.ppermute(value, ('planes', 'chan'), pairs)  107 us
    ppermute x60, waiting for transfers between devices, over_owners(): return lax.ppermute(value, ('planes', 'chan'), pairs)  60.8 us
    pallas_call x5, Pallas kernels, group_call(): pl.pallas_call(body, grid_spec=pltpu.PrefetchScalarGridSpec(num_scalar_pr...  58.5 us
    ppermute x24, waiting for transfers between devices, over_chan(): lax.ppermute(values[d], 'chan', [(i, i ^ d) for i in range(s.chan)])  35.3 us
    pallas_call x4, Pallas kernels, mix(): pl.pallas_call(functools.partial(mix_kernel, s, count, adjoint), grid_spe...  32.8 us
    ppermute x24, starting transfers between devices, over_chan(): lax.ppermute(values[d], 'chan', [(i, i ^ d) for i in range(s.chan)])  26.7 us
    pallas_call x2, Pallas kernels, pointwise(): pl.pallas_call(pointwise_kernel, grid=(lx,), in_specs=[spec, whole(mixing...  21.5 us
    pallas_call x4, Pallas kernels, first_inverse(): pl.pallas_call(body, grid=(pairs,), in_specs=[pl.BlockSpec((4 * s.jxl, LA...  15.7 us
  transfers between devices with their start and end apart: 84, of which 27 were waited for; matrix products, arithmetic and copies ran while one was open for 2% of the time, Pallas kernels for 26%

profile of v2, /device:TPU:13, one launch (start us, length us, event | category | flops | bytes accessed | tf_op | source)
XLA Modules:
  0.0 406.7 jit_solution(3842362896067657289)
XLA Ops:
  0.7 12.2 %shard_map.184 = (f32[256,128]{1,0:T(8,128)}, f32[256,128]{1,0:T(8,128)}, f32[256,128]{1,0:T(8,128)}, f32[256,128]{1,0:T(8,128)}, f32[256,128]{1,0:T(8,128)}, /*...) custom-call(s32[1]{0:T(128)} %bitcast.me_ref.refs_0_, ...), custom_call_target="tpu_custom_call" | custom-call | flops 6000000000 | bytes 10485760 | tf_op jit(solution)/shard_map/pallas_call | solution.py:458
  36.2 6.1 %collective-permute-done.6.refs_7_ = f32[256,128]{1,0:T(8,128)S(1)} collective-permute-done((f32[256,128]{1,0:T(8,128)}, f32[256,128]{1,0:T(8,128)S(1)}, u32[]{:S(2)}, u32[]{:S(2)}) %collective-permute-start.6) | collective-permute-done | bytes 131104 | tf_op jit(solution)/shard_map/ppermute | solution.py:827
  49.9 10.7 %pointwise.2.refs_17_.refs_8_ = f32[1,16,8,128,128]{4,3,2,1,0:T(8,128)} custom-call(f32[1,16,8,128,128]{4,3,2,1,0:T(8,128)} %values_ref.1, bf16[512,256]{1,0:T(8,128)(2,1)} %pad_maximum_fusion.mixing_ref, f32[256,128]{1,0:T(8,128)} %broadcast_in_dim.21.bias_ref), custom_call_target="tpu_custom_call" | custom-call | flops 6000000000 | bytes 16777216 | tf_op jit(solution)/shard_map/pointwise/pallas_call | solution.py:569
  80.3 10.8 %collective-permute-done.23.refs_4_ = f32[256,128]{1,0:T(8,128)S(1)} collective-permute-done((f32[256,128]{1,0:T(8,128)}, f32[256,128]{1,0:T(8,128)S(1)}, u32[]{:S(2)}, u32[]{:S(2)}) %collective-permute-start.23) | collective-permute-done | bytes 131104 | tf_op jit(solution)/shard_map/ppermute | solution.py:833
  91.7 8.2 %mix.3 = (f32[256,128]{1,0:T(8,128)}, f32[256,128]{1,0:T(8,128)}, f32[256,128]{1,0:T(8,128)}, f32[256,128]{1,0:T(8,128)}, f32[2,16,8,512]{3,2,1,0:T(8,128)}) custom-call(s32[1]{0:T(128)} %bitcast.me_ref.refs_0_, f32[256,128]{1,0:T(8,128)} %get-tuple-element.155.refs_17_.refs_1_, f32[256,128]{1,0:T(8,128)} %copy-done.47, f32[256,128]{1,0:T(8,128)} %copy-done.53, ...), custom_call_target="tpu_custom_call" | custom-call | flops 100000000 | bytes 5242880 | tf_op jit(solution)/shard_map/mix/pallas_call | solution.py:772
  103.3 8.2 %mix.2 = (f32[256,128]{1,0:T(8,128)}, f32[256,128]{1,0:T(8,128)}, f32[256,128]{1,0:T(8,128)}, f32[256,128]{1,0:T(8,128)}, f32[2,16,8,512]{3,2,1,0:T(8,128)}) custom-call(s32[1]{0:T(128)} %bitcast.me_ref.refs_0_, f32[256,128]{1,0:T(8,128)} %get-tuple-element.156.refs_1_, f32[256,128]{1,0:T(8,128)} %copy-done.44, f32[256,128]{1,0:T(8,128)} %copy-done.50, ...), custom_call_target="tpu_custom_call" | custom-call | flops 100000000 | bytes 5242880 | tf_op jit(solution)/shard_map/mix/pallas_call | solution.py:772
  119.4 6.4 %collective-permute-done.20.refs_3_ = f32[256,128]{1,0:T(8,128)S(1)} collective-permute-done((f32[256,128]{1,0:T(8,128)}, f32[256,128]{1,0:T(8,128)S(1)}, u32[]{:S(2)}, u32[]{:S(2)}) %collective-permute-start.20) | collective-permute-done | bytes 131104 | tf_op jit(solution)/shard_map/ppermute | solution.py:833
  134.6 6.2 %collective-permute-done.27.refs_0_ = f32[256,128]{1,0:T(8,128)S(1)} collective-permute-done((f32[256,128]{1,0:T(8,128)}, f32[256,128]{1,0:T(8,128)S(1)}, u32[]{:S(2)}, u32[]{:S(2)}) %collective-permute-start.27) | collective-permute-done | bytes 131104 | tf_op jit(solution)/shard_map/ppermute | solution.py:827
  163.9 15.8 %shard_map.185 = (f32[1,16,8,128,128]{4,3,2,1,0:T(8,128)}, f32[1,16,8,128,128]{4,3,2,1,0:T(8,128)}, f32[256,128]{1,0:T(8,128)}, f32[256,128]{1,0:T(8,128)}, f32[...) custom-call(s32[1]{0:T(128)} %bitcast.me_ref.refs_0_, ...), custom_call_target="tpu_custom_call" | custom-call | flops 6000000000 | bytes 18874368 | tf_op jit(solution)/shard_map/pallas_call | solution.py:458
  185.5 15.8 %shard_map.186 = (f32[1,16,8,128,128]{4,3,2,1,0:T(8,128)}, f32[1,16,8,128,128]{4,3,2,1,0:T(8,128)}, f32[256,128]{1,0:T(8,128)}, f32[256,128]{1,0:T(8,128)}, f32[...) custom-call(s32[1]{0:T(128)} %bitcast.me_ref.refs_0_, ...), custom_call_target="tpu_custom_call", output_to_operand_aliasing={{0}: (15, {}), {1}: (16, {})} | custom-call | flops 6000000000 | bytes 18874368 | tf_op jit(solution)/shard_map/pallas_call | solution.py:458
  202.4 7.5 %collective-permute-start.47 = (f32[256,128]{1,0:T(8,128)}, f32[256,128]{1,0:T(8,128)S(1)}, u32[]{:S(2)}, u32[]{:S(2)}) collective-permute-start(f32[256,128]{1,0:T(8,128)} %get-tuple-element.212), channel_id=1, source_target_pairs={{0,6},{1,7},{2,4},{3,5},{4,2},{5,3},{6,0},{7,1},{8,14},{9,15},{10,... | collective-permute-start | bytes 393224 | tf_op jit(solution)/shard_map/ppermute | solution.py:827
  216.8 11.0 %collective-permute-start.52 = (f32[256,128]{1,0:T(8,128)}, f32[256,128]{1,0:T(8,128)S(1)}, u32[]{:S(2)}, u32[]{:S(2)}) collective-permute-start(f32[256,128]{1,0:T(8,128)} %get-tuple-element.217), channel_id=1, source_target_pairs={{0,11},{1,10},{2,9},{3,8},{4,15},{5,14},{6,13},{7,12},{8,3},{9,2},... | collective-permute-start | bytes 393224 | tf_op jit(solution)/shard_map/ppermute | solution.py:827
  233.1 9.7 %collective-permute-start.45 = (f32[256,128]{1,0:T(8,128)}, f32[256,128]{1,0:T(8,128)S(1)}, u32[]{:S(2)}, u32[]{:S(2)}) collective-permute-start(f32[256,128]{1,0:T(8,128)} %get-tuple-element.210), channel_id=1, source_target_pairs={{0,4},{1,5},{2,6},{3,7},{4,0},{5,1},{6,2},{7,3},{8,12},{9,13},{10,... | collective-permute-start | bytes 393224 | tf_op jit(solution)/shard_map/ppermute | solution.py:827
  255.5 10.8 %pointwise.3.refs_17_.refs_8_ = f32[1,16,8,128,128]{4,3,2,1,0:T(8,128)} custom-call(f32[1,16,8,128,128]{4,3,2,1,0:T(8,128)} %get-tuple-element.222.values_ref, bf16[512,256]{1,0:T(8,128)(2,1)} %pad_maximum_fusion.1.mixing_ref, f32[256,128]{1,0:T(8,128)} %broadcast_in_dim.22.bias_ref), custom_call_target="tpu_custom_call" | custom-call | flops 6000000000 | bytes 16777216 | tf_op jit(solution)/shard_map/pointwise/pallas_call | solution.py:569
  280.4 10.7 %collective-permute-done.65.refs_4_ = f32[256,128]{1,0:T(8,128)S(1)} collective-permute-done((f32[256,128]{1,0:T(8,128)}, f32[256,128]{1,0:T(8,128)S(1)}, u32[]{:S(2)}, u32[]{:S(2)}) %collective-permute-start.65) | collective-permute-done | bytes 131104 | tf_op jit(solution)/shard_map/ppermute | solution.py:833
  291.8 8.2 %unmix.3 = (f32[256,128]{1,0:T(8,128)}, f32[256,128]{1,0:T(8,128)}, f32[256,128]{1,0:T(8,128)}, f32[256,128]{1,0:T(8,128)}, f32[2,16,8,512]{3,2,1,0:T(8,128)}) custom-call(s32[1]{0:T(128)} %bitcast.me_ref.refs_0_, f32[256,128]{1,0:T(8,128)} %get-tuple-element.223.refs_17_.refs_1_, f32[256,128]{1,0:T(8,128)} %copy-done.45, f32[256,128]{1,0:T(8,128)} %copy-done.51, ...), custom_call_target="tpu_custom_call" | custom-call | flops 100000000 | bytes 5242880 | tf_op jit(solution)/shard_map/unmix/pallas_call | solution.py:772
  303.4 8.2 %unmix.2 = (f32[256,128]{1,0:T(8,128)}, f32[256,128]{1,0:T(8,128)}, f32[256,128]{1,0:T(8,128)}, f32[256,128]{1,0:T(8,128)}, f32[2,16,8,512]{3,2,1,0:T(8,128)}) custom-call(s32[1]{0:T(128)} %bitcast.me_ref.refs_0_, f32[256,128]{1,0:T(8,128)} %get-tuple-element.224.refs_1_, f32[256,128]{1,0:T(8,128)} %copy-done.46, f32[256,128]{1,0:T(8,128)} %copy-done.52, ...), custom_call_target="tpu_custom_call" | custom-call | flops 100000000 | bytes 5242880 | tf_op jit(solution)/shard_map/unmix/pallas_call | solution.py:772
  319.0 6.6 %collective-permute-done.62.refs_3_ = f32[256,128]{1,0:T(8,128)S(1)} collective-permute-done((f32[256,128]{1,0:T(8,128)}, f32[256,128]{1,0:T(8,128)S(1)}, u32[]{:S(2)}, u32[]{:S(2)}) %collective-permute-start.62) | collective-permute-done | bytes 131104 | tf_op jit(solution)/shard_map/ppermute | solution.py:833
  352.3 6.6 %weight_grads.2.refs_0_ = f32[2,16,16,16,512]{4,3,2,1,0:T(8,128)} custom-call(f32[2,16,8,512]{3,2,1,0:T(8,128)} %get-tuple-element.273.spec_ref, f32[2,16,8,512]{3,2,1,0:T(8,128)} %get-tuple-element.274.grad_ref), custom_call_target="tpu_custom_call" | custom-call | flops 100000000 | bytes 16777216 | tf_op jit(solution)/shard_map/weight_grads/pallas_call | solution.py:810
  359.0 6.8 %weight_grads.3 = f32[2,16,16,16,512]{4,3,2,1,0:T(8,128)} custom-call(f32[2,16,8,512]{3,2,1,0:T(8,128)} %get-tuple-element.271.spec_ref, f32[2,16,8,512]{3,2,1,0:T(8,128)} %get-tuple-element.272.grad_ref, f32[2,16,16,16,512]{4,3,2,1,0:T(8,128)} %weight_grads.2.refs_0_), custom_call_target="tpu_custom_call", output_to_operand_aliasing={{}: (2, {})} | custom-call | flops 100000000 | bytes 16777216 | tf_op jit(solution)/shard_map/weight_grads/pallas_call | solution.py:810
  373.2 7.3 %shard_map.187.refs_11_ = f32[1,16,8,128,128]{4,3,2,1,0:T(8,128)} custom-call(s32[1]{0:T(128)} %bitcast.me_ref.refs_0_, f32[256,128]{1,0:T(8,128)} %get-tuple-element.263.refs_0_, f32[256,128]{1,0:T(8,128)} %copy-done.32, f32[256,128]{1,0:T(8,128)} %copy-done.33, f32[256,128]{1,0:T(8,128)} %copy-done.35, f32[256,128]{1,0:T(8,128)} %copy-done.37, ...), custom_call_target="tpu_custom_call" | custom-call | flops 3000000000 | bytes 9437184 | tf_op jit(solution)/shard_map/pallas_call | solution.py:458
  380.5 6.1 %collective-permute-done.73.refs_4_ = f32[256,128]{1,0:T(8,128)S(1)} collective-permute-done((f32[256,128]{1,0:T(8,128)S(1)}, f32[256,128]{1,0:T(8,128)S(1)}, u32[]{:S(2)}, u32[]{:S(2)}) %collective-permute-start.73) | collective-permute-done | bytes 131104 | tf_op jit(solution)/shard_map/ppermute | solution.py:827
  386.6 7.2 %collective-permute-done.74.refs_5_ = f32[256,128]{1,0:T(8,128)S(1)} collective-permute-done((f32[256,128]{1,0:T(8,128)S(1)}, f32[256,128]{1,0:T(8,128)S(1)}, u32[]{:S(2)}, u32[]{:S(2)}) %collective-permute-start.74) | collective-permute-done | bytes 131104 | tf_op jit(solution)/shard_map/ppermute | solution.py:827
  399.4 7.3 %shard_map.188 = f32[1,16,8,128,128]{4,3,2,1,0:T(8,128)} custom-call(s32[1]{0:T(128)} %bitcast.me_ref.refs_0_, f32[256,128]{1,0:T(8,128)} %copy-done.29, f32[256,128]{1,0:T(8,128)} %copy-done.30, f32[256,128]{1,0:T(8,128)} %copy-done.31, f32[256,128]{1,0:T(8,128)} %copy-done.40, f32[256,128]{1,0:T(8,128)} %copy-done.43, ...), custom_call_target="tpu_custom_call", output_to_operand_aliasing={{}: (12, {})} | custom-call | flops 3000000000 | bytes 9437184 | tf_op jit(solution)/shard_map/pallas_call | solution.py:458
  (360 shorter events, 190.8 us)
Async XLA Ops:
  36.2 24.4 %collective-permute-start.10 = (f32[256,128]{1,0:T(8,128)}, f32[256,128]{1,0:T(8,128)S(1)}, u32[]{:S(2)}, u32[]{:S(2)}) collective-permute-start(f32[256,128]{1,0:T(8,128)} %get-tuple-element.150), channel_id=1, source_target_pairs={{0,11},{1,10},{2,9},{3,8},{4,15},{5,14},{6,13},{7,12},{8,3},{9,2},... | collective-permute-start | bytes 393224 | tf_op jit(solution)/shard_map/ppermute | solution.py:827
  76.6 23.9 %collective-permute-start.15 = (f32[256,128]{1,0:T(8,128)}, f32[256,128]{1,0:T(8,128)S(1)}, u32[]{:S(2)}, u32[]{:S(2)}) collective-permute-start(f32[256,128]{1,0:T(8,128)} %get-tuple-element.157), channel_id=1, source_target_pairs={{0,1},{1,0},{2,3},{3,2},{4,5},{5,4},{6,7},{7,6},{8,9},{9,8},{10,11... | collective-permute-start | bytes 393224 | tf_op jit(solution)/shard_map/ppermute | solution.py:833
  79.0 23.6 %collective-permute-start.16 = (f32[256,128]{1,0:T(8,128)}, f32[256,128]{1,0:T(8,128)S(1)}, u32[]{:S(2)}, u32[]{:S(2)}) collective-permute-start(f32[256,128]{1,0:T(8,128)} %get-tuple-element.158), channel_id=1, source_target_pairs={{0,2},{1,3},{2,0},{3,1},{4,6},{5,7},{6,4},{7,5},{8,10},{9,11},{10,... | collective-permute-start | bytes 393224 | tf_op jit(solution)/shard_map/ppermute | solution.py:833
  79.0 23.6 %collective-permute-start.17 = (f32[256,128]{1,0:T(8,128)}, f32[256,128]{1,0:T(8,128)S(1)}, u32[]{:S(2)}, u32[]{:S(2)}) collective-permute-start(f32[256,128]{1,0:T(8,128)} %get-tuple-element.159), channel_id=1, source_target_pairs={{0,3},{1,2},{2,1},{3,0},{4,7},{5,6},{6,5},{7,4},{8,11},{9,10},{10,... | collective-permute-start | bytes 393224 | tf_op jit(solution)/shard_map/ppermute | solution.py:833
  151.9 27.9 %collective-permute-start.30 = (f32[256,128]{1,0:T(8,128)}, f32[256,128]{1,0:T(8,128)S(1)}, u32[]{:S(2)}, u32[]{:S(2)}) collective-permute-start(f32[256,128]{1,0:T(8,128)} %get-tuple-element.190), channel_id=1, source_target_pairs={{0,14},{1,15},{2,12},{3,13},{4,10},{5,11},{6,8},{7,9},{8,6},{9,7},... | collective-permute-start | bytes 393224 | tf_op jit(solution)/shard_map/ppermute | solution.py:827
  154.3 25.5 %collective-permute-start.31 = (f32[256,128]{1,0:T(8,128)}, f32[256,128]{1,0:T(8,128)S(1)}, u32[]{:S(2)}, u32[]{:S(2)}) collective-permute-start(f32[256,128]{1,0:T(8,128)} %get-tuple-element.191), channel_id=1, source_target_pairs={{0,3},{1,2},{2,1},{3,0},{4,7},{5,6},{6,5},{7,4},{8,11},{9,10},{10,... | collective-permute-start | bytes 393224 | tf_op jit(solution)/shard_map/ppermute | solution.py:827
  156.2 23.7 %collective-permute-start.32 = (f32[256,128]{1,0:T(8,128)}, f32[256,128]{1,0:T(8,128)S(1)}, u32[]{:S(2)}, u32[]{:S(2)}) collective-permute-start(f32[256,128]{1,0:T(8,128)} %get-tuple-element.192), channel_id=1, source_target_pairs={{0,7},{1,6},{2,5},{3,4},{4,3},{5,2},{6,1},{7,0},{8,15},{9,14},{10,... | collective-permute-start | bytes 393224 | tf_op jit(solution)/shard_map/ppermute | solution.py:827
  161.0 21.0 %collective-permute-start.33 = (f32[256,128]{1,0:T(8,128)}, f32[256,128]{1,0:T(8,128)S(1)}, u32[]{:S(2)}, u32[]{:S(2)}) collective-permute-start(f32[256,128]{1,0:T(8,128)} %get-tuple-element.193), channel_id=1, source_target_pairs={{0,11},{1,10},{2,9},{3,8},{4,15},{5,14},{6,13},{7,12},{8,3},{9,2},... | collective-permute-start | bytes 393224 | tf_op jit(solution)/shard_map/ppermute | solution.py:827
  163.1 21.7 %collective-permute-start.34 = (f32[256,128]{1,0:T(8,128)}, f32[256,128]{1,0:T(8,128)S(1)}, u32[]{:S(2)}, u32[]{:S(2)}) collective-permute-start(f32[256,128]{1,0:T(8,128)} %get-tuple-element.194), channel_id=1, source_target_pairs={{0,15},{1,14},{2,13},{3,12},{4,11},{5,10},{6,9},{7,8},{8,7},{9,6},... | collective-permute-start | bytes 393224 | tf_op jit(solution)/shard_map/ppermute | solution.py:827
  201.3 26.5 %collective-permute-start.44 = (f32[256,128]{1,0:T(8,128)}, f32[256,128]{1,0:T(8,128)S(1)}, u32[]{:S(2)}, u32[]{:S(2)}) collective-permute-start(f32[256,128]{1,0:T(8,128)} %get-tuple-element.209), channel_id=1, source_target_pairs={{0,3},{1,2},{2,1},{3,0},{4,7},{5,6},{6,5},{7,4},{8,11},{9,10},{10,... | collective-permute-start | bytes 393224 | tf_op jit(solution)/shard_map/ppermute | solution.py:827
  202.4 25.4 %collective-permute-start.47 = (f32[256,128]{1,0:T(8,128)}, f32[256,128]{1,0:T(8,128)S(1)}, u32[]{:S(2)}, u32[]{:S(2)}) collective-permute-start(f32[256,128]{1,0:T(8,128)} %get-tuple-element.212), channel_id=1, source_target_pairs={{0,6},{1,7},{2,4},{3,5},{4,2},{5,3},{6,0},{7,1},{8,14},{9,15},{10,... | collective-permute-start | bytes 393224 | tf_op jit(solution)/shard_map/ppermute | solution.py:827
  209.9 22.4 %collective-permute-start.48 = (f32[256,128]{1,0:T(8,128)}, f32[256,128]{1,0:T(8,128)S(1)}, u32[]{:S(2)}, u32[]{:S(2)}) collective-permute-start(f32[256,128]{1,0:T(8,128)} %get-tuple-element.213), channel_id=1, source_target_pairs={{0,7},{1,6},{2,5},{3,4},{4,3},{5,2},{6,1},{7,0},{8,15},{9,14},{10,... | collective-permute-start | bytes 393224 | tf_op jit(solution)/shard_map/ppermute | solution.py:827
  211.0 22.1 %collective-permute-start.51 = (f32[256,128]{1,0:T(8,128)}, f32[256,128]{1,0:T(8,128)S(1)}, u32[]{:S(2)}, u32[]{:S(2)}) collective-permute-start(f32[256,128]{1,0:T(8,128)} %get-tuple-element.216), channel_id=1, source_target_pairs={{0,10},{1,11},{2,8},{3,9},{4,14},{5,15},{6,12},{7,13},{8,2},{9,3},... | collective-permute-start | bytes 393224 | tf_op jit(solution)/shard_map/ppermute | solution.py:827
  216.8 31.0 %collective-permute-start.52 = (f32[256,128]{1,0:T(8,128)}, f32[256,128]{1,0:T(8,128)S(1)}, u32[]{:S(2)}, u32[]{:S(2)}) collective-permute-start(f32[256,128]{1,0:T(8,128)} %get-tuple-element.217), channel_id=1, source_target_pairs={{0,11},{1,10},{2,9},{3,8},{4,15},{5,14},{6,13},{7,12},{8,3},{9,2},... | collective-permute-start | bytes 393224 | tf_op jit(solution)/shard_map/ppermute | solution.py:827
  227.8 21.4 %collective-permute-start.56 = (f32[256,128]{1,0:T(8,128)}, f32[256,128]{1,0:T(8,128)S(1)}, u32[]{:S(2)}, u32[]{:S(2)}) collective-permute-start(f32[256,128]{1,0:T(8,128)} %get-tuple-element.221), channel_id=1, source_target_pairs={{0,15},{1,14},{2,13},{3,12},{4,11},{5,10},{6,9},{7,8},{8,7},{9,6},... | collective-permute-start | bytes 393224 | tf_op jit(solution)/shard_map/ppermute | solution.py:827
  277.7 22.7 %collective-permute-start.57 = (f32[256,128]{1,0:T(8,128)}, f32[256,128]{1,0:T(8,128)S(1)}, u32[]{:S(2)}, u32[]{:S(2)}) collective-permute-start(f32[256,128]{1,0:T(8,128)} %get-tuple-element.225), channel_id=1, source_target_pairs={{0,1},{1,0},{2,3},{3,2},{4,5},{5,4},{6,7},{7,6},{8,9},{9,8},{10,11... | collective-permute-start | bytes 393224 | tf_op jit(solution)/shard_map/ppermute | solution.py:833
  278.9 23.7 %collective-permute-start.58 = (f32[256,128]{1,0:T(8,128)}, f32[256,128]{1,0:T(8,128)S(1)}, u32[]{:S(2)}, u32[]{:S(2)}) collective-permute-start(f32[256,128]{1,0:T(8,128)} %get-tuple-element.226), channel_id=1, source_target_pairs={{0,2},{1,3},{2,0},{3,1},{4,6},{5,7},{6,4},{7,5},{8,10},{9,11},{10,... | collective-permute-start | bytes 393224 | tf_op jit(solution)/shard_map/ppermute | solution.py:833
  279.0 23.7 %collective-permute-start.59 = (f32[256,128]{1,0:T(8,128)}, f32[256,128]{1,0:T(8,128)S(1)}, u32[]{:S(2)}, u32[]{:S(2)}) collective-permute-start(f32[256,128]{1,0:T(8,128)} %get-tuple-element.227), channel_id=1, source_target_pairs={{0,3},{1,2},{2,1},{3,0},{4,7},{5,6},{6,5},{7,4},{8,11},{9,10},{10,... | collective-permute-start | bytes 393224 | tf_op jit(solution)/shard_map/ppermute | solution.py:833
  341.8 24.0 %collective-permute-start.79 = (f32[256,128]{1,0:T(8,128)}, f32[256,128]{1,0:T(8,128)S(1)}, u32[]{:S(2)}, u32[]{:S(2)}) collective-permute-start(f32[256,128]{1,0:T(8,128)} %get-tuple-element.266), channel_id=1, source_target_pairs={{0,12},{1,13},{2,14},{3,15},{4,8},{5,9},{6,10},{7,11},{8,4},{9,5},... | collective-permute-start | bytes 393224 | tf_op jit(solution)/shard_map/ppermute | solution.py:827
  344.8 23.0 %collective-permute-start.80 = (f32[256,128]{1,0:T(8,128)}, f32[256,128]{1,0:T(8,128)S(1)}, u32[]{:S(2)}, u32[]{:S(2)}) collective-permute-start(f32[256,128]{1,0:T(8,128)} %get-tuple-element.267), channel_id=1, source_target_pairs={{0,1},{1,0},{2,3},{3,2},{4,5},{5,4},{6,7},{7,6},{8,9},{9,8},{10,11... | collective-permute-start | bytes 393224 | tf_op jit(solution)/shard_map/ppermute | solution.py:827
  349.6 21.2 %collective-permute-start.82 = (f32[256,128]{1,0:T(8,128)}, f32[256,128]{1,0:T(8,128)S(1)}, u32[]{:S(2)}, u32[]{:S(2)}) collective-permute-start(f32[256,128]{1,0:T(8,128)} %get-tuple-element.269), channel_id=1, source_target_pairs={{0,9},{1,8},{2,11},{3,10},{4,13},{5,12},{6,15},{7,14},{8,1},{9,0},... | collective-permute-start | bytes 393224 | tf_op jit(solution)/shard_map/ppermute | solution.py:827
  368.2 25.7 %collective-permute-start.74 = (f32[256,128]{1,0:T(8,128)S(1)}, f32[256,128]{1,0:T(8,128)S(1)}, u32[]{:S(2)}, u32[]{:S(2)}) collective-permute-start(f32[256,128]{1,0:T(8,128)S(1)} %copy-done.68), channel_id=1, source_target_pairs={{0,7},{1,6},{2,5},{3,4},{4,3},{5,2},{6,1},{7,0},{8,15},{9,14},{10,... | collective-permute-start | bytes 393224 | tf_op jit(solution)/shard_map/ppermute | solution.py:827
  370.8 25.1 %collective-permute-start.75 = (f32[256,128]{1,0:T(8,128)S(1)}, f32[256,128]{1,0:T(8,128)S(1)}, u32[]{:S(2)}, u32[]{:S(2)}) collective-permute-start(f32[256,128]{1,0:T(8,128)S(1)} %copy-done.69), channel_id=1, source_target_pairs={{0,11},{1,10},{2,9},{3,8},{4,15},{5,14},{6,13},{7,12},{8,3},{9,2},... | collective-permute-start | bytes 393224 | tf_op jit(solution)/shard_map/ppermute | solution.py:827
  371.6 27.1 %collective-permute-start.76 = (f32[256,128]{1,0:T(8,128)S(1)}, f32[256,128]{1,0:T(8,128)S(1)}, u32[]{:S(2)}, u32[]{:S(2)}) collective-permute-start(f32[256,128]{1,0:T(8,128)S(1)} %copy-done.71), channel_id=1, source_target_pairs={{0,15},{1,14},{2,13},{3,12},{4,11},{5,10},{6,9},{7,8},{8,7},{9,6},... | collective-permute-start | bytes 393224 | tf_op jit(solution)/shard_map/ppermute | solution.py:827
  (151 other events, 2071.6 us)

commit v3 on v2

--- a/solution.py
+++ b/solution.py
@@ -430,9 +430,9 @@
     return lax.axis_index("chan").astype(jnp.int32).reshape(1)
 
 
-def grid_spec(s, start):
+def grid_spec(s, start, step=1):
     return pl.BlockSpec(
-        (1, s.gw, BLOCK, s.gy, s.gz), lambda k, x, me: (0, me[0] ^ (start + k), x, 0, 0)
+        (1, s.gw, BLOCK, s.gy, s.gz), lambda k, x, me: (0, me[0] ^ (start + step * k), x, 0, 0)
     )
 
 
@@ -470,23 +470,24 @@
     )(chan_index(), *operands)
 
 
-def analysis(s, field, second, third):
+def analysis(s, field, start, step, second, third, after):
     tables = (third[0], second[0])
     out = mode_shape(s)
     count = 1 + len(tables)
 
     def body(me_ref, *refs):
-        analysis_kernel(s, *refs[:count], by_group(s, refs[count:-2]), *refs[-2:])
+        outs = by_group(s, refs[count + len(after):-2])
+        analysis_kernel(s, *refs[:count], outs, *refs[-2:])
 
     return by_group(s, group_call(
-        s, s.chan, body,
-        [grid_spec(s, 0)] + [whole(t) for t in tables],
-        [whole(out)] * s.owners,
-        [out] * s.owners,
+        s, s.chan // 2, body,
+        [grid_spec(s, start, step)] + [whole(t) for t in tables] + [anywhere()] * len(after),
+        [whole(out)] * (s.owners // 2),
+        [out] * (s.owners // 2),
         forward_scratch(s),
         {},
-        cost(6e9, *[out] * 80),
-        (field, *tables),
+        cost(3e9, *[out] * 40),
+        (field, *tables, *after),
     ))
 
 
@@ -827,6 +828,10 @@
     return lax.ppermute(value, ("planes", "chan"), pairs)
 
 
+def turns(chan):
+    return ((0, 2), (1, 2)) if chan > 2 else ((0, 1), (1, 1))
+
+
 def over_chan(s, values):
     moved = [values[0]]
     for d in range(1, s.chan):
@@ -856,7 +861,12 @@
     third = third_tables(s)
     first = first_tables(s)
     halves = [range(k, k + s.chan // 2) for k in (0, s.chan // 2)]
-    sent = analysis(s, field, second, third)
+    sent, after = [None] * s.chan, ()
+    for start, step in turns(s.chan):
+        parts = analysis(s, field, start, step, second, third, after)
+        after = parts[0][:1]
+        for k, part in enumerate(parts):
+            sent[start + k * step] = part
     point = pointwise(field, point_weight, bias)
     back, spec_kept = mode_side(s, sent, first, spec_weight, False, (point,))
     totals, sent = (), []

time: 410 us -> 406 us (level)
  the two profiles are of different devices: /device:TPU:13 before, /device:TPU:11 now
where the time goes in v3:
time: 406 us; the launch traced here: 403 us
  Pallas kernels  159 us (39%)
  starting transfers between devices  122 us (30%)
  waiting for transfers between devices  102 us (25%)
  local copies, waits for them, and re-layouts  15.5 us (4%)
    ppermute x60, starting transfers between devices, over_owners(): return lax.ppermute(value, ('planes', 'chan'), pairs)  100 us
    ppermute x60, waiting for transfers between devices, over_owners(): return lax.ppermute(value, ('planes', 'chan'), pairs)  67.8 us
    pallas_call x6, Pallas kernels, group_call(): pl.pallas_call(body, grid_spec=pltpu.PrefetchScalarGridSpec(num_scalar_pr...  60.2 us
    ppermute x24, waiting for transfers between devices, over_chan(): lax.ppermute(values[d], 'chan', [(i, i ^ d) for i in range(s.chan)])  34.4 us
    pallas_call x4, Pallas kernels, mix(): pl.pallas_call(functools.partial(mix_kernel, s, count, adjoint), grid_spe...  32.8 us
    pallas_call x2, Pallas kernels, pointwise(): pl.pallas_call(pointwise_kernel, grid=(lx,), in_specs=[spec, whole(mixing...  21.5 us
    ppermute x24, starting transfers between devices, over_chan(): lax.ppermute(values[d], 'chan', [(i, i ^ d) for i in range(s.chan)])  21.4 us
    pallas_call x4, Pallas kernels, first_inverse(): pl.pallas_call(body, grid=(pairs,), in_specs=[pl.BlockSpec((4 * s.jxl, LA...  15.7 us
  transfers between devices with their start and end apart: 84, of which 23 were waited for; matrix products, arithmetic and copies ran while one was open for 2% of the time, Pallas kernels for 28%

profile of v3, /device:TPU:11, one launch (start us, length us, event | category | flops | bytes accessed | tf_op | source)
XLA Modules:
  0.0 403.0 jit_solution(1688950873283429518)
XLA Ops:
  0.6 7.0 %shard_map.184 = (f32[256,128]{1,0:T(8,128)}, f32[256,128]{1,0:T(8,128)}, f32[256,128]{1,0:T(8,128)}, f32[256,128]{1,0:T(8,128)}, f32[256,128]{1,0:T(8,128)}, /*...) custom-call(s32[1]{0:T(128)} %bitcast.me_ref.refs_0_, f32[1,16,8,128,128]{4,3,2,1,0:T(8,128)} %values_ref.1, ...), custom_call_target="tpu_custom_call" | custom-call | flops 3000000000 | bytes 5242880 | tf_op jit(solution)/shard_map/pallas_call | solution.py:458
  16.0 7.0 %shard_map.185 = (f32[256,128]{1,0:T(8,128)}, f32[256,128]{1,0:T(8,128)}, f32[256,128]{1,0:T(8,128)}, f32[256,128]{1,0:T(8,128)}, f32[256,128]{1,0:T(8,128)}, /*...) custom-call(s32[1]{0:T(128)} %bitcast.me_ref.refs_0_, f32[1,16,8,128,128]{4,3,2,1,0:T(8,128)} %values_ref.1, ...), custom_call_target="tpu_custom_call" | custom-call | flops 3000000000 | bytes 5242880 | tf_op jit(solution)/shard_map/pallas_call | solution.py:458
  47.5 10.7 %pointwise.2.refs_17_.refs_8_ = f32[1,16,8,128,128]{4,3,2,1,0:T(8,128)} custom-call(f32[1,16,8,128,128]{4,3,2,1,0:T(8,128)} %values_ref.1, bf16[512,256]{1,0:T(8,128)(2,1)} %pad_maximum_fusion.mixing_ref, f32[256,128]{1,0:T(8,128)} %broadcast_in_dim.21.bias_ref), custom_call_target="tpu_custom_call" | custom-call | flops 6000000000 | bytes 16777216 | tf_op jit(solution)/shard_map/pointwise/pallas_call | solution.py:570
  72.2 10.4 %collective-permute-done.23.refs_4_ = f32[256,128]{1,0:T(8,128)S(1)} collective-permute-done((f32[256,128]{1,0:T(8,128)}, f32[256,128]{1,0:T(8,128)S(1)}, u32[]{:S(2)}, u32[]{:S(2)}) %collective-permute-start.23) | collective-permute-done | bytes 131104 | tf_op jit(solution)/shard_map/ppermute | solution.py:838
  83.3 8.2 %mix.3 = (f32[256,128]{1,0:T(8,128)}, f32[256,128]{1,0:T(8,128)}, f32[256,128]{1,0:T(8,128)}, f32[256,128]{1,0:T(8,128)}, f32[2,16,8,512]{3,2,1,0:T(8,128)}) custom-call(s32[1]{0:T(128)} %bitcast.me_ref.refs_0_, f32[256,128]{1,0:T(8,128)} %get-tuple-element.155.refs_17_.refs_1_, f32[256,128]{1,0:T(8,128)} %copy-done.47, f32[256,128]{1,0:T(8,128)} %copy-done.53, ...), custom_call_target="tpu_custom_call" | custom-call | flops 100000000 | bytes 5242880 | tf_op jit(solution)/shard_map/mix/pallas_call | solution.py:773
  94.9 8.2 %mix.2 = (f32[256,128]{1,0:T(8,128)}, f32[256,128]{1,0:T(8,128)}, f32[256,128]{1,0:T(8,128)}, f32[256,128]{1,0:T(8,128)}, f32[2,16,8,512]{3,2,1,0:T(8,128)}) custom-call(s32[1]{0:T(128)} %bitcast.me_ref.refs_0_, f32[256,128]{1,0:T(8,128)} %get-tuple-element.156.refs_1_, f32[256,128]{1,0:T(8,128)} %copy-done.44, f32[256,128]{1,0:T(8,128)} %copy-done.50, ...), custom_call_target="tpu_custom_call" | custom-call | flops 100000000 | bytes 5242880 | tf_op jit(solution)/shard_map/mix/pallas_call | solution.py:773
  110.4 6.0 %collective-permute-done.20.refs_3_ = f32[256,128]{1,0:T(8,128)S(1)} collective-permute-done((f32[256,128]{1,0:T(8,128)}, f32[256,128]{1,0:T(8,128)S(1)}, u32[]{:S(2)}, u32[]{:S(2)}) %collective-permute-start.20) | collective-permute-done | bytes 131104 | tf_op jit(solution)/shard_map/ppermute | solution.py:838
  127.7 8.6 %collective-permute-start.37 = (f32[256,128]{1,0:T(8,128)}, f32[256,128]{1,0:T(8,128)S(1)}, u32[]{:S(2)}, u32[]{:S(2)}) collective-permute-start(f32[256,128]{1,0:T(8,128)} %get-tuple-element.198), channel_id=1, source_target_pairs={{0,12},{1,13},{2,14},{3,15},{4,8},{5,9},{6,10},{7,11},{8,4},{9,5},... | collective-permute-start | bytes 393224 | tf_op jit(solution)/shard_map/ppermute | solution.py:828
  157.6 15.8 %shard_map.186 = (f32[1,16,8,128,128]{4,3,2,1,0:T(8,128)}, f32[1,16,8,128,128]{4,3,2,1,0:T(8,128)}, f32[256,128]{1,0:T(8,128)}, f32[256,128]{1,0:T(8,128)}, f32[...) custom-call(s32[1]{0:T(128)} %bitcast.me_ref.refs_0_, ...), custom_call_target="tpu_custom_call" | custom-call | flops 6000000000 | bytes 18874368 | tf_op jit(solution)/shard_map/pallas_call | solution.py:458
  177.8 15.8 %shard_map.187 = (f32[1,16,8,128,128]{4,3,2,1,0:T(8,128)}, f32[1,16,8,128,128]{4,3,2,1,0:T(8,128)}, f32[256,128]{1,0:T(8,128)}, f32[256,128]{1,0:T(8,128)}, f32[...) custom-call(s32[1]{0:T(128)} %bitcast.me_ref.refs_0_, ...), custom_call_target="tpu_custom_call", output_to_operand_aliasing={{0}: (15, {}), {1}: (16, {})} | custom-call | flops 6000000000 | bytes 18874368 | tf_op jit(solution)/shard_map/pallas_call | solution.py:458
  194.3 9.1 %collective-permute-start.44 = (f32[256,128]{1,0:T(8,128)}, f32[256,128]{1,0:T(8,128)S(1)}, u32[]{:S(2)}, u32[]{:S(2)}) collective-permute-start(f32[256,128]{1,0:T(8,128)} %get-tuple-element.209), channel_id=1, source_target_pairs={{0,3},{1,2},{2,1},{3,0},{4,7},{5,6},{6,5},{7,4},{8,11},{9,10},{10,... | collective-permute-start | bytes 393224 | tf_op jit(solution)/shard_map/ppermute | solution.py:828
  210.4 13.8 %collective-permute-done.44.refs_3_ = f32[256,128]{1,0:T(8,128)S(1)} collective-permute-done((f32[256,128]{1,0:T(8,128)}, f32[256,128]{1,0:T(8,128)S(1)}, u32[]{:S(2)}, u32[]{:S(2)}) %collective-permute-start.44) | collective-permute-done | bytes 131104 | tf_op jit(solution)/shard_map/ppermute | solution.py:828
  226.9 9.0 %collective-permute-done.48.refs_7_ = f32[256,128]{1,0:T(8,128)S(1)} collective-permute-done((f32[256,128]{1,0:T(8,128)}, f32[256,128]{1,0:T(8,128)S(1)}, u32[]{:S(2)}, u32[]{:S(2)}) %collective-permute-start.48) | collective-permute-done | bytes 131104 | tf_op jit(solution)/shard_map/ppermute | solution.py:828
  251.5 10.7 %pointwise.3.refs_17_.refs_8_ = f32[1,16,8,128,128]{4,3,2,1,0:T(8,128)} custom-call(f32[1,16,8,128,128]{4,3,2,1,0:T(8,128)} %get-tuple-element.222.values_ref, bf16[512,256]{1,0:T(8,128)(2,1)} %pad_maximum_fusion.1.mixing_ref, f32[256,128]{1,0:T(8,128)} %broadcast_in_dim.22.bias_ref), custom_call_target="tpu_custom_call" | custom-call | flops 6000000000 | bytes 16777216 | tf_op jit(solution)/shard_map/pointwise/pallas_call | solution.py:570
  276.4 10.9 %collective-permute-done.65.refs_4_ = f32[256,128]{1,0:T(8,128)S(1)} collective-permute-done((f32[256,128]{1,0:T(8,128)}, f32[256,128]{1,0:T(8,128)S(1)}, u32[]{:S(2)}, u32[]{:S(2)}) %collective-permute-start.65) | collective-permute-done | bytes 131104 | tf_op jit(solution)/shard_map/ppermute | solution.py:838
  287.9 8.2 %unmix.3 = (f32[256,128]{1,0:T(8,128)}, f32[256,128]{1,0:T(8,128)}, f32[256,128]{1,0:T(8,128)}, f32[256,128]{1,0:T(8,128)}, f32[2,16,8,512]{3,2,1,0:T(8,128)}) custom-call(s32[1]{0:T(128)} %bitcast.me_ref.refs_0_, f32[256,128]{1,0:T(8,128)} %get-tuple-element.223.refs_17_.refs_1_, f32[256,128]{1,0:T(8,128)} %copy-done.45, f32[256,128]{1,0:T(8,128)} %copy-done.51, ...), custom_call_target="tpu_custom_call" | custom-call | flops 100000000 | bytes 5242880 | tf_op jit(solution)/shard_map/unmix/pallas_call | solution.py:773
  299.5 8.2 %unmix.2 = (f32[256,128]{1,0:T(8,128)}, f32[256,128]{1,0:T(8,128)}, f32[256,128]{1,0:T(8,128)}, f32[256,128]{1,0:T(8,128)}, f32[2,16,8,512]{3,2,1,0:T(8,128)}) custom-call(s32[1]{0:T(128)} %bitcast.me_ref.refs_0_, f32[256,128]{1,0:T(8,128)} %get-tuple-element.224.refs_1_, f32[256,128]{1,0:T(8,128)} %copy-done.46, f32[256,128]{1,0:T(8,128)} %copy-done.52, ...), custom_call_target="tpu_custom_call" | custom-call | flops 100000000 | bytes 5242880 | tf_op jit(solution)/shard_map/unmix/pallas_call | solution.py:773
  315.4 6.6 %collective-permute-done.62.refs_3_ = f32[256,128]{1,0:T(8,128)S(1)} collective-permute-done((f32[256,128]{1,0:T(8,128)}, f32[256,128]{1,0:T(8,128)S(1)}, u32[]{:S(2)}, u32[]{:S(2)}) %collective-permute-start.62) | collective-permute-done | bytes 131104 | tf_op jit(solution)/shard_map/ppermute | solution.py:838
  332.3 6.1 %collective-permute-done.69.refs_0_ = f32[256,128]{1,0:T(8,128)S(1)} collective-permute-done((f32[256,128]{1,0:T(8,128)}, f32[256,128]{1,0:T(8,128)S(1)}, u32[]{:S(2)}, u32[]{:S(2)}) %collective-permute-start.69) | collective-permute-done | bytes 131104 | tf_op jit(solution)/shard_map/ppermute | solution.py:828
  348.9 6.6 %weight_grads.2.refs_0_ = f32[2,16,16,16,512]{4,3,2,1,0:T(8,128)} custom-call(f32[2,16,8,512]{3,2,1,0:T(8,128)} %get-tuple-element.273.spec_ref, f32[2,16,8,512]{3,2,1,0:T(8,128)} %get-tuple-element.274.grad_ref), custom_call_target="tpu_custom_call" | custom-call | flops 100000000 | bytes 16777216 | tf_op jit(solution)/shard_map/weight_grads/pallas_call | solution.py:811
  355.6 6.8 %weight_grads.3 = f32[2,16,16,16,512]{4,3,2,1,0:T(8,128)} custom-call(f32[2,16,8,512]{3,2,1,0:T(8,128)} %get-tuple-element.271.spec_ref, f32[2,16,8,512]{3,2,1,0:T(8,128)} %get-tuple-element.272.grad_ref, f32[2,16,16,16,512]{4,3,2,1,0:T(8,128)} %weight_grads.2.refs_0_), custom_call_target="tpu_custom_call", output_to_operand_aliasing={{}: (2, {})} | custom-call | flops 100000000 | bytes 16777216 | tf_op jit(solution)/shard_map/weight_grads/pallas_call | solution.py:811
  369.5 7.3 %shard_map.188.refs_11_ = f32[1,16,8,128,128]{4,3,2,1,0:T(8,128)} custom-call(s32[1]{0:T(128)} %bitcast.me_ref.refs_0_, f32[256,128]{1,0:T(8,128)} %get-tuple-element.263.refs_0_, f32[256,128]{1,0:T(8,128)} %copy-done.32, f32[256,128]{1,0:T(8,128)} %copy-done.33, f32[256,128]{1,0:T(8,128)} %copy-done.35, f32[256,128]{1,0:T(8,128)} %copy-done.37, ...), custom_call_target="tpu_custom_call" | custom-call | flops 3000000000 | bytes 9437184 | tf_op jit(solution)/shard_map/pallas_call | solution.py:458
  376.9 7.7 %collective-permute-done.73.refs_4_ = f32[256,128]{1,0:T(8,128)S(1)} collective-permute-done((f32[256,128]{1,0:T(8,128)S(1)}, f32[256,128]{1,0:T(8,128)S(1)}, u32[]{:S(2)}, u32[]{:S(2)}) %collective-permute-start.73) | collective-permute-done | bytes 131104 | tf_op jit(solution)/shard_map/ppermute | solution.py:828
  395.7 7.3 %shard_map.189 = f32[1,16,8,128,128]{4,3,2,1,0:T(8,128)} custom-call(s32[1]{0:T(128)} %bitcast.me_ref.refs_0_, f32[256,128]{1,0:T(8,128)} %copy-done.29, f32[256,128]{1,0:T(8,128)} %copy-done.30, f32[256,128]{1,0:T(8,128)} %copy-done.31, f32[256,128]{1,0:T(8,128)} %copy-done.40, f32[256,128]{1,0:T(8,128)} %copy-done.43, ...), custom_call_target="tpu_custom_call", output_to_operand_aliasing={{}: (12, {})} | custom-call | flops 3000000000 | bytes 9437184 | tf_op jit(solution)/shard_map/pallas_call | solution.py:458
  (361 shorter events, 185.3 us)
Async XLA Ops:
  34.3 24.0 %collective-permute-start.6 = (f32[256,128]{1,0:T(8,128)}, f32[256,128]{1,0:T(8,128)S(1)}, u32[]{:S(2)}, u32[]{:S(2)}) collective-permute-start(f32[256,128]{1,0:T(8,128)} %get-tuple-element.146), channel_id=1, source_target_pairs={{0,7},{1,6},{2,5},{3,4},{4,3},{5,2},{6,1},{7,0},{8,15},{9,14},{10,... | collective-permute-start | bytes 393224 | tf_op jit(solution)/shard_map/ppermute | solution.py:828
  35.5 22.8 %collective-permute-start.8 = (f32[256,128]{1,0:T(8,128)}, f32[256,128]{1,0:T(8,128)S(1)}, u32[]{:S(2)}, u32[]{:S(2)}) collective-permute-start(f32[256,128]{1,0:T(8,128)} %get-tuple-element.148), channel_id=1, source_target_pairs={{0,9},{1,8},{2,11},{3,10},{4,13},{5,12},{6,15},{7,14},{8,1},{9,0},... | collective-permute-start | bytes 393224 | tf_op jit(solution)/shard_map/ppermute | solution.py:828
  69.5 22.0 %collective-permute-start.15 = (f32[256,128]{1,0:T(8,128)}, f32[256,128]{1,0:T(8,128)S(1)}, u32[]{:S(2)}, u32[]{:S(2)}) collective-permute-start(f32[256,128]{1,0:T(8,128)} %get-tuple-element.157), channel_id=1, source_target_pairs={{0,1},{1,0},{2,3},{3,2},{4,5},{5,4},{6,7},{7,6},{8,9},{9,8},{10,11... | collective-permute-start | bytes 393224 | tf_op jit(solution)/shard_map/ppermute | solution.py:838
  70.7 23.4 %collective-permute-start.16 = (f32[256,128]{1,0:T(8,128)}, f32[256,128]{1,0:T(8,128)S(1)}, u32[]{:S(2)}, u32[]{:S(2)}) collective-permute-start(f32[256,128]{1,0:T(8,128)} %get-tuple-element.158), channel_id=1, source_target_pairs={{0,2},{1,3},{2,0},{3,1},{4,6},{5,7},{6,4},{7,5},{8,10},{9,11},{10,... | collective-permute-start | bytes 393224 | tf_op jit(solution)/shard_map/ppermute | solution.py:838
  71.4 22.8 %collective-permute-start.17 = (f32[256,128]{1,0:T(8,128)}, f32[256,128]{1,0:T(8,128)S(1)}, u32[]{:S(2)}, u32[]{:S(2)}) collective-permute-start(f32[256,128]{1,0:T(8,128)} %get-tuple-element.159), channel_id=1, source_target_pairs={{0,3},{1,2},{2,1},{3,0},{4,7},{5,6},{6,5},{7,4},{8,11},{9,10},{10,... | collective-permute-start | bytes 393224 | tf_op jit(solution)/shard_map/ppermute | solution.py:838
  145.3 28.1 %collective-permute-start.30 = (f32[256,128]{1,0:T(8,128)}, f32[256,128]{1,0:T(8,128)S(1)}, u32[]{:S(2)}, u32[]{:S(2)}) collective-permute-start(f32[256,128]{1,0:T(8,128)} %get-tuple-element.190), channel_id=1, source_target_pairs={{0,14},{1,15},{2,12},{3,13},{4,10},{5,11},{6,8},{7,9},{8,6},{9,7},... | collective-permute-start | bytes 393224 | tf_op jit(solution)/shard_map/ppermute | solution.py:828
  147.7 25.7 %collective-permute-start.31 = (f32[256,128]{1,0:T(8,128)}, f32[256,128]{1,0:T(8,128)S(1)}, u32[]{:S(2)}, u32[]{:S(2)}) collective-permute-start(f32[256,128]{1,0:T(8,128)} %get-tuple-element.191), channel_id=1, source_target_pairs={{0,3},{1,2},{2,1},{3,0},{4,7},{5,6},{6,5},{7,4},{8,11},{9,10},{10,... | collective-permute-start | bytes 393224 | tf_op jit(solution)/shard_map/ppermute | solution.py:828
  149.3 24.1 %collective-permute-start.32 = (f32[256,128]{1,0:T(8,128)}, f32[256,128]{1,0:T(8,128)S(1)}, u32[]{:S(2)}, u32[]{:S(2)}) collective-permute-start(f32[256,128]{1,0:T(8,128)} %get-tuple-element.192), channel_id=1, source_target_pairs={{0,7},{1,6},{2,5},{3,4},{4,3},{5,2},{6,1},{7,0},{8,15},{9,14},{10,... | collective-permute-start | bytes 393224 | tf_op jit(solution)/shard_map/ppermute | solution.py:828
  156.2 21.0 %collective-permute-start.34 = (f32[256,128]{1,0:T(8,128)}, f32[256,128]{1,0:T(8,128)S(1)}, u32[]{:S(2)}, u32[]{:S(2)}) collective-permute-start(f32[256,128]{1,0:T(8,128)} %get-tuple-element.194), channel_id=1, source_target_pairs={{0,15},{1,14},{2,13},{3,12},{4,11},{5,10},{6,9},{7,8},{8,7},{9,6},... | collective-permute-start | bytes 393224 | tf_op jit(solution)/shard_map/ppermute | solution.py:828
  194.3 29.8 %collective-permute-start.44 = (f32[256,128]{1,0:T(8,128)}, f32[256,128]{1,0:T(8,128)S(1)}, u32[]{:S(2)}, u32[]{:S(2)}) collective-permute-start(f32[256,128]{1,0:T(8,128)} %get-tuple-element.209), channel_id=1, source_target_pairs={{0,3},{1,2},{2,1},{3,0},{4,7},{5,6},{6,5},{7,4},{8,11},{9,10},{10,... | collective-permute-start | bytes 393224 | tf_op jit(solution)/shard_map/ppermute | solution.py:828
  203.5 23.4 %collective-permute-start.47 = (f32[256,128]{1,0:T(8,128)}, f32[256,128]{1,0:T(8,128)S(1)}, u32[]{:S(2)}, u32[]{:S(2)}) collective-permute-start(f32[256,128]{1,0:T(8,128)} %get-tuple-element.212), channel_id=1, source_target_pairs={{0,6},{1,7},{2,4},{3,5},{4,2},{5,3},{6,0},{7,1},{8,14},{9,15},{10,... | collective-permute-start | bytes 393224 | tf_op jit(solution)/shard_map/ppermute | solution.py:828
  204.5 31.4 %collective-permute-start.48 = (f32[256,128]{1,0:T(8,128)}, f32[256,128]{1,0:T(8,128)S(1)}, u32[]{:S(2)}, u32[]{:S(2)}) collective-permute-start(f32[256,128]{1,0:T(8,128)} %get-tuple-element.213), channel_id=1, source_target_pairs={{0,7},{1,6},{2,5},{3,4},{4,3},{5,2},{6,1},{7,0},{8,15},{9,14},{10,... | collective-permute-start | bytes 393224 | tf_op jit(solution)/shard_map/ppermute | solution.py:828
  204.5 31.4 %collective-permute-start.51 = (f32[256,128]{1,0:T(8,128)}, f32[256,128]{1,0:T(8,128)S(1)}, u32[]{:S(2)}, u32[]{:S(2)}) collective-permute-start(f32[256,128]{1,0:T(8,128)} %get-tuple-element.216), channel_id=1, source_target_pairs={{0,10},{1,11},{2,8},{3,9},{4,14},{5,15},{6,12},{7,13},{8,2},{9,3},... | collective-permute-start | bytes 393224 | tf_op jit(solution)/shard_map/ppermute | solution.py:828
  206.6 32.7 %collective-permute-start.52 = (f32[256,128]{1,0:T(8,128)}, f32[256,128]{1,0:T(8,128)S(1)}, u32[]{:S(2)}, u32[]{:S(2)}) collective-permute-start(f32[256,128]{1,0:T(8,128)} %get-tuple-element.217), channel_id=1, source_target_pairs={{0,11},{1,10},{2,9},{3,8},{4,15},{5,14},{6,13},{7,12},{8,3},{9,2},... | collective-permute-start | bytes 393224 | tf_op jit(solution)/shard_map/ppermute | solution.py:828
  239.3 23.1 %collective-permute-start.46 = (f32[256,128]{1,0:T(8,128)}, f32[256,128]{1,0:T(8,128)S(1)}, u32[]{:S(2)}, u32[]{:S(2)}) collective-permute-start(f32[256,128]{1,0:T(8,128)} %get-tuple-element.211), channel_id=1, source_target_pairs={{0,5},{1,4},{2,7},{3,6},{4,1},{5,0},{6,3},{7,2},{8,13},{9,12},{10,... | collective-permute-start | bytes 393224 | tf_op jit(solution)/shard_map/ppermute | solution.py:828
  273.6 22.9 %collective-permute-start.57 = (f32[256,128]{1,0:T(8,128)}, f32[256,128]{1,0:T(8,128)S(1)}, u32[]{:S(2)}, u32[]{:S(2)}) collective-permute-start(f32[256,128]{1,0:T(8,128)} %get-tuple-element.225), channel_id=1, source_target_pairs={{0,1},{1,0},{2,3},{3,2},{4,5},{5,4},{6,7},{7,6},{8,9},{9,8},{10,11... | collective-permute-start | bytes 393224 | tf_op jit(solution)/shard_map/ppermute | solution.py:838
  274.7 24.1 %collective-permute-start.58 = (f32[256,128]{1,0:T(8,128)}, f32[256,128]{1,0:T(8,128)S(1)}, u32[]{:S(2)}, u32[]{:S(2)}) collective-permute-start(f32[256,128]{1,0:T(8,128)} %get-tuple-element.226), channel_id=1, source_target_pairs={{0,2},{1,3},{2,0},{3,1},{4,6},{5,7},{6,4},{7,5},{8,10},{9,11},{10,... | collective-permute-start | bytes 393224 | tf_op jit(solution)/shard_map/ppermute | solution.py:838
  275.0 23.7 %collective-permute-start.59 = (f32[256,128]{1,0:T(8,128)}, f32[256,128]{1,0:T(8,128)S(1)}, u32[]{:S(2)}, u32[]{:S(2)}) collective-permute-start(f32[256,128]{1,0:T(8,128)} %get-tuple-element.227), channel_id=1, source_target_pairs={{0,3},{1,2},{2,1},{3,0},{4,7},{5,6},{6,5},{7,4},{8,11},{9,10},{10,... | collective-permute-start | bytes 393224 | tf_op jit(solution)/shard_map/ppermute | solution.py:838
  338.5 23.9 %collective-permute-start.79 = (f32[256,128]{1,0:T(8,128)}, f32[256,128]{1,0:T(8,128)S(1)}, u32[]{:S(2)}, u32[]{:S(2)}) collective-permute-start(f32[256,128]{1,0:T(8,128)} %get-tuple-element.266), channel_id=1, source_target_pairs={{0,12},{1,13},{2,14},{3,15},{4,8},{5,9},{6,10},{7,11},{8,4},{9,5},... | collective-permute-start | bytes 393224 | tf_op jit(solution)/shard_map/ppermute | solution.py:828
  341.3 23.0 %collective-permute-start.80 = (f32[256,128]{1,0:T(8,128)}, f32[256,128]{1,0:T(8,128)S(1)}, u32[]{:S(2)}, u32[]{:S(2)}) collective-permute-start(f32[256,128]{1,0:T(8,128)} %get-tuple-element.267), channel_id=1, source_target_pairs={{0,1},{1,0},{2,3},{3,2},{4,5},{5,4},{6,7},{7,6},{8,9},{9,8},{10,11... | collective-permute-start | bytes 393224 | tf_op jit(solution)/shard_map/ppermute | solution.py:828
  347.6 20.6 %collective-permute-start.83 = (f32[256,128]{1,0:T(8,128)}, f32[256,128]{1,0:T(8,128)S(1)}, u32[]{:S(2)}, u32[]{:S(2)}) collective-permute-start(f32[256,128]{1,0:T(8,128)} %get-tuple-element.270), channel_id=1, source_target_pairs={{0,13},{1,12},{2,15},{3,14},{4,9},{5,8},{6,11},{7,10},{8,5},{9,4},... | collective-permute-start | bytes 393224 | tf_op jit(solution)/shard_map/ppermute | solution.py:828
  365.1 24.7 %collective-permute-start.74 = (f32[256,128]{1,0:T(8,128)S(1)}, f32[256,128]{1,0:T(8,128)S(1)}, u32[]{:S(2)}, u32[]{:S(2)}) collective-permute-start(f32[256,128]{1,0:T(8,128)S(1)} %copy-done.68), channel_id=1, source_target_pairs={{0,7},{1,6},{2,5},{3,4},{4,3},{5,2},{6,1},{7,0},{8,15},{9,14},{10,... | collective-permute-start | bytes 393224 | tf_op jit(solution)/shard_map/ppermute | solution.py:828
  367.2 24.9 %collective-permute-start.75 = (f32[256,128]{1,0:T(8,128)S(1)}, f32[256,128]{1,0:T(8,128)S(1)}, u32[]{:S(2)}, u32[]{:S(2)}) collective-permute-start(f32[256,128]{1,0:T(8,128)S(1)} %copy-done.69), channel_id=1, source_target_pairs={{0,11},{1,10},{2,9},{3,8},{4,15},{5,14},{6,13},{7,12},{8,3},{9,2},... | collective-permute-start | bytes 393224 | tf_op jit(solution)/shard_map/ppermute | solution.py:828
  368.1 26.9 %collective-permute-start.76 = (f32[256,128]{1,0:T(8,128)S(1)}, f32[256,128]{1,0:T(8,128)S(1)}, u32[]{:S(2)}, u32[]{:S(2)}) collective-permute-start(f32[256,128]{1,0:T(8,128)S(1)} %copy-done.71), channel_id=1, source_target_pairs={{0,15},{1,14},{2,13},{3,12},{4,11},{5,10},{6,9},{7,8},{8,7},{9,6},... | collective-permute-start | bytes 393224 | tf_op jit(solution)/shard_map/ppermute | solution.py:828
  (151 other events, 2039.3 us)

commit v4 on v3

--- a/solution.py
+++ b/solution.py
@@ -217,9 +217,8 @@
     return high, low
 
 
-def stacked_square(table):
-    high, low = two_terms(table)
-    return np.concatenate([np.concatenate([high, high], 1), np.concatenate([low, low], 1)], 0)
+def stacked(table):
+    return np.concatenate(two_terms(table), 0)
 
 
 def second_tables(s):
@@ -228,7 +227,7 @@
     inverse = np.concatenate(
         [np.concatenate([cosine.T, -sine.T], 1), np.concatenate([sine.T, cosine.T], 1)], 0
     )
-    return stacked_square(forward), stacked_square(inverse)
+    return stacked(forward), stacked(inverse)
 
 
 def third_tables(s):
@@ -240,8 +239,7 @@
     table = table.reshape(2 * s.gz, LANES)
     forward = np.concatenate(two_terms(table), 1)
     high, low = two_terms(table.T)
-    wide = np.concatenate([high, low], 1)
-    return forward, np.concatenate([wide, wide], 0)
+    return forward, np.concatenate([high, low], 1)
 
 
 def first_tables(s):
@@ -268,7 +266,7 @@
 
 def square_dot(table, value):
     high, low = terms(value)
-    both = dot(table, jnp.concatenate([high, low], 0))
+    both = dot(jnp.concatenate([table, table], 1), jnp.concatenate([high, low], 0))
     half = both.shape[0] // 2
     return both[:half] + both[half:]
 
@@ -355,7 +353,8 @@
             ):
                 high, low = terms(side)
                 sides.append(jnp.concatenate([high, low], 1))
-    both = dot(jnp.concatenate(sides, 0), third_ref[...])
+    table = third_ref[...]
+    both = dot(jnp.concatenate(sides, 0), jnp.concatenate([table, table], 0))
     planes[...] = both[:, :2 * s.gz] + both[:, 2 * s.gz:]
 
 
@@ -562,10 +561,14 @@
 def pointwise(values, weight, bias):
     _, channels, lx, gy, gz = values.shape
     strip = 2 * LANES // channels
-    mixing = jnp.kron(weight.T, jnp.eye(strip, dtype=f32))
+    rows = channels * strip
+    spread = np.repeat(np.eye(channels, dtype=np.float32), strip, 0)
+    diagonal = np.tile(np.eye(strip, dtype=bool), (channels, channels))
+    exact = functools.partial(jnp.dot, precision=lax.Precision.HIGHEST)
+    mixing = jnp.where(diagonal, exact(exact(spread, weight.T), spread.T), 0.0)
     high = lax.reduce_precision(mixing, 8, 7)
     mixing = jnp.concatenate([high.astype(bf16), (mixing - high).astype(bf16)], 0)
-    bias_rows = jnp.broadcast_to(jnp.repeat(bias, strip)[:, None], (channels * strip, LANES))
+    bias_rows = jnp.broadcast_to(exact(spread, bias[:, None]), (rows, LANES))
     spec = pl.BlockSpec((1, channels, 1, gy, gz), lambda x: (0, 0, x, 0, 0))
     return pl.pallas_call(
         pointwise_kernel,
@@ -589,27 +592,29 @@
 
 def first_kernel(s, ins, stacked_ref, outs, gathered, held):
     me = lax.axis_index("chan")
-    rows = held.shape[0]
+    rows = held.shape[1]
     per = 2 * s.lx
-    for in_ref, (p, c) in zip(ins, distances(s)):
-        for j in range(2):
-            gathered[owner_rows(s, p, c, per), j * LANES:(j + 1) * LANES] = in_ref[j * per:(j + 1) * per, :]
-    high, low = terms(gathered[...])
-    both = dot(stacked_ref[...], high)
-    held[...] = both[:rows] + both[rows:] + dot(stacked_ref[:rows, :], low)
-    step = rows // s.chan
-    for d, out_ref in enumerate(outs):
-        at = pl.ds(pl.multiple_of((me ^ d) * step, step), step)
-        for j in range(2):
-            out_ref[j * step:(j + 1) * step, :] = held[at, j * LANES:(j + 1) * LANES]
+    step = rows // len(outs)
+    for pair in range(gathered.shape[0]):
+        for in_ref, (p, c) in zip(ins, distances(s)):
+            for j in range(2):
+                start = (2 * pair + j) * per
+                gathered[pair, owner_rows(s, p, c, per), j * LANES:(j + 1) * LANES] = in_ref[start:start + per, :]
+        high, low = terms(gathered[pair])
+        both = dot(stacked_ref[...], high)
+        held[pair] = both[:rows] + both[rows:] + dot(stacked_ref[:rows, :], low)
+        for d, out_ref in enumerate(outs):
+            at = pl.ds(pl.multiple_of((me ^ d) * step, step), step)
+            for j in range(2):
+                start = (2 * pair + j) * step
+                out_ref[start:start + step, :] = held[pair, at, j * LANES:(j + 1) * LANES]
 
 
 def first_pass(s, arrived, table, mode_chunk, after):
     rows = table.shape[0]
-    stacked = np.concatenate(two_terms(table), 0)
+    tall = stacked(table)
     pairs = s.jl // MODE_CHUNKS // 2
     out = jax.ShapeDtypeStruct((pairs * 2 * 2 * s.jxl, LANES), f32)
-    offset = mode_chunk * pairs
 
     def body(*refs):
         outs = refs[s.owners + 1 + len(after):-2]
@@ -617,39 +622,45 @@
 
     return pl.pallas_call(
         body,
-        grid=(pairs,),
-        in_specs=[pl.BlockSpec((4 * s.lx, LANES), lambda j: (j + offset, 0))] * s.owners
-        + [whole(stacked)]
+        grid=(1,),
+        in_specs=[
+            pl.BlockSpec(
+                (pairs * 4 * s.lx, LANES), lambda j: (mode_chunk, 0), pipeline_mode=pl.Buffered(1)
+            )
+        ] * s.owners
+        + [whole(tall)]
         + [anywhere()] * len(after),
-        out_specs=[pl.BlockSpec((4 * s.jxl, LANES), lambda j: (j, 0))] * s.chan,
+        out_specs=[whole(out)] * s.chan,
         out_shape=[out] * s.chan,
         scratch_shapes=[
-            pltpu.VMEM((s.owners * 2 * s.lx, 2 * LANES), f32),
-            pltpu.VMEM((rows, 2 * LANES), f32),
+            pltpu.VMEM((pairs, s.owners * 2 * s.lx, 2 * LANES), f32),
+            pltpu.VMEM((pairs, rows, 2 * LANES), f32),
         ],
         cost_estimate=cost(1e9 / MODE_CHUNKS, *[out] * 12),
         name="first_forward",
-    )(*arrived, stacked, *after)
+    )(*arrived, tall, *after)
 
 
 def back_kernel(s, ins, table_ref, outs, gathered, held):
     me = lax.axis_index("chan")
     step = 2 * s.jxl
-    for d, in_ref in enumerate(ins):
-        at = pl.ds(pl.multiple_of((me ^ d) * step, step), step)
-        for j in range(2):
-            gathered[at, j * LANES:(j + 1) * LANES] = in_ref[j * step:(j + 1) * step, :]
-    held[...] = square_dot(table_ref[...], gathered[...])
     per = 2 * s.lx
-    for out_ref, (p, c) in zip(outs, distances(s)):
-        for j in range(2):
-            out_ref[j * per:(j + 1) * per, :] = held[owner_rows(s, p, c, per), j * LANES:(j + 1) * LANES]
+    for pair in range(gathered.shape[0]):
+        for d, in_ref in enumerate(ins):
+            at = pl.ds(pl.multiple_of((me ^ d) * step, step), step)
+            for j in range(2):
+                start = (2 * pair + j) * step
+                gathered[pair, at, j * LANES:(j + 1) * LANES] = in_ref[start:start + step, :]
+        held[pair] = square_dot(table_ref[...], gathered[pair])
+        for out_ref, (p, c) in zip(outs, distances(s)):
+            for j in range(2):
+                start = (2 * pair + j) * per
+                out_ref[start:start + per, :] = held[pair, owner_rows(s, p, c, per), j * LANES:(j + 1) * LANES]
 
 
 def first_inverse(s, modes, table, mode_chunk, totals):
-    square = stacked_square(table)
+    square = stacked(table)
     pairs = s.jl // MODE_CHUNKS // 2
-    offset = mode_chunk * pairs
     out = mode_shape(s)
     count = s.chan + 1
 
@@ -658,15 +669,19 @@
 
     return pl.pallas_call(
         body,
-        grid=(pairs,),
-        in_specs=[pl.BlockSpec((4 * s.jxl, LANES), lambda j: (j, 0))] * s.chan
+        grid=(1,),
+        in_specs=[whole(v) for v in modes]
         + [whole(square)]
         + [anywhere()] * len(totals),
-        out_specs=[pl.BlockSpec((4 * s.lx, LANES), lambda j: (j + offset, 0))] * s.owners,
+        out_specs=[
+            pl.BlockSpec(
+                (pairs * 4 * s.lx, LANES), lambda j: (mode_chunk, 0), pipeline_mode=pl.Buffered(1)
+            )
+        ] * s.owners,
         out_shape=[out] * s.owners,
         scratch_shapes=[
-            pltpu.VMEM((s.chan * 2 * s.jxl, 2 * LANES), f32),
-            pltpu.VMEM((s.owners * 2 * s.lx, 2 * LANES), f32),
+            pltpu.VMEM((pairs, s.chan * 2 * s.jxl, 2 * LANES), f32),
+            pltpu.VMEM((pairs, s.owners * 2 * s.lx, 2 * LANES), f32),
         ],
         input_output_aliases={count + i: i for i in range(len(totals))},
         cost_estimate=cost(1e9 / MODE_CHUNKS, *modes, *modes, *modes),
@@ -694,9 +709,11 @@
 def spread_modes(s, count, ins, out_ref, factor=None):
     stride = 2 * s.jxl
     me = lax.axis_index("chan")
-    for d, in_ref in enumerate(ins):
-        for part in range(2):
-            for a in range(s.jxl // s.gw):
+
+    def one(a, carry):
+        at = pl.ds(pl.multiple_of(a * LANES, LANES), LANES)
+        for d, in_ref in enumerate(ins):
+            for part in range(2):
                 pieces = [
                     in_ref[pl.ds(part * s.jxl + a * s.gw + b, count, stride=stride), :]
                     for b in range(s.gw)
@@ -704,7 +721,10 @@
                 for c, piece in enumerate(swap_groups(pieces, s.modes)):
                     if factor is not None:
                         piece = piece * factor
-                    out_ref[part, (me ^ d) * s.gw + c, :, a * LANES:(a + 1) * LANES] = piece
+                    out_ref[part, (me ^ d) * s.gw + c, :, at] = piece
+        return carry
+
+    lax.fori_loop(0, s.jxl // s.gw, one, 0)
 
 
 def depth_factor(s, shape):
@@ -842,13 +862,14 @@
 def mode_side(s, sent, tables, spec_weight, adjoint, after):
     mode_chunks = range(MODE_CHUNKS)
     arrived = [over_owners(s, p, c, sent[c][p]) for p, c in distances(s)]
-    owned = []
+    owned, mixed, returned = [], [], []
     for m in mode_chunks:
         sent_on = first_pass(s, arrived, tables[0], m, after)
         after = sent_on[:1]
         owned.append(over_chan(s, sent_on))
-    mixed = [mix(s, owned[m], spec_weight, m, adjoint) for m in mode_chunks]
-    returned = [over_chan(s, v[0]) for v in mixed]
+    for m in mode_chunks:
+        mixed.append(mix(s, owned[m], spec_weight, m, adjoint))
+        returned.append(over_chan(s, mixed[m][0]))
     totals = ()
     for m in mode_chunks:
         totals = first_inverse(s, returned[m], tables[1], m, totals)

time: 406 us -> 400 us (0.985)
  starting transfers between devices: 122 us -> 149 us
  waiting for transfers between devices: 102 us -> 87.8 us
  Pallas kernels: 159 us -> 146 us
  local copies, waits for them, and re-layouts: 15.5 us -> 10.3 us
    ppermute x60, starting transfers between devices: 100 us -> 125 us  [over_owners(): return lax.ppermute(value, ('planes', 'chan'), pairs)]
    ppermute x60, waiting for transfers between devices: 67.8 us -> 49.4 us  [over_owners(): return lax.ppermute(value, ('planes', 'chan'), pairs)]
    pallas_call x8, Pallas kernels: 31.2 us -> 21.3 us  [the longest x4 10.7 us: first_inverse(): pl.pallas_call(body, grid=(1,), in_specs=[whole(v) for v in modes] + [who...]
    ppermute x24, waiting for transfers between devices: 34.4 us -> 38.5 us  [over_chan(): lax.ppermute(values[d], 'chan', [(i, i ^ d) for i in range(s.chan)])]
    unnamed x182 -> x208, local copies, waits for them, and re-layouts: 10.5 us -> 8.92 us
  transfers between devices with their start and end apart: 84 -> 84, of which waited for: 23 -> 27; matrix products, arithmetic and copies ran while one was open for 2% -> 1% of each run, Pallas kernels for 28% -> 27%
where the time goes in v4:
time: 400 us; the launch traced here: 398 us
  starting transfers between devices  149 us (37%)
  Pallas kernels  146 us (36%)
  waiting for transfers between devices  87.8 us (22%)
  local copies, waits for them, and re-layouts  10.3 us (3%)
    ppermute x60, starting transfers between devices, over_owners(): return lax.ppermute(value, ('planes', 'chan'), pairs)  125 us
    pallas_call x6, Pallas kernels, group_call(): pl.pallas_call(body, grid_spec=pltpu.PrefetchScalarGridSpec(num_scalar_pr...  59.8 us
    ppermute x60, waiting for transfers between devices, over_owners(): return lax.ppermute(value, ('planes', 'chan'), pairs)  49.4 us
    ppermute x24, waiting for transfers between devices, over_chan(): lax.ppermute(values[d], 'chan', [(i, i ^ d) for i in range(s.chan)])  38.5 us
    pallas_call x4, Pallas kernels, mix(): pl.pallas_call(functools.partial(mix_kernel, s, count, adjoint), grid_spe...  30.4 us
    ppermute x24, starting transfers between devices, over_chan(): lax.ppermute(values[d], 'chan', [(i, i ^ d) for i in range(s.chan)])  24.4 us
    pallas_call x2, Pallas kernels, pointwise(): pl.pallas_call(pointwise_kernel, grid=(lx,), in_specs=[spec, whole(mixing...  21.5 us
    pallas_call x2, Pallas kernels, weight_grads(): pl.pallas_call(body, grid=(s.ch // width,), in_specs=[pl.BlockSpec((2, wi...  13.4 us
  transfers between devices with their start and end apart: 84, of which 27 were waited for; matrix products, arithmetic and copies ran while one was open for 1% of the time, Pallas kernels for 27%

profile of v4, /device:TPU:11, one launch (start us, length us, event | category | flops | bytes accessed | tf_op | source)
XLA Modules:
  0.0 398.3 jit_solution(11935838951086104001)
XLA Ops:
  0.7 6.9 %shard_map.238 = (f32[256,128]{1,0:T(8,128)}, f32[256,128]{1,0:T(8,128)}, f32[256,128]{1,0:T(8,128)}, f32[256,128]{1,0:T(8,128)}, f32[256,128]{1,0:T(8,128)}, /*...) custom-call(s32[1]{0:T(128)} %bitcast.me_ref.refs_0_, f32[1,16,8,128,128]{4,3,2,1,0:T(8,128)} %values_ref.1, ...), custom_call_target="tpu_custom_call" | custom-call | flops 3000000000 | bytes 5242880 | tf_op jit(solution)/shard_map/pallas_call | solution.py:457
  14.4 6.9 %shard_map.239 = (f32[256,128]{1,0:T(8,128)}, f32[256,128]{1,0:T(8,128)}, f32[256,128]{1,0:T(8,128)}, f32[256,128]{1,0:T(8,128)}, f32[256,128]{1,0:T(8,128)}, /*...) custom-call(s32[1]{0:T(128)} %bitcast.me_ref.refs_0_, f32[1,16,8,128,128]{4,3,2,1,0:T(8,128)} %values_ref.1, ...), custom_call_target="tpu_custom_call" | custom-call | flops 3000000000 | bytes 5242880 | tf_op jit(solution)/shard_map/pallas_call | solution.py:457
  36.9 6.6 %collective-permute-start.10 = (f32[256,128]{1,0:T(8,128)}, f32[256,128]{1,0:T(8,128)S(1)}, u32[]{:S(2)}, u32[]{:S(2)}) collective-permute-start(f32[256,128]{1,0:T(8,128)} %get-tuple-element.150), channel_id=1, source_target_pairs={{0,11},{1,10},{2,9},{3,8},{4,15},{5,14},{6,13},{7,12},{8,3},{9,2},... | collective-permute-start | bytes 393224 | tf_op jit(solution)/shard_map/ppermute | solution.py:848
  49.1 10.7 %pointwise.2.refs_17_.refs_8_ = f32[1,16,8,128,128]{4,3,2,1,0:T(8,128)} custom-call(f32[1,16,8,128,128]{4,3,2,1,0:T(8,128)} %values_ref.1, bf16[512,256]{1,0:T(8,128)(2,1)} %pad_maximum_fusion.mixing_ref, f32[256,128]{1,0:T(8,128)} %broadcast_in_dim.17.bias_ref), custom_call_target="tpu_custom_call" | custom-call | flops 6000000000 | bytes 16777216 | tf_op jit(solution)/shard_map/pointwise/pallas_call | solution.py:573
  74.1 11.2 %collective-permute-done.23.refs_4_ = f32[256,128]{1,0:T(8,128)S(1)} collective-permute-done((f32[256,128]{1,0:T(8,128)}, f32[256,128]{1,0:T(8,128)S(1)}, u32[]{:S(2)}, u32[]{:S(2)}) %collective-permute-start.23) | collective-permute-done | bytes 131104 | tf_op jit(solution)/shard_map/ppermute | solution.py:858
  86.0 7.6 %mix.3 = (f32[256,128]{1,0:T(8,128)}, f32[256,128]{1,0:T(8,128)}, f32[256,128]{1,0:T(8,128)}, f32[256,128]{1,0:T(8,128)}, f32[2,16,8,512]{3,2,1,0:T(8,128)}) custom-call(s32[1]{0:T(128)} %bitcast.me_ref.refs_0_, f32[256,128]{1,0:T(8,128)} %get-tuple-element.155.refs_17_.refs_1_, f32[256,128]{1,0:T(8,128)} %copy-done.55, f32[256,128]{1,0:T(8,128)} %copy-done.61, ...), custom_call_target="tpu_custom_call" | custom-call | flops 100000000 | bytes 5242880 | tf_op jit(solution)/shard_map/mix/pallas_call | solution.py:793
  97.0 7.6 %mix.2 = (f32[256,128]{1,0:T(8,128)}, f32[256,128]{1,0:T(8,128)}, f32[256,128]{1,0:T(8,128)}, f32[256,128]{1,0:T(8,128)}, f32[2,16,8,512]{3,2,1,0:T(8,128)}) custom-call(s32[1]{0:T(128)} %bitcast.me_ref.refs_0_, f32[256,128]{1,0:T(8,128)} %get-tuple-element.156.refs_1_, f32[256,128]{1,0:T(8,128)} %copy-done.52, f32[256,128]{1,0:T(8,128)} %copy-done.58, ...), custom_call_target="tpu_custom_call" | custom-call | flops 100000000 | bytes 5242880 | tf_op jit(solution)/shard_map/mix/pallas_call | solution.py:793
  111.5 7.3 %collective-permute-done.20.refs_3_ = f32[256,128]{1,0:T(8,128)S(1)} collective-permute-done((f32[256,128]{1,0:T(8,128)}, f32[256,128]{1,0:T(8,128)S(1)}, u32[]{:S(2)}, u32[]{:S(2)}) %collective-permute-start.20) | collective-permute-done | bytes 131104 | tf_op jit(solution)/shard_map/ppermute | solution.py:858
  127.9 7.7 %collective-permute-start.37 = (f32[256,128]{1,0:T(8,128)}, f32[256,128]{1,0:T(8,128)S(1)}, u32[]{:S(2)}, u32[]{:S(2)}) collective-permute-start(f32[256,128]{1,0:T(8,128)} %get-tuple-element.198), channel_id=1, source_target_pairs={{0,12},{1,13},{2,14},{3,15},{4,8},{5,9},{6,10},{7,11},{8,4},{9,5},... | collective-permute-start | bytes 393224 | tf_op jit(solution)/shard_map/ppermute | solution.py:848
  156.1 15.7 %shard_map.240 = (f32[1,16,8,128,128]{4,3,2,1,0:T(8,128)}, f32[1,16,8,128,128]{4,3,2,1,0:T(8,128)}, f32[256,128]{1,0:T(8,128)}, f32[256,128]{1,0:T(8,128)}, f32[...) custom-call(s32[1]{0:T(128)} %bitcast.me_ref.refs_0_, ...), custom_call_target="tpu_custom_call" | custom-call | flops 6000000000 | bytes 18874368 | tf_op jit(solution)/shard_map/pallas_call | solution.py:457
  177.8 15.7 %shard_map.241 = (f32[1,16,8,128,128]{4,3,2,1,0:T(8,128)}, f32[1,16,8,128,128]{4,3,2,1,0:T(8,128)}, f32[256,128]{1,0:T(8,128)}, f32[256,128]{1,0:T(8,128)}, f32[...) custom-call(s32[1]{0:T(128)} %bitcast.me_ref.refs_0_, ...), custom_call_target="tpu_custom_call", output_to_operand_aliasing={{0}: (15, {}), {1}: (16, {})} | custom-call | flops 6000000000 | bytes 18874368 | tf_op jit(solution)/shard_map/pallas_call | solution.py:457
  193.5 10.0 %collective-permute-start.44 = (f32[256,128]{1,0:T(8,128)}, f32[256,128]{1,0:T(8,128)S(1)}, u32[]{:S(2)}, u32[]{:S(2)}) collective-permute-start(f32[256,128]{1,0:T(8,128)} %get-tuple-element.209), channel_id=1, source_target_pairs={{0,3},{1,2},{2,1},{3,0},{4,7},{5,6},{6,5},{7,4},{8,11},{9,10},{10,... | collective-permute-start | bytes 393224 | tf_op jit(solution)/shard_map/ppermute | solution.py:848
  207.5 10.8 %collective-permute-start.52 = (f32[256,128]{1,0:T(8,128)}, f32[256,128]{1,0:T(8,128)S(1)}, u32[]{:S(2)}, u32[]{:S(2)}) collective-permute-start(f32[256,128]{1,0:T(8,128)} %get-tuple-element.217), channel_id=1, source_target_pairs={{0,11},{1,10},{2,9},{3,8},{4,15},{5,14},{6,13},{7,12},{8,3},{9,2},... | collective-permute-start | bytes 393224 | tf_op jit(solution)/shard_map/ppermute | solution.py:848
  225.1 6.0 %collective-permute-done.48.refs_7_ = f32[256,128]{1,0:T(8,128)S(1)} collective-permute-done((f32[256,128]{1,0:T(8,128)}, f32[256,128]{1,0:T(8,128)S(1)}, u32[]{:S(2)}, u32[]{:S(2)}) %collective-permute-start.48) | collective-permute-done | bytes 131104 | tf_op jit(solution)/shard_map/ppermute | solution.py:848
  249.5 10.7 %pointwise.3.refs_17_.refs_8_ = f32[1,16,8,128,128]{4,3,2,1,0:T(8,128)} custom-call(f32[1,16,8,128,128]{4,3,2,1,0:T(8,128)} %get-tuple-element.222.values_ref, bf16[512,256]{1,0:T(8,128)(2,1)} %pad_maximum_fusion.1.mixing_ref, f32[256,128]{1,0:T(8,128)} %broadcast_in_dim.18.bias_ref), custom_call_target="tpu_custom_call" | custom-call | flops 6000000000 | bytes 16777216 | tf_op jit(solution)/shard_map/pointwise/pallas_call | solution.py:573
  274.8 8.9 %collective-permute-done.65.refs_4_ = f32[256,128]{1,0:T(8,128)S(1)} collective-permute-done((f32[256,128]{1,0:T(8,128)}, f32[256,128]{1,0:T(8,128)S(1)}, u32[]{:S(2)}, u32[]{:S(2)}) %collective-permute-start.65) | collective-permute-done | bytes 131104 | tf_op jit(solution)/shard_map/ppermute | solution.py:858
  284.3 7.6 %unmix.3 = (f32[256,128]{1,0:T(8,128)}, f32[256,128]{1,0:T(8,128)}, f32[256,128]{1,0:T(8,128)}, f32[256,128]{1,0:T(8,128)}, f32[2,16,8,512]{3,2,1,0:T(8,128)}) custom-call(s32[1]{0:T(128)} %bitcast.me_ref.refs_0_, f32[256,128]{1,0:T(8,128)} %get-tuple-element.223.refs_17_.refs_1_, f32[256,128]{1,0:T(8,128)} %copy-done.53, f32[256,128]{1,0:T(8,128)} %copy-done.59, ...), custom_call_target="tpu_custom_call" | custom-call | flops 100000000 | bytes 5242880 | tf_op jit(solution)/shard_map/unmix/pallas_call | solution.py:793
  295.9 7.6 %unmix.2 = (f32[256,128]{1,0:T(8,128)}, f32[256,128]{1,0:T(8,128)}, f32[256,128]{1,0:T(8,128)}, f32[256,128]{1,0:T(8,128)}, f32[2,16,8,512]{3,2,1,0:T(8,128)}) custom-call(s32[1]{0:T(128)} %bitcast.me_ref.refs_0_, f32[256,128]{1,0:T(8,128)} %get-tuple-element.224.refs_1_, f32[256,128]{1,0:T(8,128)} %copy-done.54, f32[256,128]{1,0:T(8,128)} %copy-done.60, ...), custom_call_target="tpu_custom_call" | custom-call | flops 100000000 | bytes 5242880 | tf_op jit(solution)/shard_map/unmix/pallas_call | solution.py:793
  310.8 6.3 %collective-permute-done.62.refs_3_ = f32[256,128]{1,0:T(8,128)S(1)} collective-permute-done((f32[256,128]{1,0:T(8,128)}, f32[256,128]{1,0:T(8,128)S(1)}, u32[]{:S(2)}, u32[]{:S(2)}) %collective-permute-start.62) | collective-permute-done | bytes 131104 | tf_op jit(solution)/shard_map/ppermute | solution.py:858
  327.1 9.5 %collective-permute-start.79 = (f32[256,128]{1,0:T(8,128)}, f32[256,128]{1,0:T(8,128)S(1)}, u32[]{:S(2)}, u32[]{:S(2)}) collective-permute-start(f32[256,128]{1,0:T(8,128)} %get-tuple-element.266), channel_id=1, source_target_pairs={{0,12},{1,13},{2,14},{3,15},{4,8},{5,9},{6,10},{7,11},{8,4},{9,5},... | collective-permute-start | bytes 393224 | tf_op jit(solution)/shard_map/ppermute | solution.py:848
  345.9 6.6 %weight_grads.2.refs_0_ = f32[2,16,16,16,512]{4,3,2,1,0:T(8,128)} custom-call(f32[2,16,8,512]{3,2,1,0:T(8,128)} %get-tuple-element.273.spec_ref, f32[2,16,8,512]{3,2,1,0:T(8,128)} %get-tuple-element.274.grad_ref), custom_call_target="tpu_custom_call" | custom-call | flops 100000000 | bytes 16777216 | tf_op jit(solution)/shard_map/weight_grads/pallas_call | solution.py:831
  352.7 6.8 %weight_grads.3 = f32[2,16,16,16,512]{4,3,2,1,0:T(8,128)} custom-call(f32[2,16,8,512]{3,2,1,0:T(8,128)} %get-tuple-element.271.spec_ref, f32[2,16,8,512]{3,2,1,0:T(8,128)} %get-tuple-element.272.grad_ref, f32[2,16,16,16,512]{4,3,2,1,0:T(8,128)} %weight_grads.2.refs_0_), custom_call_target="tpu_custom_call", output_to_operand_aliasing={{}: (2, {})} | custom-call | flops 100000000 | bytes 16777216 | tf_op jit(solution)/shard_map/weight_grads/pallas_call | solution.py:831
  365.1 7.3 %shard_map.242.refs_11_ = f32[1,16,8,128,128]{4,3,2,1,0:T(8,128)} custom-call(s32[1]{0:T(128)} %bitcast.me_ref.refs_0_, f32[256,128]{1,0:T(8,128)} %get-tuple-element.263.refs_0_, f32[256,128]{1,0:T(8,128)} %copy-done.40, f32[256,128]{1,0:T(8,128)} %copy-done.41, f32[256,128]{1,0:T(8,128)} %copy-done.43, f32[256,128]{1,0:T(8,128)} %copy-done.45, ...), custom_call_target="tpu_custom_call" | custom-call | flops 3000000000 | bytes 9437184 | tf_op jit(solution)/shard_map/pallas_call | solution.py:457
  391.1 7.2 %shard_map.243 = f32[1,16,8,128,128]{4,3,2,1,0:T(8,128)} custom-call(s32[1]{0:T(128)} %bitcast.me_ref.refs_0_, f32[256,128]{1,0:T(8,128)} %copy-done.37, f32[256,128]{1,0:T(8,128)} %copy-done.38, f32[256,128]{1,0:T(8,128)} %copy-done.39, f32[256,128]{1,0:T(8,128)} %copy-done.48, f32[256,128]{1,0:T(8,128)} %copy-done.51, ...), custom_call_target="tpu_custom_call", output_to_operand_aliasing={{}: (12, {})} | custom-call | flops 3000000000 | bytes 9437184 | tf_op jit(solution)/shard_map/pallas_call | solution.py:457
  (383 shorter events, 187.4 us)
Async XLA Ops:
  34.1 25.8 %collective-permute-start.6 = (f32[256,128]{1,0:T(8,128)}, f32[256,128]{1,0:T(8,128)S(1)}, u32[]{:S(2)}, u32[]{:S(2)}) collective-permute-start(f32[256,128]{1,0:T(8,128)} %get-tuple-element.146), channel_id=1, source_target_pairs={{0,7},{1,6},{2,5},{3,4},{4,3},{5,2},{6,1},{7,0},{8,15},{9,14},{10,... | collective-permute-start | bytes 393224 | tf_op jit(solution)/shard_map/ppermute | solution.py:848
  36.0 24.0 %collective-permute-start.8 = (f32[256,128]{1,0:T(8,128)}, f32[256,128]{1,0:T(8,128)S(1)}, u32[]{:S(2)}, u32[]{:S(2)}) collective-permute-start(f32[256,128]{1,0:T(8,128)} %get-tuple-element.148), channel_id=1, source_target_pairs={{0,9},{1,8},{2,11},{3,10},{4,13},{5,12},{6,15},{7,14},{8,1},{9,0},... | collective-permute-start | bytes 393224 | tf_op jit(solution)/shard_map/ppermute | solution.py:848
  36.9 23.0 %collective-permute-start.10 = (f32[256,128]{1,0:T(8,128)}, f32[256,128]{1,0:T(8,128)S(1)}, u32[]{:S(2)}, u32[]{:S(2)}) collective-permute-start(f32[256,128]{1,0:T(8,128)} %get-tuple-element.150), channel_id=1, source_target_pairs={{0,11},{1,10},{2,9},{3,8},{4,15},{5,14},{6,13},{7,12},{8,3},{9,2},... | collective-permute-start | bytes 393224 | tf_op jit(solution)/shard_map/ppermute | solution.py:848
  70.6 23.5 %collective-permute-start.15 = (f32[256,128]{1,0:T(8,128)}, f32[256,128]{1,0:T(8,128)S(1)}, u32[]{:S(2)}, u32[]{:S(2)}) collective-permute-start(f32[256,128]{1,0:T(8,128)} %get-tuple-element.157), channel_id=1, source_target_pairs={{0,1},{1,0},{2,3},{3,2},{4,5},{5,4},{6,7},{7,6},{8,9},{9,8},{10,11... | collective-permute-start | bytes 393224 | tf_op jit(solution)/shard_map/ppermute | solution.py:858
  72.9 23.4 %collective-permute-start.16 = (f32[256,128]{1,0:T(8,128)}, f32[256,128]{1,0:T(8,128)S(1)}, u32[]{:S(2)}, u32[]{:S(2)}) collective-permute-start(f32[256,128]{1,0:T(8,128)} %get-tuple-element.158), channel_id=1, source_target_pairs={{0,2},{1,3},{2,0},{3,1},{4,6},{5,7},{6,4},{7,5},{8,10},{9,11},{10,... | collective-permute-start | bytes 393224 | tf_op jit(solution)/shard_map/ppermute | solution.py:858
  72.9 23.4 %collective-permute-start.17 = (f32[256,128]{1,0:T(8,128)}, f32[256,128]{1,0:T(8,128)S(1)}, u32[]{:S(2)}, u32[]{:S(2)}) collective-permute-start(f32[256,128]{1,0:T(8,128)} %get-tuple-element.159), channel_id=1, source_target_pairs={{0,3},{1,2},{2,1},{3,0},{4,7},{5,6},{6,5},{7,4},{8,11},{9,10},{10,... | collective-permute-start | bytes 393224 | tf_op jit(solution)/shard_map/ppermute | solution.py:858
  144.7 27.1 %collective-permute-start.30 = (f32[256,128]{1,0:T(8,128)}, f32[256,128]{1,0:T(8,128)S(1)}, u32[]{:S(2)}, u32[]{:S(2)}) collective-permute-start(f32[256,128]{1,0:T(8,128)} %get-tuple-element.190), channel_id=1, source_target_pairs={{0,14},{1,15},{2,12},{3,13},{4,10},{5,11},{6,8},{7,9},{8,6},{9,7},... | collective-permute-start | bytes 393224 | tf_op jit(solution)/shard_map/ppermute | solution.py:848
  146.5 25.3 %collective-permute-start.31 = (f32[256,128]{1,0:T(8,128)}, f32[256,128]{1,0:T(8,128)S(1)}, u32[]{:S(2)}, u32[]{:S(2)}) collective-permute-start(f32[256,128]{1,0:T(8,128)} %get-tuple-element.191), channel_id=1, source_target_pairs={{0,3},{1,2},{2,1},{3,0},{4,7},{5,6},{6,5},{7,4},{8,11},{9,10},{10,... | collective-permute-start | bytes 393224 | tf_op jit(solution)/shard_map/ppermute | solution.py:848
  146.8 25.5 %collective-permute-start.32 = (f32[256,128]{1,0:T(8,128)}, f32[256,128]{1,0:T(8,128)S(1)}, u32[]{:S(2)}, u32[]{:S(2)}) collective-permute-start(f32[256,128]{1,0:T(8,128)} %get-tuple-element.192), channel_id=1, source_target_pairs={{0,7},{1,6},{2,5},{3,4},{4,3},{5,2},{6,1},{7,0},{8,15},{9,14},{10,... | collective-permute-start | bytes 393224 | tf_op jit(solution)/shard_map/ppermute | solution.py:848
  151.6 22.7 %collective-permute-start.33 = (f32[256,128]{1,0:T(8,128)}, f32[256,128]{1,0:T(8,128)S(1)}, u32[]{:S(2)}, u32[]{:S(2)}) collective-permute-start(f32[256,128]{1,0:T(8,128)} %get-tuple-element.193), channel_id=1, source_target_pairs={{0,11},{1,10},{2,9},{3,8},{4,15},{5,14},{6,13},{7,12},{8,3},{9,2},... | collective-permute-start | bytes 393224 | tf_op jit(solution)/shard_map/ppermute | solution.py:848
  154.6 22.5 %collective-permute-start.34 = (f32[256,128]{1,0:T(8,128)}, f32[256,128]{1,0:T(8,128)S(1)}, u32[]{:S(2)}, u32[]{:S(2)}) collective-permute-start(f32[256,128]{1,0:T(8,128)} %get-tuple-element.194), channel_id=1, source_target_pairs={{0,15},{1,14},{2,13},{3,12},{4,11},{5,10},{6,9},{7,8},{8,7},{9,6},... | collective-permute-start | bytes 393224 | tf_op jit(solution)/shard_map/ppermute | solution.py:848
  193.5 27.2 %collective-permute-start.44 = (f32[256,128]{1,0:T(8,128)}, f32[256,128]{1,0:T(8,128)S(1)}, u32[]{:S(2)}, u32[]{:S(2)}) collective-permute-start(f32[256,128]{1,0:T(8,128)} %get-tuple-element.209), channel_id=1, source_target_pairs={{0,3},{1,2},{2,1},{3,0},{4,7},{5,6},{6,5},{7,4},{8,11},{9,10},{10,... | collective-permute-start | bytes 393224 | tf_op jit(solution)/shard_map/ppermute | solution.py:848
  203.5 27.5 %collective-permute-start.48 = (f32[256,128]{1,0:T(8,128)}, f32[256,128]{1,0:T(8,128)S(1)}, u32[]{:S(2)}, u32[]{:S(2)}) collective-permute-start(f32[256,128]{1,0:T(8,128)} %get-tuple-element.213), channel_id=1, source_target_pairs={{0,7},{1,6},{2,5},{3,4},{4,3},{5,2},{6,1},{7,0},{8,15},{9,14},{10,... | collective-permute-start | bytes 393224 | tf_op jit(solution)/shard_map/ppermute | solution.py:848
  204.0 29.9 %collective-permute-start.51 = (f32[256,128]{1,0:T(8,128)}, f32[256,128]{1,0:T(8,128)S(1)}, u32[]{:S(2)}, u32[]{:S(2)}) collective-permute-start(f32[256,128]{1,0:T(8,128)} %get-tuple-element.216), channel_id=1, source_target_pairs={{0,10},{1,11},{2,8},{3,9},{4,14},{5,15},{6,12},{7,13},{8,2},{9,3},... | collective-permute-start | bytes 393224 | tf_op jit(solution)/shard_map/ppermute | solution.py:848
  207.5 33.6 %collective-permute-start.52 = (f32[256,128]{1,0:T(8,128)}, f32[256,128]{1,0:T(8,128)S(1)}, u32[]{:S(2)}, u32[]{:S(2)}) collective-permute-start(f32[256,128]{1,0:T(8,128)} %get-tuple-element.217), channel_id=1, source_target_pairs={{0,11},{1,10},{2,9},{3,8},{4,15},{5,14},{6,13},{7,12},{8,3},{9,2},... | collective-permute-start | bytes 393224 | tf_op jit(solution)/shard_map/ppermute | solution.py:848
  269.2 26.1 %collective-permute-start.57 = (f32[256,128]{1,0:T(8,128)}, f32[256,128]{1,0:T(8,128)S(1)}, u32[]{:S(2)}, u32[]{:S(2)}) collective-permute-start(f32[256,128]{1,0:T(8,128)} %get-tuple-element.225), channel_id=1, source_target_pairs={{0,1},{1,0},{2,3},{3,2},{4,5},{5,4},{6,7},{7,6},{8,9},{9,8},{10,11... | collective-permute-start | bytes 393224 | tf_op jit(solution)/shard_map/ppermute | solution.py:858
  270.5 24.7 %collective-permute-start.58 = (f32[256,128]{1,0:T(8,128)}, f32[256,128]{1,0:T(8,128)S(1)}, u32[]{:S(2)}, u32[]{:S(2)}) collective-permute-start(f32[256,128]{1,0:T(8,128)} %get-tuple-element.226), channel_id=1, source_target_pairs={{0,2},{1,3},{2,0},{3,1},{4,6},{5,7},{6,4},{7,5},{8,10},{9,11},{10,... | collective-permute-start | bytes 393224 | tf_op jit(solution)/shard_map/ppermute | solution.py:858
  271.9 23.3 %collective-permute-start.59 = (f32[256,128]{1,0:T(8,128)}, f32[256,128]{1,0:T(8,128)S(1)}, u32[]{:S(2)}, u32[]{:S(2)}) collective-permute-start(f32[256,128]{1,0:T(8,128)} %get-tuple-element.227), channel_id=1, source_target_pairs={{0,3},{1,2},{2,1},{3,0},{4,7},{5,6},{6,5},{7,4},{8,11},{9,10},{10,... | collective-permute-start | bytes 393224 | tf_op jit(solution)/shard_map/ppermute | solution.py:858
  327.1 32.3 %collective-permute-start.79 = (f32[256,128]{1,0:T(8,128)}, f32[256,128]{1,0:T(8,128)S(1)}, u32[]{:S(2)}, u32[]{:S(2)}) collective-permute-start(f32[256,128]{1,0:T(8,128)} %get-tuple-element.266), channel_id=1, source_target_pairs={{0,12},{1,13},{2,14},{3,15},{4,8},{5,9},{6,10},{7,11},{8,4},{9,5},... | collective-permute-start | bytes 393224 | tf_op jit(solution)/shard_map/ppermute | solution.py:848
  336.7 23.7 %collective-permute-start.80 = (f32[256,128]{1,0:T(8,128)}, f32[256,128]{1,0:T(8,128)S(1)}, u32[]{:S(2)}, u32[]{:S(2)}) collective-permute-start(f32[256,128]{1,0:T(8,128)} %get-tuple-element.267), channel_id=1, source_target_pairs={{0,1},{1,0},{2,3},{3,2},{4,5},{5,4},{6,7},{7,6},{8,9},{9,8},{10,11... | collective-permute-start | bytes 393224 | tf_op jit(solution)/shard_map/ppermute | solution.py:848
  339.4 21.9 %collective-permute-start.81 = (f32[256,128]{1,0:T(8,128)}, f32[256,128]{1,0:T(8,128)S(1)}, u32[]{:S(2)}, u32[]{:S(2)}) collective-permute-start(f32[256,128]{1,0:T(8,128)} %get-tuple-element.268), channel_id=1, source_target_pairs={{0,5},{1,4},{2,7},{3,6},{4,1},{5,0},{6,3},{7,2},{8,13},{9,12},{10,... | collective-permute-start | bytes 393224 | tf_op jit(solution)/shard_map/ppermute | solution.py:848
  361.3 23.6 %collective-permute-start.74 = (f32[256,128]{1,0:T(8,128)S(1)}, f32[256,128]{1,0:T(8,128)S(1)}, u32[]{:S(2)}, u32[]{:S(2)}) collective-permute-start(f32[256,128]{1,0:T(8,128)S(1)} %copy-done.76), channel_id=1, source_target_pairs={{0,7},{1,6},{2,5},{3,4},{4,3},{5,2},{6,1},{7,0},{8,15},{9,14},{10,... | collective-permute-start | bytes 393224 | tf_op jit(solution)/shard_map/ppermute | solution.py:848
  362.6 24.0 %collective-permute-start.75 = (f32[256,128]{1,0:T(8,128)S(1)}, f32[256,128]{1,0:T(8,128)S(1)}, u32[]{:S(2)}, u32[]{:S(2)}) collective-permute-start(f32[256,128]{1,0:T(8,128)S(1)} %copy-done.77), channel_id=1, source_target_pairs={{0,11},{1,10},{2,9},{3,8},{4,15},{5,14},{6,13},{7,12},{8,3},{9,2},... | collective-permute-start | bytes 393224 | tf_op jit(solution)/shard_map/ppermute | solution.py:848
  364.4 26.1 %collective-permute-start.76 = (f32[256,128]{1,0:T(8,128)S(1)}, f32[256,128]{1,0:T(8,128)S(1)}, u32[]{:S(2)}, u32[]{:S(2)}) collective-permute-start(f32[256,128]{1,0:T(8,128)S(1)} %copy-done.79), channel_id=1, source_target_pairs={{0,15},{1,14},{2,13},{3,12},{4,11},{5,10},{6,9},{7,8},{8,7},{9,6},... | collective-permute-start | bytes 393224 | tf_op jit(solution)/shard_map/ppermute | solution.py:848
  (164 other events, 2419.6 us)
